TPU v7x, 512 devices: a whole 4x8x8 slice. The times are simulated.
512 devices in a mesh: seq: 64 (over y, x, z_lo), head: 8 (over z_hi, core).
Axes of the slice: x: 4, y: 8, z: 8 (z_hi: 4, z_lo: 2; z = z_hi * 2 + z_lo), core: 2. Of those that a mesh axis runs over, the one named last changes fastest.
Arguments:
- layer_input: bfloat16 [32768, 5376], P('seq', 'head'), may hold values from -6 to 6
- omega_in: bfloat16 [5376, 128], P('head'), may hold values from -0.00390625 to 0.00390625
- upstream: bfloat16 [32768, 5376], P('seq', 'head'), may hold values from -6 to 6
- omega_out: bfloat16 [5376, 128], P('head'), may hold values from -0.00390625 to 0.00390625
- q_raw: bfloat16 [32768, 4096], P('seq', 'head'), may hold values from -6 to 6
- k_raw: bfloat16 [32768, 2048], P('seq', 'head'), may hold values from -6 to 6
- values: bfloat16 [32768, 2048], P('seq', 'head'), may hold values from -6 to 6
- d_out: bfloat16 [32768, 4096], P('seq', 'head'), may hold values from -16 to 16
- q_gain: float32 [128], replicated, may hold values from 0.1 to 1.9
- k_gain: float32 [128], replicated, may hold values from 0.1 to 1.9
Outputs:
- query_grad: bfloat16 [32768, 4096], P('seq', 'head')
- key_grad: bfloat16 [32768, 2048], P('seq', 'head')
- value_grad: bfloat16 [32768, 2048], P('seq', 'head')
- sketch_q: float32 [128, 4096], P('seq', 'head')
- sketch_k: float32 [128, 2048], P('seq', 'head')
- sketch_v: float32 [128, 2048], P('seq', 'head')
- sketch_o: float32 [128, 4096], P('seq', 'head')
All inputs are finite; a program needn't handle non-finite values.
Results may differ from a plain program's by a relative error of at most 0.013.
Values may be sent and summed in bfloat16 or wider, within the bound.
No kernel may reach another device: no remote copies, remote signals or barrier semaphores. Data moves between devices by JAX's collectives and lax.ppermute only.
A program may use at most 64 MiB of HBM per device.

v0:
```python
import jax
import jax.numpy as jnp
from jax import lax
from jax.sharding import PartitionSpec as P

WINDOW = 1024


score_scale = 168.0 ** (-0.5)
epsilon = 1e-06
rope_base = 10000.0


def from_behind(shard, axis, by):
    count = lax.axis_size(axis)
    pairs = [(i, i + by) for i in range(count) if 0 <= i + by < count]
    return lax.ppermute(shard, axis, pairs)


def prepare(raw_input, gain, positions):
    mean_square = jnp.mean(raw_input * raw_input, axis=-1, keepdims=True)
    normed = raw_input * lax.rsqrt(mean_square + epsilon) * gain
    half_dim = raw_input.shape[-1] // 2
    inverse_freq = rope_base ** (
        -(jnp.arange(half_dim, dtype=jnp.float32) * 2.0 / raw_input.shape[-1])
    )
    angles = positions.astype(jnp.float32)[:, None] * inverse_freq[None, :]
    cos_table = jnp.cos(angles)[:, None, :]
    sin_table = jnp.sin(angles)[:, None, :]
    lower_half = normed[..., :half_dim]
    upper_half = normed[..., half_dim:]
    return jnp.concatenate(
        [
            lower_half * cos_table - upper_half * sin_table,
            upper_half * cos_table + lower_half * sin_table,
        ],
        axis=-1,
    )


def head_core(query_rows, key_rows, value_rows, grad_rows, allowed):
    scores = score_scale * jnp.dot(query_rows, key_rows.T, preferred_element_type=jnp.float32)
    exp_scores = jnp.where(allowed, jnp.exp(scores), 0.0)
    probs = exp_scores / jnp.sum(exp_scores, axis=-1, keepdims=True)
    probs_low = probs.astype(jnp.bfloat16)
    attn_rows = jnp.dot(probs_low, value_rows, preferred_element_type=jnp.float32).astype(
        jnp.bfloat16
    )
    grad_probs = jnp.dot(grad_rows, value_rows.T, preferred_element_type=jnp.float32)
    row_delta = jnp.sum(probs * grad_probs, axis=-1, keepdims=True)
    grad_low = (probs * (grad_probs - row_delta)).astype(jnp.bfloat16)
    query_grad = score_scale * jnp.dot(grad_low, key_rows, preferred_element_type=jnp.float32)
    key_grad = score_scale * jnp.dot(grad_low.T, query_rows, preferred_element_type=jnp.float32)
    value_grad = jnp.dot(probs_low.T, grad_rows, preferred_element_type=jnp.float32)
    return (attn_rows, query_grad, key_grad, value_grad)


def per_device(
    layer_input, omega_in, upstream, omega_out, q_raw, k_raw, values, d_out, q_gain, k_gain
):
    tok_rows = q_raw.shape[0]
    head_dim = q_gain.shape[0]
    heads_q = q_raw.shape[1] // head_dim
    heads_kv = k_raw.shape[1] // head_dim
    group_size = heads_q // heads_kv
    kv_cols = heads_kv * head_dim
    q_cols = heads_q * head_dim
    halo_devices = (WINDOW + tok_rows - 1) // tok_rows
    ext_rows = halo_devices * tok_rows
    span_rows = ext_rows + tok_rows
    partial_x = jnp.dot(layer_input, omega_in, preferred_element_type=jnp.float32)
    partial_y = jnp.dot(upstream, omega_out, preferred_element_type=jnp.float32)
    summed_x, summed_y = lax.psum((partial_x, partial_y), "head")
    x_sketch = summed_x.astype(jnp.bfloat16)
    dy_sketch = summed_y.astype(jnp.bfloat16)
    offset = lax.axis_index("seq") * tok_rows
    positions = offset + jnp.arange(tok_rows, dtype=jnp.int32)
    query_f = q_raw.astype(jnp.float32).reshape(tok_rows, heads_q, head_dim)
    key_f = k_raw.astype(jnp.float32).reshape(tok_rows, heads_kv, head_dim)
    query_full, query_back = jax.vjp(
        lambda raw_input: prepare(raw_input, q_gain, positions), query_f
    )
    key_full, key_back = jax.vjp(lambda raw_input: prepare(raw_input, k_gain, positions), key_f)
    query_prep = query_full.astype(jnp.bfloat16)
    key_flat = key_full.astype(jnp.bfloat16).reshape(tok_rows, kv_cols)
    pieces = [
        from_behind((key_flat, values), "seq", distance) for distance in range(halo_devices, 0, -1)
    ]
    key_ext = jnp.concatenate([piece[0] for piece in pieces] + [key_flat], axis=0)
    value_ext = jnp.concatenate([piece[1] for piece in pieces] + [values], axis=0)
    row_index = jnp.arange(tok_rows, dtype=jnp.int32)[:, None]
    col_index = jnp.arange(span_rows, dtype=jnp.int32)[None, :]
    gap = row_index - col_index + ext_rows
    key_pos = offset - ext_rows + col_index
    allowed = (key_pos >= 0) & (gap >= 0) & (gap < WINDOW)
    query_heads = query_prep.transpose(1, 0, 2)
    grad_heads = d_out.reshape(tok_rows, heads_q, head_dim).transpose(1, 0, 2)
    key_rep = jnp.repeat(
        key_ext.reshape(span_rows, heads_kv, head_dim).transpose(1, 0, 2), group_size, axis=0
    )
    value_rep = jnp.repeat(
        value_ext.reshape(span_rows, heads_kv, head_dim).transpose(1, 0, 2), group_size, axis=0
    )
    attn_heads, query_grads, key_grads, value_grads = lax.map(
        lambda items: head_core(items[0], items[1], items[2], items[3], allowed),
        (query_heads, key_rep, value_rep, grad_heads),
    )
    key_sum = (
        key_grads.reshape(heads_kv, group_size, span_rows, head_dim)
        .sum(axis=1)
        .transpose(1, 0, 2)
        .reshape(span_rows, kv_cols)
    )
    value_sum = (
        value_grads.reshape(heads_kv, group_size, span_rows, head_dim)
        .sum(axis=1)
        .transpose(1, 0, 2)
        .reshape(span_rows, kv_cols)
    )
    key_total = key_sum[ext_rows:]
    value_total = value_sum[ext_rows:]
    for distance in range(1, halo_devices + 1):
        block_start = (halo_devices - distance) * tok_rows
        back_key, back_value = from_behind(
            (
                key_sum[block_start : block_start + tok_rows],
                value_sum[block_start : block_start + tok_rows],
            ),
            "seq",
            -distance,
        )
        key_total = key_total + back_key
        value_total = value_total + back_value
    query_grad_prep = query_grads.transpose(1, 0, 2)
    query_grad = query_back(query_grad_prep)[0].reshape(tok_rows, q_cols).astype(jnp.bfloat16)
    key_grad = (
        key_back(key_total.reshape(tok_rows, heads_kv, head_dim))[0]
        .reshape(tok_rows, kv_cols)
        .astype(jnp.bfloat16)
    )
    value_grad = value_total.astype(jnp.bfloat16)
    attn_out = attn_heads.transpose(1, 0, 2).reshape(tok_rows, q_cols)
    grads_joined = jnp.concatenate([query_grad, key_grad, value_grad], axis=1)
    input_side = jnp.dot(x_sketch.T, grads_joined, preferred_element_type=jnp.float32)
    output_side = jnp.dot(dy_sketch.T, attn_out, preferred_element_type=jnp.float32)
    sketches = lax.psum_scatter(
        jnp.concatenate([input_side, output_side], axis=1), "seq", scatter_dimension=0, tiled=True
    )
    sketch_q = sketches[:, :q_cols]
    sketch_k = sketches[:, q_cols : q_cols + kv_cols]
    sketch_v = sketches[:, q_cols + kv_cols : q_cols + 2 * kv_cols]
    sketch_o = sketches[:, q_cols + 2 * kv_cols :]
    return (query_grad, key_grad, value_grad, sketch_q, sketch_k, sketch_v, sketch_o)


def solution(mesh):
    in_specs = (
        P("seq", "head"),
        P("head", None),
        P("seq", "head"),
        P("head", None),
        P("seq", "head"),
        P("seq", "head"),
        P("seq", "head"),
        P("seq", "head"),
        P(),
        P(),
    )
    out_specs = (
        P("seq", "head"),
        P("seq", "head"),
        P("seq", "head"),
        P("seq", "head"),
        P("seq", "head"),
        P("seq", "head"),
        P("seq", "head"),
    )
    return jax.shard_map(
        per_device, mesh=mesh, in_specs=in_specs, out_specs=out_specs, check_vma=False
    )
```

profile of v0, /device:TPU:128, one launch (start us, length us, event | category | flops | bytes accessed | tf_op | source)
XLA Modules:
  0.0 833.8 jit_solution(16140426114121211258)
XLA Ops:
  13.3 4.1 collective-permute-start
  17.4 5.0 collective-permute-start.1
  22.4 2.7 collective-permute-start.2
  25.1 2.9 collective-permute-start.3
  31.5 2.2 fusion.65
  33.9 36.6 %all-reduce.10 = (bf16[512,128]{1,0:T(8,128)(2,1)}, bf16[512,128]{1,0:T(8,128)(2,1)}) all-reduce(f32[512,128]{1,0:T(8,128)} %fusion.65, f32[512,128]{1,0:T(8,128)} %fusion.64), channel_id=1, replica_groups=mesh['seq'=64,'head'=8] {'head'}, use_global_device_ids=true, to_apply=%region_11.12 | all-reduce | flops 131072 | bytes 786432 | tf_op jit(solution)/shard_map/psum | solution.py:73
  77.5 9.9 %maximum_bitcast_fusion = bf16[2,1536,128]{2,0,1:T(2,128)(2,1)S(1)} fusion(bf16[512,2,128]{2,1,0:T(2,128)(2,1)S(1)} %maximum_convert_fusion, bf16[512,2,128]{2,1,0:T(2,128)(2,1)S(1)} %concatenate.27, bf16[512,2,128]{2,1,0:T(2,128)(2,1)S(1)} %concatenate.26), kind=kLoop, calls=%fused_computation.66 | loop fusion | flops 786432 | bytes 1572864 | tf_op jit(solution)/shard_map/transpose | solution.py:99
  89.8 2.5 broadcast_in_dim.55
  93.7 58.9 %while.17 = (s32[]{:T(128)}, bf16[4,512,128]{1,2,0:T(8,128)(2,1)}, f32[4,512,128]{1,2,0:T(8,128)}, f32[4,1536,128]{2,1,0:T(8,128)}, f32[4,1536,128]{2,1,0:T(8,12...) while((s32[]{:T(128)}, bf16[4,512,128]{1,2,0:T(8,128)(2,1)}, ...), condition=%wide.region_5.6_spmd.clone, body=%wide.region_2.5_spmd.clone.sunk | while | flops 1224014848 | bytes 57563300 | solution.py:104
  95.5 2.3 multiply_reduce_fusion.4
  102.3 3.7 fusion.101
  110.3 2.3 multiply_reduce_fusion.4
  117.1 3.7 fusion.101
  125.0 2.3 multiply_reduce_fusion.4
  131.8 3.7 fusion.101
  139.7 2.3 multiply_reduce_fusion.4
  146.5 3.7 fusion.101
  152.6 3.7 bitcast_reduce_fusion
  165.4 2.1 copy.124
  174.8 2.1 copy.123
  176.9 2.2 fusion.66
  180.1 7.5 collective-permute-done.4
  187.6 3.4 collective-permute-done.5
  206.7 617.4 %all-reduce.9.cloned.1.call-done = f32[128,1536]{1,0:T(8,128)} async-done(((f32[128,1536]{1,0:T(8,128)}), f32[128,1536]{1,0:T(8,128)}) %all-reduce.9.cloned.1.call-update) | async-done | bytes 786448
  (164 shorter events, 90.3 us)
Async XLA Ops:
  7.2 22.2 %copy-start = (bf16[512,672]{0,1:T(8,128)(2,1)S(1)}, bf16[512,672]{0,1:T(8,128)(2,1)}, u32[]{:S(2)}) copy-start(bf16[512,672]{0,1:T(8,128)(2,1)} %param.12) | copy-start | bytes 2064388
  7.2 816.9 %all-reduce.9.cloned.1.call-start = ((), (), s32[]{:S(2)}) async-start(), calls=%async_computation | async-start | bytes 1572864
  9.4 19.8 %copy-start.4 = (f32[512,2]{1,0:T(8,128)}, f32[512,2]{1,0:T(8,128)S(1)}, u32[]{:S(2)}) copy-start(f32[512,2]{1,0:T(8,128)S(1)} %copy.114) | copy-start | bytes 12292
  10.0 60.4 %copy-start.10 = (f32[512,64]{0,1:T(8,128)}, f32[512,64]{0,1:T(8,128)S(1)}, u32[]{:S(2)}) copy-start(f32[512,64]{0,1:T(8,128)S(1)} %get-tuple-element.238) | copy-start | bytes 393220
  10.1 19.2 %copy-start.6 = (f32[512,64]{1,0:T(8,128)}, f32[512,64]{1,0:T(8,128)S(1)}, u32[]{:S(2)}) copy-start(f32[512,64]{1,0:T(8,128)S(1)} %copy.115) | copy-start | bytes 393220
  10.3 19.1 %copy-start.8 = (f32[512,64]{1,0:T(8,128)}, f32[512,64]{1,0:T(8,128)S(1)}, u32[]{:S(2)}) copy-start(f32[512,64]{1,0:T(8,128)S(1)} %copy.116) | copy-start | bytes 393220
  11.0 22.7 %copy-start.17 = (f32[128]{0:T(128)S(1)}, f32[128]{0:T(128)}, u32[]{:S(2)}) copy-start(f32[128]{0:T(128)} %param.20) | copy-start | bytes 1540
  13.3 62.1 %collective-permute-start = (bf16[512,256]{1,0:T(8,128)(2,1)}, bf16[512,256]{1,0:T(8,128)(2,1)}, u32[]{:S(2)}, u32[]{:S(2)}) collective-permute-start(bf16[512,256]{1,0:T(8,128)(2,1)} %bitcast.103), channel_id=1, source_target_pairs={{0,16},{8,24},{16,32},{24,40},{32,48},{40,56},{48,64},{56,72},{64,... | collective-permute-start | bytes 786440 | tf_op jit(solution)/shard_map/ppermute | solution.py:17
  17.4 59.1 %collective-permute-start.1 = (bf16[512,256]{1,0:T(8,128)(2,1)}, bf16[512,256]{1,0:T(8,128)(2,1)}, u32[]{:S(2)}, u32[]{:S(2)}) collective-permute-start(bf16[512,256]{1,0:T(8,128)(2,1)} %bitcast.103), channel_id=1, source_target_pairs={{0,8},{8,16},{16,24},{24,32},{32,40},{40,48},{48,56},{56,64},{64,7... | collective-permute-start | bytes 786440 | tf_op jit(solution)/shard_map/ppermute | solution.py:17
  22.4 66.0 %collective-permute-start.2 = (bf16[512,256]{1,0:T(8,128)(2,1)}, bf16[512,256]{1,0:T(8,128)(2,1)}, u32[]{:S(2)}, u32[]{:S(2)}) collective-permute-start(bf16[512,256]{1,0:T(8,128)(2,1)} %param.18), channel_id=1, source_target_pairs={{0,16},{8,24},{16,32},{24,40},{32,48},{40,56},{48,64},{56,72},{64,... | collective-permute-start | bytes 786440 | tf_op jit(solution)/shard_map/ppermute | solution.py:17
  25.1 63.3 %collective-permute-start.3 = (bf16[512,256]{1,0:T(8,128)(2,1)}, bf16[512,256]{1,0:T(8,128)(2,1)}, u32[]{:S(2)}, u32[]{:S(2)}) collective-permute-start(bf16[512,256]{1,0:T(8,128)(2,1)} %param.18), channel_id=1, source_target_pairs={{0,8},{8,16},{16,24},{24,32},{32,40},{40,48},{48,56},{56,64},{64,7... | collective-permute-start | bytes 786440 | tf_op jit(solution)/shard_map/ppermute | solution.py:17
  71.4 17.0 %copy-start.16 = (bf16[512,256]{1,0:T(8,128)(2,1)S(1)}, bf16[512,256]{1,0:T(8,128)(2,1)}, u32[]{:S(2)}) copy-start(bf16[512,256]{1,0:T(8,128)(2,1)} %param.18) | copy-start | bytes 786436
  89.7 4.0 copy-start.3
  159.6 40.3 %collective-permute-start.6 = (f32[512,256]{0,1:T(8,128)}, f32[512,256]{0,1:T(8,128)}, u32[]{:S(2)}, u32[]{:S(2)}) collective-permute-start(f32[512,256]{0,1:T(8,128)} %bitcast.145), channel_id=1, source_target_pairs={{8,0},{16,8},{24,16},{32,24},{40,32},{48,40},{56,48},{64,56},{72,6... | collective-permute-start | bytes 1572872 | tf_op jit(solution)/shard_map/ppermute | solution.py:17
  162.9 37.0 %collective-permute-start.7 = (f32[512,256]{0,1:T(8,128)}, f32[512,256]{0,1:T(8,128)}, u32[]{:S(2)}, u32[]{:S(2)}) collective-permute-start(f32[512,256]{0,1:T(8,128)} %bitcast.146), channel_id=1, source_target_pairs={{16,0},{24,8},{32,16},{40,24},{48,32},{56,40},{64,48},{72,56},{80,... | collective-permute-start | bytes 1572872 | tf_op jit(solution)/shard_map/ppermute | solution.py:17
  165.4 8.4 %copy-start.12 = (f32[512,2,128]{2,0,1:T(8,128)S(1)}, f32[512,2,128]{2,0,1:T(8,128)}, u32[]{:S(2)}) copy-start(f32[512,2,128]{2,0,1:T(8,128)} %get-tuple-element.217) | copy-start | bytes 1572868
  167.5 20.1 %collective-permute-start.4 = (f32[512,256]{0,1:T(8,128)}, f32[512,256]{0,1:T(8,128)}, u32[]{:S(2)}, u32[]{:S(2)}) collective-permute-start(f32[512,256]{0,1:T(8,128)} %bitcast.14), channel_id=1, source_target_pairs={{8,0},{16,8},{24,16},{32,24},{40,32},{48,40},{56,48},{64,56},{72,6... | collective-permute-start | bytes 1572872 | tf_op jit(solution)/shard_map/ppermute | solution.py:17
  170.8 20.2 %collective-permute-start.5 = (f32[512,256]{0,1:T(8,128)}, f32[512,256]{0,1:T(8,128)}, u32[]{:S(2)}, u32[]{:S(2)}) collective-permute-start(f32[512,256]{0,1:T(8,128)} %bitcast.15), channel_id=1, source_target_pairs={{16,0},{24,8},{32,16},{40,24},{48,32},{56,40},{64,48},{72,56},{80,... | collective-permute-start | bytes 1572872 | tf_op jit(solution)/shard_map/ppermute | solution.py:17
  176.9 14.1 %copy-start.13 = (f32[512,2,128]{0,2,1:T(8,128)S(1)}, f32[512,2,128]{0,2,1:T(8,128)}, u32[]{:S(2)}) copy-start(f32[512,2,128]{0,2,1:T(8,128)} %copy.123) | copy-start | bytes 1572868
  179.1 15.4 %copy-start.7 = (f32[512,64]{1,0:T(8,128)S(1)}, f32[512,64]{1,0:T(8,128)}, u32[]{:S(2)}) copy-start(f32[512,64]{1,0:T(8,128)} %copy-done.6) | copy-start | bytes 393220
  179.1 15.4 %copy-start.9 = (f32[512,64]{1,0:T(8,128)S(1)}, f32[512,64]{1,0:T(8,128)}, u32[]{:S(2)}) copy-start(f32[512,64]{1,0:T(8,128)} %copy-done.8) | copy-start | bytes 393220
  192.4 5.4 copy-start.5
  197.4 4.0 copy-start.11
  197.4 4.0 copy-start.19
  (11 other events, 32.3 us)
Sparse Core Ops, SparseCore 0:
  203.0 621.0 all-reduce.8
where the time goes:
time: 836 us; the launch traced here: 834 us
  waiting for transfers between devices  628 us (75%)
  matrix products  57 us (7%)
  local copies, waits for them, and re-layouts  41.9 us (5%)
  blocking collectives  36.6 us (4%)
  other arithmetic  34.7 us (4%)
  starting transfers between devices  19.9 us (2%)
  between operations  15.2 us (2%)
    unnamed x2, waiting for transfers between devices  617 us
    psum x1, blocking collectives, per_device(): summed_x, summed_y = lax.psum((partial_x, partial_y), 'head')  36.6 us
    ppermute x8, starting transfers between devices, from_behind(): return lax.ppermute(shard, axis, pairs)  19.8 us
  transfers between devices with their start and end apart: 9, of which 3 were waited for; matrix products, arithmetic and copies ran while one was open for 6% of the time, Pallas kernels for 0%

commit v1 on v0

v1 whole, which is shorter than its diff:
```python
import jax
import jax.numpy as jnp
import numpy as np
from jax import lax
from jax.experimental import pallas as pl
from jax.experimental.pallas import tpu as pltpu
from jax.sharding import PartitionSpec as P

WINDOW = 1024
HD = 128
TOK = 512
QT = 256
KB = 256
SPAN = 1536
NBLK = 5
score_scale = 168.0 ** (-0.5)
LOG2E = 1.4426950408889634
epsilon = 1e-06
rope_base = 10000.0
F32 = jnp.float32
BF16 = jnp.bfloat16


def rope_tables(shards):
    freq = rope_base ** (-(np.arange(64, dtype=np.float64) * 2.0 / HD))
    freq = np.concatenate([freq, freq])[None, :]
    base = ((np.arange(shards + 2) - 2) * TOK).astype(np.float64)[:, None] * freq
    local = np.arange(TOK, dtype=np.float64)[:, None] * freq
    pad = (-base.shape[0]) % 8
    base = np.pad(base, ((0, pad), (0, 0)))
    tables = [np.cos(base), np.sin(base), np.cos(local), np.sin(local)]
    return [t.astype(np.float32) for t in tables]


def norm_scale(raw):
    return lax.rsqrt(jnp.mean(raw * raw, axis=-1, keepdims=True) + epsilon)


def rope_forward(normed, cos, sin_signed):
    return normed * cos + pltpu.roll(normed, 64, 1) * sin_signed


def prep_back(raw, gain, cos, sin_signed, grad):
    r = norm_scale(raw)
    d_norm = (grad * cos - pltpu.roll(grad, 64, 1) * sin_signed) * gain
    return r * d_norm - raw * ((r * r * r) * jnp.mean(raw * d_norm, axis=-1, keepdims=True))


def mm(a, b):
    return lax.dot_general(a, b, (((1,), (0,)), ((), ())), preferred_element_type=F32)


def mm_t(a, b):
    return lax.dot_general(a, b, (((1,), (1,)), ((), ())), preferred_element_type=F32)


def attention_kernel(
    shard_ref, q_ref, do_ref, k0_ref, k1_ref, k2_ref, v0_ref, v1_ref, v2_ref,
    qg_ref, kg_ref, cb_ref, sb_ref, cl_ref, sl_ref,
    qgrad_ref, attn_ref, dk_ref, dv_ref, back1_ref, back2_ref,
    kp, vx, cos, sin, e_sc, dp_sc, dkt, dvt,
):
    tile = pl.program_id(1)
    shard = shard_ref[0]

    @pl.when((pl.program_id(0) == 0) & (tile == 0))
    def _():
        lane = lax.broadcasted_iota(jnp.int32, (1, HD), 1)
        sign = jnp.where(lane < HD // 2, -1.0, 1.0)
        for part in range(3):
            cb = cb_ref[pl.ds(shard + part, 1), :]
            sb = sb_ref[pl.ds(shard + part, 1), :]
            rows = slice(part * TOK, (part + 1) * TOK)
            cos[rows, :] = cb * cl_ref[...] - sb * sl_ref[...]
            sin[rows, :] = (sb * cl_ref[...] + cb * sl_ref[...]) * sign

    @pl.when(tile == 0)
    def _():
        for part, (k_ref, v_ref) in enumerate(((k2_ref, v2_ref), (k1_ref, v1_ref), (k0_ref, v0_ref))):
            rows = slice(part * TOK, (part + 1) * TOK)
            raw = k_ref[...].astype(F32)
            normed = raw * norm_scale(raw) * kg_ref[...]
            kp[rows, :] = rope_forward(normed, cos[rows, :], sin[rows, :]).astype(BF16)
            vx[rows, :] = v_ref[...]
        dkt[...] = jnp.zeros_like(dkt)
        dvt[...] = jnp.zeros_like(dvt)

    q_rows = pl.ds(pl.multiple_of(2 * TOK + tile * QT, QT), QT)
    cos_q = cos[q_rows, :]
    sin_q = sin[q_rows, :]
    q_parts = []
    for g in range(2):
        raw = q_ref[:, g * HD : (g + 1) * HD].astype(F32)
        normed = raw * norm_scale(raw) * qg_ref[...]
        q_parts.append(rope_forward(normed, cos_q, sin_q))
    q = jnp.concatenate(q_parts, axis=0)
    d_out = jnp.concatenate([do_ref[:, :HD], do_ref[:, HD:]], axis=0)
    q_low = q.astype(BF16)
    q_t = q.T.astype(BF16)
    do_t = d_out.astype(F32).T.astype(BF16)

    rows_i = lax.broadcasted_iota(jnp.int32, (QT, KB), 0)
    cols_i = lax.broadcasted_iota(jnp.int32, (QT, KB), 1)
    lower = (cols_i <= rows_i).astype(F32)
    upper = 1.0 - lower
    lower = jnp.concatenate([lower, lower], axis=0)
    upper = jnp.concatenate([upper, upper], axis=0)

    l_acc = jnp.zeros((2 * QT, HD), F32)
    u_acc = jnp.zeros((2 * QT, HD), F32)
    for b in range(NBLK):
        at = pl.ds(pl.multiple_of(tile * QT + b * KB, KB), KB)
        cols = slice(b * KB, (b + 1) * KB)
        s = mm_t(q_low, kp[at, :])
        e = jnp.exp2(s * (score_scale * LOG2E))
        key_shard = shard - 2 + (tile * QT + b * KB) // TOK
        if b == 0:
            e = e * (upper * jnp.where(key_shard >= 0, 1.0, 0.0))
        elif b == NBLK - 1:
            e = e * lower
        else:
            e = e * jnp.where(key_shard >= 0, 1.0, 0.0)
        dp = mm_t(d_out, vx[at, :])
        ed = e * dp
        l_acc = l_acc + e[:, :HD] + e[:, HD:]
        u_acc = u_acc + ed[:, :HD] + ed[:, HD:]
        e_sc[:, cols] = e
        dp_sc[:, cols] = dp
    inv = 1.0 / jnp.sum(l_acc, axis=-1, keepdims=True)
    delta = jnp.sum(u_acc, axis=-1, keepdims=True) * inv

    out = jnp.zeros((2 * QT, HD), F32)
    dq = jnp.zeros((2 * QT, HD), F32)
    for b in range(NBLK):
        at = pl.ds(pl.multiple_of(tile * QT + b * KB, KB), KB)
        cols = slice(b * KB, (b + 1) * KB)
        p = e_sc[:, cols] * inv
        ds = (p * (dp_sc[:, cols] - delta)).astype(BF16)
        p = p.astype(BF16)
        out = out + mm(p, vx[at, :])
        dq = dq + mm(ds, kp[at, :])
        dvt[:, at] += mm(do_t, p)
        dkt[:, at] += mm(q_t, ds)
    for g in range(2):
        rows = slice(g * QT, (g + 1) * QT)
        lanes = slice(g * HD, (g + 1) * HD)
        attn_ref[:, lanes] = out[rows].astype(BF16)
        raw = q_ref[:, lanes].astype(F32)
        qgrad_ref[:, lanes] = prep_back(
            raw, qg_ref[...], cos_q, sin_q, dq[rows] * score_scale
        ).astype(BF16)

    @pl.when(tile == 1)
    def _():
        for part, k_ref in enumerate((k2_ref, k1_ref, k0_ref)):
            rows = slice(part * TOK, (part + 1) * TOK)
            raw = k_ref[...].astype(F32)
            dk = prep_back(
                raw, kg_ref[...], cos[rows, :], sin[rows, :], dkt[:, rows].T * score_scale
            )
            dv = dvt[:, rows].T
            if part == 2:
                dk_ref[...] = dk
                dv_ref[...] = dv
            else:
                back = back2_ref if part == 0 else back1_ref
                back[0, 0] = dk.astype(BF16)
                back[0, 1] = dv.astype(BF16)


def attention(shard, q_raw, d_out, k_raw, values, kv1, kv2, q_gain, k_gain, tables):
    whole = lambda a: pl.BlockSpec(a.shape, lambda h, t: (0,) * a.ndim)
    tile_spec = pl.BlockSpec((QT, 2 * HD), lambda h, t: (t, h))
    k_spec = pl.BlockSpec((TOK, HD), lambda h, t: (0, h))
    v_spec = pl.BlockSpec((TOK, HD), lambda h, t: (0, 2 + h))
    back_spec = pl.BlockSpec((1, 2, TOK, HD), lambda h, t: (h, 0, 0, 0))
    back_shape = jax.ShapeDtypeStruct((2, 2, TOK, HD), BF16)
    gains = [q_gain[None, :], k_gain[None, :]]
    return pl.pallas_call(
        attention_kernel,
        grid=(2, 2),
        in_specs=[
            pl.BlockSpec(memory_space=pltpu.SMEM),
            tile_spec, tile_spec,
            k_spec, k_spec, k_spec, k_spec, v_spec, v_spec,
        ] + [whole(a) for a in gains + tables],
        out_specs=[tile_spec, tile_spec, k_spec, k_spec, back_spec, back_spec],
        out_shape=[
            jax.ShapeDtypeStruct((TOK, 4 * HD), BF16),
            jax.ShapeDtypeStruct((TOK, 4 * HD), BF16),
            jax.ShapeDtypeStruct((TOK, 2 * HD), F32),
            jax.ShapeDtypeStruct((TOK, 2 * HD), F32),
            back_shape, back_shape,
        ],
        scratch_shapes=[
            pltpu.VMEM((SPAN, HD), BF16),
            pltpu.VMEM((SPAN, HD), BF16),
            pltpu.VMEM((SPAN, HD), F32),
            pltpu.VMEM((SPAN, HD), F32),
            pltpu.VMEM((2 * QT, NBLK * KB), F32),
            pltpu.VMEM((2 * QT, NBLK * KB), F32),
            pltpu.VMEM((HD, SPAN), F32),
            pltpu.VMEM((HD, SPAN), F32),
        ],
        compiler_params=pltpu.CompilerParams(vmem_limit_bytes=40 << 20),
        cost_estimate=pl.CostEstimate(
            flops=6 * 4 * 2 * TOK * SPAN * HD, bytes_accessed=6 << 20, transcendentals=4 * TOK * SPAN
        ),
    )(shard, q_raw, d_out, k_raw, kv1, kv2, values, kv1, kv2, *gains, *tables)


def sketch_kernel(x0_ref, x1_ref, x2_ref, y_ref, qgrad_ref, attn_ref, dk_ref, dv_ref, b1_ref, b2_ref, out_ref):
    def tokens(a, b):
        return lax.dot_general(a, b, (((0,), (0,)), ((), ())), preferred_element_type=F32)

    x0, x1, x2 = x0_ref[...], x1_ref[...], x2_ref[...]
    out_ref[:, 0 : 4 * HD] = tokens(x0, qgrad_ref[...]).astype(BF16)
    out_ref[:, 8 * HD : 12 * HD] = tokens(y_ref[...], attn_ref[...]).astype(BF16)
    for kind, own_ref in enumerate((dk_ref, dv_ref)):
        for h in range(2):
            total = tokens(x0, own_ref[:, h * HD : (h + 1) * HD].astype(BF16))
            total += tokens(x1, b1_ref[h, kind])
            total += tokens(x2, b2_ref[h, kind])
            at = (4 + 2 * kind + h) * HD
            out_ref[:, at : at + HD] = total.astype(BF16)


def sketch(*args):
    return pl.pallas_call(
        sketch_kernel,
        out_shape=jax.ShapeDtypeStruct((HD, 12 * HD), BF16),
        compiler_params=pltpu.CompilerParams(vmem_limit_bytes=24 << 20),
        cost_estimate=pl.CostEstimate(
            flops=2 * TOK * HD * 16 * HD, bytes_accessed=5 << 20, transcendentals=0
        ),
    )(*args)


def shift(x, by):
    count = lax.axis_size("seq")
    pairs = [(i, i + by) for i in range(count) if 0 <= i + by < count]
    return lax.ppermute(x, "seq", pairs)


def swap(x, bit):
    count = lax.axis_size("head")
    return lax.ppermute(x, "head", [(i, i ^ bit) for i in range(count)])


def sum_over_head(partial_x, partial_y):
    first = lax.axis_index("head") % 2 == 0
    got = swap(jnp.where(first, partial_y, partial_x).astype(BF16), 1)
    total = jnp.where(first, partial_x, partial_y) + got.astype(F32)
    for bit in (2, 4):
        total = total + swap(total.astype(BF16), bit).astype(F32)
    mine = total.astype(BF16)
    other = swap(mine, 1)
    return jnp.where(first, mine, other), jnp.where(first, other, mine)


def per_device(
    layer_input, omega_in, upstream, omega_out, q_raw, k_raw, values, d_out, q_gain, k_gain
):
    kv = jnp.concatenate([k_raw, values], axis=1)
    kv2 = shift(kv, 2)
    kv1 = shift(kv, 1)
    partial_x = jnp.dot(layer_input, omega_in, preferred_element_type=F32)
    partial_y = jnp.dot(upstream, omega_out, preferred_element_type=F32)
    x0, y0 = sum_over_head(partial_x, partial_y)
    x1 = shift(x0, 1)
    x2 = shift(x0, 2)
    shard = lax.axis_index("seq").astype(jnp.int32)[None]
    tables = [jnp.asarray(t) for t in rope_tables(lax.axis_size("seq"))]
    query_grad, attn_out, dk, dv, back1, back2 = attention(
        shard, q_raw, d_out, k_raw, values, kv1, kv2, q_gain, k_gain, tables
    )
    got2 = shift(back2, -2)
    got1 = shift(back1, -1)
    sketches = sketch(x0, x1, x2, y0, query_grad, attn_out, dk, dv, back1, back2)
    shards = lax.axis_size("seq")
    pieces = lax.all_to_all(sketches.reshape(shards, HD // shards, 12 * HD), "seq", 0, 0, tiled=True)
    total = jnp.sum(pieces.astype(F32), axis=0)

    def finish(own, kind):
        far = (got1[:, kind].astype(F32) + got2[:, kind].astype(F32)).transpose(1, 0, 2)
        return (own + far.reshape(own.shape)).astype(BF16)

    q_cols, kv_cols = 4 * HD, 2 * HD
    return (
        query_grad,
        finish(dk, 0),
        finish(dv, 1),
        total[:, :q_cols],
        total[:, q_cols : q_cols + kv_cols],
        total[:, q_cols + kv_cols : q_cols + 2 * kv_cols],
        total[:, q_cols + 2 * kv_cols :],
    )


def solution(mesh):
    split = P("seq", "head")
    in_specs = (split, P("head", None), split, P("head", None), split, split, split, split, P(), P())
    return jax.shard_map(
        per_device, mesh=mesh, in_specs=in_specs, out_specs=(split,) * 7, check_vma=False
    )
```

time: 836 us -> 126 us (0.15)
  the two profiles are of different devices: /device:TPU:128 before, /device:TPU:12 now
where the time goes in v1:
time: 126 us
  starting transfers between devices  52.5 us (42%)
  waiting for transfers between devices  37 us (29%)
  Pallas kernels  20.1 us (16%)
  local copies, waits for them, and re-layouts  9.37 us (7%)
  other arithmetic  3.52 us (3%)
  matrix products  2.02 us (2%)
    ppermute x6, starting transfers between devices, shift(): return lax.ppermute(x, 'seq', pairs)  19.2 us
    ppermute x4, starting transfers between devices, swap(): return lax.ppermute(x, 'head', [(i, i ^ bit) for i in range(count)])  18.6 us
    pallas_call x1, Pallas kernels, attention(): pl.pallas_call(attention_kernel, grid=(2, 2), in_specs=[pl.BlockSpec(memo...  18.3 us
    ppermute x4, waiting for transfers between devices, swap(): return lax.ppermute(x, 'head', [(i, i ^ bit) for i in range(count)])  16 us
    all_to_all x1, starting transfers between devices, per_device(): lax.all_to_all(sketches.reshape(shards, HD // shards, 12 * HD), 'seq', 0,...  14.7 us
    all_to_all x1, waiting for transfers between devices, per_device(): lax.all_to_all(sketches.reshape(shards, HD // shards, 12 * HD), 'seq', 0,...  13.2 us
    ppermute x6, waiting for transfers between devices, shift(): return lax.ppermute(x, 'seq', pairs)  7.75 us
    unnamed x35, local copies, waits for them, and re-layouts  6.46 us
  transfers between devices with their start and end apart: 11, of which 5 were waited for; matrix products, arithmetic and copies ran while one was open for 3% of the time, Pallas kernels for 16%

profile of v1, /device:TPU:12, one launch (start us, length us, event | category | flops | bytes accessed | tf_op | source)
XLA Modules:
  0.0 125.5 jit_solution(4695989847250184391)
XLA Ops:
  0.7 1.6 %fusion.4 = f32[512,128]{1,0:T(8,128)S(1)} fusion(bf16[512,672]{0,1:T(8,128)(2,1)} %param.14, bf16[672,128]{1,0:T(8,128)(2,1)} %param.15), kind=kOutput, calls=%fused_computation.17 | convolution fusion | flops 88080384 | bytes 1122304 | tf_op jit(solution)/shard_map/dot_general | solution.py:267
  2.7 1.9 %collective-permute-start.4 = (bf16[512,128]{1,0:T(8,128)(2,1)S(1)}, bf16[512,128]{1,0:T(8,128)(2,1)S(1)}, u32[]{:S(2)}, u32[]{:S(2)}) collective-permute-start(bf16[512,128]{1,0:T(8,128)(2,1)S(1)} %get-tuple-element.29), channel_id=1, source_target_pairs={{0,1},{1,0},{2,3},{3,2},{4,5},{5,4},{6,7},{7,6},{8,9},{9,8},{10,11... | collective-permute-start | bytes 393224 | tf_op jit(solution)/shard_map/ppermute | solution.py:247
  4.7 1.3 %collective-permute-done.4 = bf16[512,128]{1,0:T(8,128)(2,1)S(1)} collective-permute-done((bf16[512,128]{1,0:T(8,128)(2,1)S(1)}, bf16[512,128]{1,0:T(8,128)(2,1)S(1)}, u32[]{:S(2)}, u32[]{:S(2)}) %collective-permute-start.4) | collective-permute-done | bytes 131104 | tf_op jit(solution)/shard_map/ppermute | solution.py:247
  6.0 6.2 %collective-permute-start.5 = (bf16[512,128]{1,0:T(8,128)(2,1)S(1)}, bf16[512,128]{1,0:T(8,128)(2,1)S(1)}, u32[]{:S(2)}, u32[]{:S(2)}) collective-permute-start(bf16[512,128]{1,0:T(8,128)(2,1)S(1)} %get-tuple-element.19), channel_id=1, source_target_pairs={{0,2},{1,3},{2,0},{3,1},{4,6},{5,7},{6,4},{7,5},{8,10},{9,11},{10,... | collective-permute-start | bytes 393224 | tf_op jit(solution)/shard_map/ppermute | solution.py:247
  12.3 3.1 %collective-permute-start.1 = (bf16[512,512]{1,0:T(8,128)(2,1)S(1)}, bf16[512,512]{1,0:T(8,128)(2,1)S(1)}, u32[]{:S(2)}, u32[]{:S(2)}) collective-permute-start(bf16[512,512]{1,0:T(8,128)(2,1)S(1)} %constant_dynamic-update-slice_fusion), channel_id=1, source_target_pairs={{0,16},{8,24},{16,32},{24,40},{32,48},{40,56},{48,64},{56,72},{64,... | collective-permute-start | bytes 1572872 | tf_op jit(solution)/shard_map/ppermute | solution.py:242
  15.4 4.3 %collective-permute-start = (bf16[512,512]{1,0:T(8,128)(2,1)S(1)}, bf16[512,512]{1,0:T(8,128)(2,1)S(1)}, u32[]{:S(2)}, u32[]{:S(2)}) collective-permute-start(bf16[512,512]{1,0:T(8,128)(2,1)S(1)} %constant_dynamic-update-slice_fusion), channel_id=1, source_target_pairs={{0,8},{8,16},{16,24},{24,32},{32,40},{40,48},{48,56},{56,64},{64,7... | collective-permute-start | bytes 1572872 | tf_op jit(solution)/shard_map/ppermute | solution.py:242
  19.8 8.5 %collective-permute-start.6 = (bf16[512,128]{1,0:T(8,128)(2,1)S(1)}, bf16[512,128]{1,0:T(8,128)(2,1)S(1)}, u32[]{:S(2)}, u32[]{:S(2)}) collective-permute-start(bf16[512,128]{1,0:T(8,128)(2,1)S(1)} %fusion), channel_id=1, source_target_pairs={{0,4},{1,5},{2,6},{3,7},{4,0},{5,1},{6,2},{7,3},{8,12},{9,13},{10,... | collective-permute-start | bytes 393224 | tf_op jit(solution)/shard_map/ppermute | solution.py:247
  28.3 14.7 %collective-permute-done.6 = bf16[512,128]{1,0:T(8,128)(2,1)S(1)} collective-permute-done((bf16[512,128]{1,0:T(8,128)(2,1)S(1)}, bf16[512,128]{1,0:T(8,128)(2,1)S(1)}, u32[]{:S(2)}, u32[]{:S(2)}) %collective-permute-start.6) | collective-permute-done | bytes 131104 | tf_op jit(solution)/shard_map/ppermute | solution.py:247
  43.1 1.9 %collective-permute-start.7 = (bf16[512,128]{1,0:T(8,128)(2,1)S(1)}, bf16[512,128]{1,0:T(8,128)(2,1)S(1)}, u32[]{:S(2)}, u32[]{:S(2)}) collective-permute-start(bf16[512,128]{1,0:T(8,128)(2,1)S(1)} %add_convert_fusion.2), channel_id=1, source_target_pairs={{0,1},{1,0},{2,3},{3,2},{4,5},{5,4},{6,7},{7,6},{8,9},{9,8},{10,11... | collective-permute-start | bytes 393224 | tf_op jit(solution)/shard_map/ppermute | solution.py:247
  47.3 1.0 copy-done.4
  48.3 1.0 copy-done.5
  49.4 1.0 copy-done.7
  50.4 1.0 copy-done.9
  51.5 18.3 %shard_map.189 = (bf16[512,512]{1,0:T(8,128)(2,1)}, bf16[512,512]{1,0:T(8,128)(2,1)S(1)}, f32[512,256]{1,0:T(8,128)S(1)}, f32[512,256]{1,0:T(8,128)S(1)}, bf16[2...) custom-call(s32[1]{0:T(128)} %bitcast.shard_ref, bf16[512,512]{1,0:T(8,128)(2,1)S(1)} %copy-done.4, ...), custom_call_target="tpu_custom_call" | custom-call | flops 4831838208 | bytes 6291456 | tf_op jit(solution)/shard_map/pallas_call | solution.py:179
  69.8 2.1 %collective-permute-start.2 = (bf16[2,2,512,128]{3,2,1,0:T(8,128)(2,1)}, bf16[2,2,512,128]{3,2,1,0:T(8,128)(2,1)S(1)}, u32[]{:S(2)}, u32[]{:S(2)}) collective-permute-start(bf16[2,2,512,128]{3,2,1,0:T(8,128)(2,1)} %get-tuple-element.15.b1_ref), channel_id=1, source_target_pairs={{8,0},{16,8},{24,16},{32,24},{40,32},{48,40},{56,48},{64,56},{72,6... | collective-permute-start | bytes 1572872 | tf_op jit(solution)/shard_map/ppermute | solution.py:242
  71.9 2.7 %collective-permute-start.3 = (bf16[2,2,512,128]{3,2,1,0:T(8,128)(2,1)S(1)}, bf16[2,2,512,128]{3,2,1,0:T(8,128)(2,1)}, u32[]{:S(2)}, u32[]{:S(2)}) collective-permute-start(bf16[2,2,512,128]{3,2,1,0:T(8,128)(2,1)S(1)} %get-tuple-element.16.b2_ref), channel_id=1, source_target_pairs={{16,0},{24,8},{32,16},{40,24},{48,32},{56,40},{64,48},{72,56},{80,... | collective-permute-start | bytes 1572872 | tf_op jit(solution)/shard_map/ppermute | solution.py:242
  74.7 3.1 %collective-permute-start.9 = (bf16[512,128]{1,0:T(8,128)(2,1)S(1)}, bf16[512,128]{1,0:T(8,128)(2,1)S(1)}, u32[]{:S(2)}, u32[]{:S(2)}) collective-permute-start(bf16[512,128]{1,0:T(8,128)(2,1)S(1)} %get-tuple-element.24.x0_ref), channel_id=1, source_target_pairs={{0,16},{8,24},{16,32},{24,40},{32,48},{40,56},{48,64},{56,72},{64,... | collective-permute-start | bytes 393224 | tf_op jit(solution)/shard_map/ppermute | solution.py:242
  77.8 3.9 %collective-permute-start.8 = (bf16[512,128]{1,0:T(8,128)(2,1)S(1)}, bf16[512,128]{1,0:T(8,128)(2,1)S(1)}, u32[]{:S(2)}, u32[]{:S(2)}) collective-permute-start(bf16[512,128]{1,0:T(8,128)(2,1)S(1)} %get-tuple-element.24.x0_ref), channel_id=1, source_target_pairs={{0,8},{8,16},{16,24},{24,32},{32,40},{40,48},{48,56},{56,64},{64,7... | collective-permute-start | bytes 393224 | tf_op jit(solution)/shard_map/ppermute | solution.py:242
  82.1 7.3 %collective-permute-done.8.x1_ref = bf16[512,128]{1,0:T(8,128)(2,1)S(1)} collective-permute-done((bf16[512,128]{1,0:T(8,128)(2,1)S(1)}, bf16[512,128]{1,0:T(8,128)(2,1)S(1)}, u32[]{:S(2)}, u32[]{:S(2)}) %collective-permute-start.8) | collective-permute-done | bytes 131104 | tf_op jit(solution)/shard_map/ppermute | solution.py:242
  89.4 1.8 %shard_map.190 = bf16[128,1536]{1,0:T(8,128)(2,1)S(1)} custom-call(bf16[512,128]{1,0:T(8,128)(2,1)S(1)} %get-tuple-element.24.x0_ref, bf16[512,128]{1,0:T(8,128)(2,1)S(1)} %collective-permute-done.8.x1_ref, bf16[512,128]{1,0:T(8,128)(2,1)S(1)} %collective-permute-done.9.x2_ref, bf16[512,128]{1,0:T(8,128)(2,1)S(1)} %get-tuple-element.23.y_ref, ...), custom_call_target="tpu_custom_call" | custom-call | flops 268435456 | bytes 5242880 | tf_op jit(solution)/shard_map/pallas_call | solution.py:229
  92.1 14.7 %all-to-all-start = ((bf16[64,2,1536]{2,1,0:T(2,128)(2,1)}), bf16[64,2,1536]{2,1,0:T(2,128)(2,1)}, u32[]{:S(2)}, u32[]{:S(2)}) async-start(bf16[64,2,1536]{2,1,0:T(2,128)(2,1)} %reshape.31), calls=%async_computation | async-start | bytes 786432 | tf_op jit(solution)/shard_map/all_to_all | solution.py:281
  106.9 1.1 add_bitcast_fusion
  109.7 13.2 %all-to-all-done = bf16[64,2,1536]{2,1,0:T(2,128)(2,1)} async-done(((bf16[64,2,1536]{2,1,0:T(2,128)(2,1)}), bf16[64,2,1536]{2,1,0:T(2,128)(2,1)}, u32[]{:S(2)}, u32[]{:S(2)}) %all-to-all-start) | async-done | bytes 393248 | tf_op jit(solution)/shard_map/all_to_all | solution.py:281
  123.0 1.3 %convert_reduce_fusion = f32[2,1536]{1,0:T(2,128)S(1)} fusion(bf16[64,2,1536]{2,1,0:T(2,128)(2,1)} %all-to-all-done), kind=kLoop, calls=%fused_computation | loop fusion | flops 390144 | bytes 405504 | tf_op jit(solution)/shard_map/reduce_sum | solution.py:282
  (52 shorter events, 7.2 us)
Async XLA Ops:
  0.6 1.7 %copy-start = (bf16[512,672]{0,1:T(8,128)(2,1)S(1)}, bf16[512,672]{0,1:T(8,128)(2,1)}, u32[]{:S(2)}) copy-start(bf16[512,672]{0,1:T(8,128)(2,1)} %param.16) | copy-start | bytes 2064388
  0.7 1.6 %copy-start.16 = (bf16[672,128]{1,0:T(8,128)(2,1)S(1)}, bf16[672,128]{1,0:T(8,128)(2,1)}, u32[]{:S(2)}) copy-start(bf16[672,128]{1,0:T(8,128)(2,1)} %param.17) | copy-start | bytes 516100
  2.7 3.2 %collective-permute-start.4 = (bf16[512,128]{1,0:T(8,128)(2,1)S(1)}, bf16[512,128]{1,0:T(8,128)(2,1)S(1)}, u32[]{:S(2)}, u32[]{:S(2)}) collective-permute-start(bf16[512,128]{1,0:T(8,128)(2,1)S(1)} %get-tuple-element.29), channel_id=1, source_target_pairs={{0,1},{1,0},{2,3},{3,2},{4,5},{5,4},{6,7},{7,6},{8,9},{9,8},{10,11... | collective-permute-start | bytes 393224 | tf_op jit(solution)/shard_map/ppermute | solution.py:247
  6.0 6.3 %copy-start.2 = (bf16[512,256]{1,0:T(8,128)(2,1)S(1)}, bf16[512,256]{1,0:T(8,128)(2,1)}, u32[]{:S(2)}) copy-start(bf16[512,256]{1,0:T(8,128)(2,1)} %k0_ref.1) | copy-start | bytes 786436
  6.0 6.3 %copy-start.3 = (bf16[512,256]{1,0:T(8,128)(2,1)S(1)}, bf16[512,256]{1,0:T(8,128)(2,1)}, u32[]{:S(2)}) copy-start(bf16[512,256]{1,0:T(8,128)(2,1)} %v0_ref.1) | copy-start | bytes 786436
  6.0 13.7 %collective-permute-start.5 = (bf16[512,128]{1,0:T(8,128)(2,1)S(1)}, bf16[512,128]{1,0:T(8,128)(2,1)S(1)}, u32[]{:S(2)}, u32[]{:S(2)}) collective-permute-start(bf16[512,128]{1,0:T(8,128)(2,1)S(1)} %get-tuple-element.19), channel_id=1, source_target_pairs={{0,2},{1,3},{2,0},{3,1},{4,6},{5,7},{6,4},{7,5},{8,10},{9,11},{10,... | collective-permute-start | bytes 393224 | tf_op jit(solution)/shard_map/ppermute | solution.py:247
  12.3 32.7 %collective-permute-start.1 = (bf16[512,512]{1,0:T(8,128)(2,1)S(1)}, bf16[512,512]{1,0:T(8,128)(2,1)S(1)}, u32[]{:S(2)}, u32[]{:S(2)}) collective-permute-start(bf16[512,512]{1,0:T(8,128)(2,1)S(1)} %constant_dynamic-update-slice_fusion), channel_id=1, source_target_pairs={{0,16},{8,24},{16,32},{24,40},{32,48},{40,56},{48,64},{56,72},{64,... | collective-permute-start | bytes 1572872 | tf_op jit(solution)/shard_map/ppermute | solution.py:242
  15.4 30.4 %collective-permute-start = (bf16[512,512]{1,0:T(8,128)(2,1)S(1)}, bf16[512,512]{1,0:T(8,128)(2,1)S(1)}, u32[]{:S(2)}, u32[]{:S(2)}) collective-permute-start(bf16[512,512]{1,0:T(8,128)(2,1)S(1)} %constant_dynamic-update-slice_fusion), channel_id=1, source_target_pairs={{0,8},{8,16},{16,24},{24,32},{32,40},{40,48},{48,56},{56,64},{64,7... | collective-permute-start | bytes 1572872 | tf_op jit(solution)/shard_map/ppermute | solution.py:242
  19.8 23.3 %collective-permute-start.6 = (bf16[512,128]{1,0:T(8,128)(2,1)S(1)}, bf16[512,128]{1,0:T(8,128)(2,1)S(1)}, u32[]{:S(2)}, u32[]{:S(2)}) collective-permute-start(bf16[512,128]{1,0:T(8,128)(2,1)S(1)} %fusion), channel_id=1, source_target_pairs={{0,4},{1,5},{2,6},{3,7},{4,0},{5,1},{6,2},{7,3},{8,12},{9,13},{10,... | collective-permute-start | bytes 393224 | tf_op jit(solution)/shard_map/ppermute | solution.py:247
  28.3 18.4 %copy-start.12 = (f32[512,128]{1,0:T(8,128)S(1)}, f32[512,128]{1,0:T(8,128)}, u32[]{:S(2)}) copy-start(f32[512,128]{1,0:T(8,128)} %constant.36.clone.sl_ref) | copy-start | bytes 786436
  28.3 18.3 %copy-start.13 = (f32[512,128]{1,0:T(8,128)S(1)}, f32[512,128]{1,0:T(8,128)}, u32[]{:S(2)}) copy-start(f32[512,128]{1,0:T(8,128)} %constant.35.clone.cl_ref) | copy-start | bytes 786436
  28.3 18.3 %copy-start.14 = (f32[72,128]{1,0:T(8,128)S(1)}, f32[72,128]{1,0:T(8,128)}, u32[]{:S(2)}) copy-start(f32[72,128]{1,0:T(8,128)} %constant.34.clone.sb_ref) | copy-start | bytes 110596
  28.3 18.3 %copy-start.15 = (f32[72,128]{1,0:T(8,128)S(1)}, f32[72,128]{1,0:T(8,128)}, u32[]{:S(2)}) copy-start(f32[72,128]{1,0:T(8,128)} %constant.33.clone.cb_ref) | copy-start | bytes 110596
  43.1 31.5 %collective-permute-start.7 = (bf16[512,128]{1,0:T(8,128)(2,1)S(1)}, bf16[512,128]{1,0:T(8,128)(2,1)S(1)}, u32[]{:S(2)}, u32[]{:S(2)}) collective-permute-start(bf16[512,128]{1,0:T(8,128)(2,1)S(1)} %add_convert_fusion.2), channel_id=1, source_target_pairs={{0,1},{1,0},{2,3},{3,2},{4,5},{5,4},{6,7},{7,6},{8,9},{9,8},{10,11... | collective-permute-start | bytes 393224 | tf_op jit(solution)/shard_map/ppermute | solution.py:247
  47.3 1.0 copy-start.4
  48.3 1.0 copy-start.5
  49.4 1.0 copy-start.7
  50.4 1.0 copy-start.9
  69.8 19.6 %copy-start.1 = (bf16[512,512]{1,0:T(8,128)(2,1)S(1)}, bf16[512,512]{1,0:T(8,128)(2,1)}, u32[]{:S(2)}) copy-start(bf16[512,512]{1,0:T(8,128)(2,1)} %get-tuple-element.6.qgrad_ref) | copy-start | bytes 1572868
  69.8 37.1 %collective-permute-start.2 = (bf16[2,2,512,128]{3,2,1,0:T(8,128)(2,1)}, bf16[2,2,512,128]{3,2,1,0:T(8,128)(2,1)S(1)}, u32[]{:S(2)}, u32[]{:S(2)}) collective-permute-start(bf16[2,2,512,128]{3,2,1,0:T(8,128)(2,1)} %get-tuple-element.15.b1_ref), channel_id=1, source_target_pairs={{8,0},{16,8},{24,16},{32,24},{40,32},{48,40},{56,48},{64,56},{72,6... | collective-permute-start | bytes 1572872 | tf_op jit(solution)/shard_map/ppermute | solution.py:242
  71.9 35.0 %collective-permute-start.3 = (bf16[2,2,512,128]{3,2,1,0:T(8,128)(2,1)S(1)}, bf16[2,2,512,128]{3,2,1,0:T(8,128)(2,1)}, u32[]{:S(2)}, u32[]{:S(2)}) collective-permute-start(bf16[2,2,512,128]{3,2,1,0:T(8,128)(2,1)S(1)} %get-tuple-element.16.b2_ref), channel_id=1, source_target_pairs={{16,0},{24,8},{32,16},{40,24},{48,32},{56,40},{64,48},{72,56},{80,... | collective-permute-start | bytes 1572872 | tf_op jit(solution)/shard_map/ppermute | solution.py:242
  74.7 7.4 %collective-permute-start.9 = (bf16[512,128]{1,0:T(8,128)(2,1)S(1)}, bf16[512,128]{1,0:T(8,128)(2,1)S(1)}, u32[]{:S(2)}, u32[]{:S(2)}) collective-permute-start(bf16[512,128]{1,0:T(8,128)(2,1)S(1)} %get-tuple-element.24.x0_ref), channel_id=1, source_target_pairs={{0,16},{8,24},{16,32},{24,40},{32,48},{40,56},{48,64},{56,72},{64,... | collective-permute-start | bytes 393224 | tf_op jit(solution)/shard_map/ppermute | solution.py:242
  77.8 11.6 %collective-permute-start.8 = (bf16[512,128]{1,0:T(8,128)(2,1)S(1)}, bf16[512,128]{1,0:T(8,128)(2,1)S(1)}, u32[]{:S(2)}, u32[]{:S(2)}) collective-permute-start(bf16[512,128]{1,0:T(8,128)(2,1)S(1)} %get-tuple-element.24.x0_ref), channel_id=1, source_target_pairs={{0,8},{8,16},{16,24},{24,32},{32,40},{40,48},{48,56},{56,64},{64,7... | collective-permute-start | bytes 393224 | tf_op jit(solution)/shard_map/ppermute | solution.py:242
  92.1 30.9 %all-to-all-start = ((bf16[64,2,1536]{2,1,0:T(2,128)(2,1)}), bf16[64,2,1536]{2,1,0:T(2,128)(2,1)}, u32[]{:S(2)}, u32[]{:S(2)}) async-start(bf16[64,2,1536]{2,1,0:T(2,128)(2,1)} %reshape.31), calls=%async_computation | async-start | bytes 786432 | tf_op jit(solution)/shard_map/all_to_all | solution.py:281
  (4 other events, 2.9 us)

commit v2 on v1

--- a/solution.py
+++ b/solution.py
@@ -11,6 +11,7 @@
 TOK = 512
 QT = 256
 KB = 256
+ATTN_VMEM = 60 << 20
 SPAN = 1536
 NBLK = 5
 score_scale = 168.0 ** (-0.5)
@@ -55,13 +56,17 @@
 
 
 def attention_kernel(
-    shard_ref, q_ref, do_ref, k0_ref, k1_ref, k2_ref, v0_ref, v1_ref, v2_ref,
-    qg_ref, kg_ref, cb_ref, sb_ref, cl_ref, sl_ref,
-    qgrad_ref, attn_ref, dk_ref, dv_ref, back1_ref, back2_ref,
-    kp, vx, cos, sin, e_sc, dp_sc, dkt, dvt,
+    shard_ref, q_ref, do_ref, k0_ref, v0_ref, kv1_ref, kv2_ref,
+    x0_ref, x1_ref, x2_ref, y_ref, qg_ref, kg_ref, cb_ref, sb_ref, cl_ref, sl_ref,
+    qgrad_ref, own_ref, back1_ref, back2_ref, sk_ref,
+    kp, vx, cos, sin, e_sc, dp_sc, dkt, dvt, xt, yt, skq, sko,
 ):
     tile = pl.program_id(1)
     shard = shard_ref[0]
+    k_lanes = pl.ds(pl.multiple_of(pl.program_id(0) * HD, HD), HD)
+    v_lanes = pl.ds(pl.multiple_of(pl.program_id(0) * HD + 2 * HD, HD), HD)
+    k_parts = (kv2_ref.at[:, k_lanes], kv1_ref.at[:, k_lanes], k0_ref)
+    v_parts = (kv2_ref.at[:, v_lanes], kv1_ref.at[:, v_lanes], v0_ref)
 
     @pl.when((pl.program_id(0) == 0) & (tile == 0))
     def _():
@@ -74,9 +79,15 @@
             cos[rows, :] = cb * cl_ref[...] - sb * sl_ref[...]
             sin[rows, :] = (sb * cl_ref[...] + cb * sl_ref[...]) * sign
 
+        for part, x_ref in enumerate((x2_ref, x1_ref, x0_ref)):
+            xt[:, part * TOK : (part + 1) * TOK] = x_ref[...].astype(F32).T.astype(BF16)
+        yt[...] = y_ref[...].astype(F32).T.astype(BF16)
+
     @pl.when(tile == 0)
     def _():
-        for part, (k_ref, v_ref) in enumerate(((k2_ref, v2_ref), (k1_ref, v1_ref), (k0_ref, v0_ref))):
+        skq[...] = jnp.zeros_like(skq)
+        sko[...] = jnp.zeros_like(sko)
+        for part, (k_ref, v_ref) in enumerate(zip(k_parts, v_parts)):
             rows = slice(part * TOK, (part + 1) * TOK)
             raw = k_ref[...].astype(F32)
             normed = raw * norm_scale(raw) * kg_ref[...]
@@ -141,57 +152,56 @@
         dq = dq + mm(ds, kp[at, :])
         dvt[:, at] += mm(do_t, p)
         dkt[:, at] += mm(q_t, ds)
+    x_tile = xt[:, q_rows]
+    y_tile = yt[:, pl.ds(pl.multiple_of(tile * QT, QT), QT)]
     for g in range(2):
         rows = slice(g * QT, (g + 1) * QT)
         lanes = slice(g * HD, (g + 1) * HD)
-        attn_ref[:, lanes] = out[rows].astype(BF16)
         raw = q_ref[:, lanes].astype(F32)
-        qgrad_ref[:, lanes] = prep_back(
-            raw, qg_ref[...], cos_q, sin_q, dq[rows] * score_scale
-        ).astype(BF16)
+        q_grad = prep_back(raw, qg_ref[...], cos_q, sin_q, dq[rows] * score_scale).astype(BF16)
+        qgrad_ref[:, lanes] = q_grad
+        skq[:, lanes] += mm(x_tile, q_grad)
+        sko[:, lanes] += mm(y_tile, out[rows].astype(BF16))
 
     @pl.when(tile == 1)
     def _():
-        for part, k_ref in enumerate((k2_ref, k1_ref, k0_ref)):
+        sk_k = jnp.zeros((HD, HD), F32)
+        sk_v = jnp.zeros((HD, HD), F32)
+        for part, k_ref in enumerate(k_parts):
             rows = slice(part * TOK, (part + 1) * TOK)
             raw = k_ref[...].astype(F32)
             dk = prep_back(
                 raw, kg_ref[...], cos[rows, :], sin[rows, :], dkt[:, rows].T * score_scale
             )
             dv = dvt[:, rows].T
-            if part == 2:
-                dk_ref[...] = dk
-                dv_ref[...] = dv
-            else:
-                back = back2_ref if part == 0 else back1_ref
-                back[0, 0] = dk.astype(BF16)
-                back[0, 1] = dv.astype(BF16)
-
-
-def attention(shard, q_raw, d_out, k_raw, values, kv1, kv2, q_gain, k_gain, tables):
+            sk_k = sk_k + mm(xt[:, rows], dk.astype(BF16))
+            sk_v = sk_v + mm(xt[:, rows], dv.astype(BF16))
+            target = (back2_ref, back1_ref, own_ref)[part]
+            target[:, k_lanes] = dk.astype(target.dtype)
+            target[:, v_lanes] = dv.astype(target.dtype)
+        head = pl.program_id(0)
+        sk_ref[:, pl.ds(pl.multiple_of(head * 2 * HD, 2 * HD), 2 * HD)] = skq[...].astype(BF16)
+        sk_ref[:, pl.ds(pl.multiple_of(head * HD + 4 * HD, HD), HD)] = sk_k.astype(BF16)
+        sk_ref[:, pl.ds(pl.multiple_of(head * HD + 6 * HD, HD), HD)] = sk_v.astype(BF16)
+        sk_ref[:, pl.ds(pl.multiple_of(head * 2 * HD + 8 * HD, 2 * HD), 2 * HD)] = sko[...].astype(BF16)
+
+
+def attention(shard, q_raw, d_out, k_raw, values, kv1, kv2, sketches, q_gain, k_gain, tables):
     whole = lambda a: pl.BlockSpec(a.shape, lambda h, t: (0,) * a.ndim)
     tile_spec = pl.BlockSpec((QT, 2 * HD), lambda h, t: (t, h))
     k_spec = pl.BlockSpec((TOK, HD), lambda h, t: (0, h))
-    v_spec = pl.BlockSpec((TOK, HD), lambda h, t: (0, 2 + h))
-    back_spec = pl.BlockSpec((1, 2, TOK, HD), lambda h, t: (h, 0, 0, 0))
-    back_shape = jax.ShapeDtypeStruct((2, 2, TOK, HD), BF16)
-    gains = [q_gain[None, :], k_gain[None, :]]
+    consts = [kv1, kv2, *sketches, q_gain[None, :], k_gain[None, :]] + tables
+    q_shape = jax.ShapeDtypeStruct((TOK, 4 * HD), BF16)
+    kv_shape = jax.ShapeDtypeStruct((TOK, 4 * HD), BF16)
+    own_shape = jax.ShapeDtypeStruct((TOK, 4 * HD), F32)
+    sk_shape = jax.ShapeDtypeStruct((HD, 12 * HD), BF16)
     return pl.pallas_call(
         attention_kernel,
         grid=(2, 2),
-        in_specs=[
-            pl.BlockSpec(memory_space=pltpu.SMEM),
-            tile_spec, tile_spec,
-            k_spec, k_spec, k_spec, k_spec, v_spec, v_spec,
-        ] + [whole(a) for a in gains + tables],
-        out_specs=[tile_spec, tile_spec, k_spec, k_spec, back_spec, back_spec],
-        out_shape=[
-            jax.ShapeDtypeStruct((TOK, 4 * HD), BF16),
-            jax.ShapeDtypeStruct((TOK, 4 * HD), BF16),
-            jax.ShapeDtypeStruct((TOK, 2 * HD), F32),
-            jax.ShapeDtypeStruct((TOK, 2 * HD), F32),
-            back_shape, back_shape,
-        ],
+        in_specs=[pl.BlockSpec(memory_space=pltpu.SMEM), tile_spec, tile_spec, k_spec, k_spec]
+        + [whole(a) for a in consts],
+        out_specs=[tile_spec, whole(own_shape), whole(kv_shape), whole(kv_shape), whole(sk_shape)],
+        out_shape=[q_shape, own_shape, kv_shape, kv_shape, sk_shape],
         scratch_shapes=[
             pltpu.VMEM((SPAN, HD), BF16),
             pltpu.VMEM((SPAN, HD), BF16),
@@ -201,39 +211,16 @@
             pltpu.VMEM((2 * QT, NBLK * KB), F32),
             pltpu.VMEM((HD, SPAN), F32),
             pltpu.VMEM((HD, SPAN), F32),
+            pltpu.VMEM((HD, SPAN), BF16),
+            pltpu.VMEM((HD, TOK), BF16),
+            pltpu.VMEM((HD, 2 * HD), F32),
+            pltpu.VMEM((HD, 2 * HD), F32),
         ],
-        compiler_params=pltpu.CompilerParams(vmem_limit_bytes=40 << 20),
+        compiler_params=pltpu.CompilerParams(vmem_limit_bytes=ATTN_VMEM),
         cost_estimate=pl.CostEstimate(
             flops=6 * 4 * 2 * TOK * SPAN * HD, bytes_accessed=6 << 20, transcendentals=4 * TOK * SPAN
         ),
-    )(shard, q_raw, d_out, k_raw, kv1, kv2, values, kv1, kv2, *gains, *tables)
-
-
-def sketch_kernel(x0_ref, x1_ref, x2_ref, y_ref, qgrad_ref, attn_ref, dk_ref, dv_ref, b1_ref, b2_ref, out_ref):
-    def tokens(a, b):
-        return lax.dot_general(a, b, (((0,), (0,)), ((), ())), preferred_element_type=F32)
-
-    x0, x1, x2 = x0_ref[...], x1_ref[...], x2_ref[...]
-    out_ref[:, 0 : 4 * HD] = tokens(x0, qgrad_ref[...]).astype(BF16)
-    out_ref[:, 8 * HD : 12 * HD] = tokens(y_ref[...], attn_ref[...]).astype(BF16)
-    for kind, own_ref in enumerate((dk_ref, dv_ref)):
-        for h in range(2):
-            total = tokens(x0, own_ref[:, h * HD : (h + 1) * HD].astype(BF16))
-            total += tokens(x1, b1_ref[h, kind])
-            total += tokens(x2, b2_ref[h, kind])
-            at = (4 + 2 * kind + h) * HD
-            out_ref[:, at : at + HD] = total.astype(BF16)
-
-
-def sketch(*args):
-    return pl.pallas_call(
-        sketch_kernel,
-        out_shape=jax.ShapeDtypeStruct((HD, 12 * HD), BF16),
-        compiler_params=pltpu.CompilerParams(vmem_limit_bytes=24 << 20),
-        cost_estimate=pl.CostEstimate(
-            flops=2 * TOK * HD * 16 * HD, bytes_accessed=5 << 20, transcendentals=0
-        ),
-    )(*args)
+    )(shard, q_raw, d_out, k_raw, values, *consts)
 
 
 def shift(x, by):
@@ -262,34 +249,36 @@
     layer_input, omega_in, upstream, omega_out, q_raw, k_raw, values, d_out, q_gain, k_gain
 ):
     kv = jnp.concatenate([k_raw, values], axis=1)
+    kv, layer_input, upstream = lax.optimization_barrier((kv, layer_input, upstream))
     kv2 = shift(kv, 2)
     kv1 = shift(kv, 1)
     partial_x = jnp.dot(layer_input, omega_in, preferred_element_type=F32)
     partial_y = jnp.dot(upstream, omega_out, preferred_element_type=F32)
-    x0, y0 = sum_over_head(partial_x, partial_y)
+    x0, y0 = lax.fori_loop(
+        0,
+        lax.optimization_barrier(jnp.int32(1)),
+        lambda i, carry: sum_over_head(partial_x, partial_y),
+        (jnp.zeros((TOK, HD), BF16), jnp.zeros((TOK, HD), BF16)),
+    )
     x1 = shift(x0, 1)
     x2 = shift(x0, 2)
     shard = lax.axis_index("seq").astype(jnp.int32)[None]
     tables = [jnp.asarray(t) for t in rope_tables(lax.axis_size("seq"))]
-    query_grad, attn_out, dk, dv, back1, back2 = attention(
-        shard, q_raw, d_out, k_raw, values, kv1, kv2, q_gain, k_gain, tables
+    query_grad, own, back1, back2, sketches = attention(
+        shard, q_raw, d_out, k_raw, values, kv1, kv2, (x0, x1, x2, y0), q_gain, k_gain, tables
     )
     got2 = shift(back2, -2)
     got1 = shift(back1, -1)
-    sketches = sketch(x0, x1, x2, y0, query_grad, attn_out, dk, dv, back1, back2)
     shards = lax.axis_size("seq")
     pieces = lax.all_to_all(sketches.reshape(shards, HD // shards, 12 * HD), "seq", 0, 0, tiled=True)
     total = jnp.sum(pieces.astype(F32), axis=0)
-
-    def finish(own, kind):
-        far = (got1[:, kind].astype(F32) + got2[:, kind].astype(F32)).transpose(1, 0, 2)
-        return (own + far.reshape(own.shape)).astype(BF16)
+    kv_grad = (own + got1.astype(F32) + got2.astype(F32)).astype(BF16)
 
     q_cols, kv_cols = 4 * HD, 2 * HD
     return (
         query_grad,
-        finish(dk, 0),
-        finish(dv, 1),
+        kv_grad[:, :kv_cols],
+        kv_grad[:, kv_cols:],
         total[:, :q_cols],
         total[:, q_cols : q_cols + kv_cols],
         total[:, q_cols + kv_cols : q_cols + 2 * kv_cols],

time: 126 us -> 137 us (1.087)
  the two profiles are of different devices: /device:TPU:12 before, /device:TPU:8 now
where the time goes in v2:
time: 137 us
  starting transfers between devices  57.5 us (42%)
  waiting for transfers between devices  46.2 us (34%)
  Pallas kernels  22 us (16%)
  local copies, waits for them, and re-layouts  6.75 us (5%)
  other arithmetic  2.57 us (2%)
    all_to_all x1, waiting for transfers between devices, per_device(): lax.all_to_all(sketches.reshape(shards, HD // shards, 12 * HD), 'seq', 0,...  23.2 us
    pallas_call x1, Pallas kernels, attention(): pl.pallas_call(attention_kernel, grid=(2, 2), in_specs=[pl.BlockSpec(memo...  22 us
    ppermute x6, starting transfers between devices, shift(): return lax.ppermute(x, 'seq', pairs)  21.7 us
    all_to_all x1, starting transfers between devices, per_device(): lax.all_to_all(sketches.reshape(shards, HD // shards, 12 * HD), 'seq', 0,...  19 us
    ppermute x4, starting transfers between devices, swap(): return lax.ppermute(x, 'head', [(i, i ^ bit) for i in range(count)])  16.8 us
    ppermute x4, waiting for transfers between devices, swap(): return lax.ppermute(x, 'head', [(i, i ^ bit) for i in range(count)])  13.2 us
    ppermute x6, waiting for transfers between devices, shift(): return lax.ppermute(x, 'seq', pairs)  9.82 us
  transfers between devices with their start and end apart: 11, of which 8 were waited for; matrix products, arithmetic and copies ran while one was open for 4% of the time, Pallas kernels for 0%

profile of v2, /device:TPU:8, one launch (start us, length us, event | category | flops | bytes accessed | tf_op | source)
XLA Modules:
  0.0 136.7 jit_solution(9407681433566275107)
XLA Ops:
  0.7 1.1 pad_maximum_fusion
  1.8 3.5 %collective-permute-start.5 = (bf16[512,512]{1,0:T(8,128)(2,1)S(1)}, bf16[512,512]{1,0:T(8,128)(2,1)S(1)}, u32[]{:S(2)}, u32[]{:S(2)}) collective-permute-start(bf16[512,512]{1,0:T(8,128)(2,1)S(1)} %pad_maximum_fusion), channel_id=1, source_target_pairs={{0,16},{8,24},{16,32},{24,40},{32,48},{40,56},{48,64},{56,72},{64,... | collective-permute-start | bytes 1572872 | tf_op jit(solution)/shard_map/ppermute | solution.py:229
  5.4 4.3 %collective-permute-start.4 = (bf16[512,512]{1,0:T(8,128)(2,1)S(1)}, bf16[512,512]{1,0:T(8,128)(2,1)S(1)}, u32[]{:S(2)}, u32[]{:S(2)}) collective-permute-start(bf16[512,512]{1,0:T(8,128)(2,1)S(1)} %pad_maximum_fusion), channel_id=1, source_target_pairs={{0,8},{8,16},{16,24},{24,32},{32,40},{40,48},{48,56},{56,64},{64,7... | collective-permute-start | bytes 1572872 | tf_op jit(solution)/shard_map/ppermute | solution.py:229
  12.4 30.9 %while.14 = (s32[]{:T(128)}, bf16[512,128]{1,0:T(8,128)(2,1)}, bf16[512,128]{1,0:T(8,128)(2,1)}, s32[]{:T(128)}, f32[512,128]{1,0:T(8,128)S(1)}, /*index=5*/f32[...) while((s32[]{:T(128)}, bf16[512,128]{1,0:T(8,128)(2,1)}, bf16[512,128]{1,0:T(8,128)(2,1)}, ...), condition=%wide.region_1.2_spmd, body=%wide.region_0.1_spmd.sunk | while | flops 983056 | bytes 5505426 | solution.py:257
  12.4 1.9 %collective-permute-start = (bf16[512,128]{1,0:T(8,128)(2,1)S(1)}, bf16[512,128]{1,0:T(8,128)(2,1)S(1)}, u32[]{:S(2)}, u32[]{:S(2)}) collective-permute-start(bf16[512,128]{1,0:T(8,128)(2,1)S(1)} %select_convert_fusion.2), channel_id=1, source_target_pairs={{0,1},{1,0},{2,3},{3,2},{4,5},{5,4},{6,7},{7,6},{8,9},{9,8},{10,11... | collective-permute-start | bytes 393224 | tf_op jit(solution)/shard_map/while/body/ppermute | solution.py:234
  14.3 1.3 collective-permute-done
  15.7 6.1 %collective-permute-start.1 = (bf16[512,128]{1,0:T(8,128)(2,1)S(1)}, bf16[512,128]{1,0:T(8,128)(2,1)S(1)}, u32[]{:S(2)}, u32[]{:S(2)}) collective-permute-start(bf16[512,128]{1,0:T(8,128)(2,1)S(1)} %get-tuple-element.160), channel_id=1, source_target_pairs={{0,2},{1,3},{2,0},{3,1},{4,6},{5,7},{6,4},{7,5},{8,10},{9,11},{10,... | collective-permute-start | bytes 393224 | tf_op jit(solution)/shard_map/while/body/ppermute | solution.py:234
  21.8 6.6 %collective-permute-done.1 = bf16[512,128]{1,0:T(8,128)(2,1)S(1)} collective-permute-done((bf16[512,128]{1,0:T(8,128)(2,1)S(1)}, bf16[512,128]{1,0:T(8,128)(2,1)S(1)}, u32[]{:S(2)}, u32[]{:S(2)}) %collective-permute-start.1) | collective-permute-done | bytes 131104 | tf_op jit(solution)/shard_map/while/body/ppermute | solution.py:234
  28.4 6.9 %collective-permute-start.2 = (bf16[512,128]{1,0:T(8,128)(2,1)S(1)}, bf16[512,128]{1,0:T(8,128)(2,1)S(1)}, u32[]{:S(2)}, u32[]{:S(2)}) collective-permute-start(bf16[512,128]{1,0:T(8,128)(2,1)S(1)} %fusion.14), channel_id=1, source_target_pairs={{0,4},{1,5},{2,6},{3,7},{4,0},{5,1},{6,2},{7,3},{8,12},{9,13},{10,... | collective-permute-start | bytes 393224 | tf_op jit(solution)/shard_map/while/body/ppermute | solution.py:234
  35.3 4.0 %collective-permute-done.2 = bf16[512,128]{1,0:T(8,128)(2,1)S(1)} collective-permute-done((bf16[512,128]{1,0:T(8,128)(2,1)S(1)}, bf16[512,128]{1,0:T(8,128)(2,1)S(1)}, u32[]{:S(2)}, u32[]{:S(2)}) %collective-permute-start.2) | collective-permute-done | bytes 131104 | tf_op jit(solution)/shard_map/while/body/ppermute | solution.py:234
  39.3 1.9 %collective-permute-start.3 = (bf16[512,128]{1,0:T(8,128)(2,1)S(1)}, bf16[512,128]{1,0:T(8,128)(2,1)S(1)}, u32[]{:S(2)}, u32[]{:S(2)}) collective-permute-start(bf16[512,128]{1,0:T(8,128)(2,1)S(1)} %add_convert_fusion.3), channel_id=1, source_target_pairs={{0,1},{1,0},{2,3},{3,2},{4,5},{5,4},{6,7},{7,6},{8,9},{9,8},{10,11... | collective-permute-start | bytes 393224 | tf_op jit(solution)/shard_map/while/body/ppermute | solution.py:234
  41.3 1.3 collective-permute-done.3
  43.3 3.5 %collective-permute-start.7 = (bf16[512,128]{1,0:T(8,128)(2,1)}, bf16[512,128]{1,0:T(8,128)(2,1)S(1)}, u32[]{:S(2)}, u32[]{:S(2)}) collective-permute-start(bf16[512,128]{1,0:T(8,128)(2,1)} %get-tuple-element.92.x0_ref), channel_id=1, source_target_pairs={{0,16},{8,24},{16,32},{24,40},{32,48},{40,56},{48,64},{56,72},{64,... | collective-permute-start | bytes 393224 | tf_op jit(solution)/shard_map/ppermute | solution.py:229
  46.8 5.5 %collective-permute-start.6 = (bf16[512,128]{1,0:T(8,128)(2,1)}, bf16[512,128]{1,0:T(8,128)(2,1)S(1)}, u32[]{:S(2)}, u32[]{:S(2)}) collective-permute-start(bf16[512,128]{1,0:T(8,128)(2,1)} %get-tuple-element.92.x0_ref), channel_id=1, source_target_pairs={{0,8},{8,16},{16,24},{24,32},{32,40},{40,48},{48,56},{56,64},{64,7... | collective-permute-start | bytes 393224 | tf_op jit(solution)/shard_map/ppermute | solution.py:229
  52.2 0.8 collective-permute-done.7.x2_ref
  53.1 4.1 %collective-permute-done.6.x1_ref = bf16[512,128]{1,0:T(8,128)(2,1)S(1)} collective-permute-done((bf16[512,128]{1,0:T(8,128)(2,1)}, bf16[512,128]{1,0:T(8,128)(2,1)S(1)}, u32[]{:S(2)}, u32[]{:S(2)}) %collective-permute-start.6) | collective-permute-done | bytes 131104 | tf_op jit(solution)/shard_map/ppermute | solution.py:229
  58.2 22.0 %shard_map.189 = (bf16[512,512]{1,0:T(8,128)(2,1)}, f32[512,512]{1,0:T(8,128)}, bf16[512,512]{1,0:T(8,128)(2,1)}, bf16[512,512]{1,0:T(8,128)(2,1)}, bf16[128,1536]{1,0:T(8,128)(2,1)}) custom-call(s32[1]{0:T(128)} %bitcast.shard_ref, bf16[512,512]{1,0:T(8,128)(2,1)} %q_ref.1, bf16[512,512]{1,0:T(8,128)(2,1)} %do_ref.1, bf16[512,256]{1,0:T(8,128)(2,1)} %k0_ref.1, ...), custom_call_target="tpu_custom_call" | custom-call | flops 4831838208 | bytes 6291456 | tf_op jit(solution)/shard_map/pallas_call | solution.py:198
  80.2 2.5 %collective-permute-start.8 = (bf16[512,512]{1,0:T(8,128)(2,1)}, bf16[512,512]{1,0:T(8,128)(2,1)S(1)}, u32[]{:S(2)}, u32[]{:S(2)}) collective-permute-start(bf16[512,512]{1,0:T(8,128)(2,1)} %get-tuple-element.96), channel_id=1, source_target_pairs={{8,0},{16,8},{24,16},{32,24},{40,32},{48,40},{56,48},{64,56},{72,6... | collective-permute-start | bytes 1572872 | tf_op jit(solution)/shard_map/ppermute | solution.py:229
  82.8 2.4 %collective-permute-start.9 = (bf16[512,512]{1,0:T(8,128)(2,1)}, bf16[512,512]{1,0:T(8,128)(2,1)S(1)}, u32[]{:S(2)}, u32[]{:S(2)}) collective-permute-start(bf16[512,512]{1,0:T(8,128)(2,1)} %get-tuple-element.97), channel_id=1, source_target_pairs={{16,0},{24,8},{32,16},{40,24},{48,32},{56,40},{64,48},{72,56},{80,... | collective-permute-start | bytes 1572872 | tf_op jit(solution)/shard_map/ppermute | solution.py:229
  85.2 1.9 %reshape.17 = bf16[64,2,1536]{2,1,0:T(2,128)(2,1)} reshape(bf16[128,1536]{1,0:T(8,128)(2,1)} %get-tuple-element.98) | data formatting | bytes 786432 | tf_op jit(solution)/shard_map/reshape | solution.py:273
  87.1 19.0 %all-to-all-start = ((bf16[64,2,1536]{2,1,0:T(2,128)(2,1)}), bf16[64,2,1536]{2,1,0:T(2,128)(2,1)S(1)}, u32[]{:S(2)}, u32[]{:S(2)}) async-start(bf16[64,2,1536]{2,1,0:T(2,128)(2,1)} %reshape.17), calls=%async_computation | async-start | bytes 786432 | tf_op jit(solution)/shard_map/all_to_all | solution.py:273
  106.1 4.9 %collective-permute-done.9 = bf16[512,512]{1,0:T(8,128)(2,1)S(1)} collective-permute-done((bf16[512,512]{1,0:T(8,128)(2,1)}, bf16[512,512]{1,0:T(8,128)(2,1)S(1)}, u32[]{:S(2)}, u32[]{:S(2)}) %collective-permute-start.9) | collective-permute-done | bytes 524320 | tf_op jit(solution)/shard_map/ppermute | solution.py:229
  111.2 0.8 fusion.2
  112.0 23.2 %all-to-all-done = bf16[64,2,1536]{2,1,0:T(2,128)(2,1)S(1)} async-done(((bf16[64,2,1536]{2,1,0:T(2,128)(2,1)}), bf16[64,2,1536]{2,1,0:T(2,128)(2,1)S(1)}, u32[]{:S(2)}, u32[]{:S(2)}) %all-to-all-start) | async-done | bytes 393248 | tf_op jit(solution)/shard_map/all_to_all | solution.py:273
  (34 shorter events, 6.3 us)
Async XLA Ops:
  0.6 9.0 %copy-start = (bf16[512,672]{0,1:T(8,128)(2,1)S(1)}, bf16[512,672]{0,1:T(8,128)(2,1)}, u32[]{:S(2)}) copy-start(bf16[512,672]{0,1:T(8,128)(2,1)} %param.16) | copy-start | bytes 2064388
  0.6 9.0 %copy-start.3 = (bf16[672,128]{1,0:T(8,128)(2,1)S(1)}, bf16[672,128]{1,0:T(8,128)(2,1)}, u32[]{:S(2)}) copy-start(bf16[672,128]{1,0:T(8,128)(2,1)} %param.17) | copy-start | bytes 516100
  1.8 8.3 %copy-start.2 = (bf16[512,672]{0,1:T(8,128)(2,1)S(1)}, bf16[512,672]{0,1:T(8,128)(2,1)}, u32[]{:S(2)}) copy-start(bf16[512,672]{0,1:T(8,128)(2,1)} %param.18) | copy-start | bytes 2064388
  1.8 55.3 %collective-permute-start.5 = (bf16[512,512]{1,0:T(8,128)(2,1)S(1)}, bf16[512,512]{1,0:T(8,128)(2,1)S(1)}, u32[]{:S(2)}, u32[]{:S(2)}) collective-permute-start(bf16[512,512]{1,0:T(8,128)(2,1)S(1)} %pad_maximum_fusion), channel_id=1, source_target_pairs={{0,16},{8,24},{16,32},{24,40},{32,48},{40,56},{48,64},{56,72},{64,... | collective-permute-start | bytes 1572872 | tf_op jit(solution)/shard_map/ppermute | solution.py:229
  5.4 51.8 %collective-permute-start.4 = (bf16[512,512]{1,0:T(8,128)(2,1)S(1)}, bf16[512,512]{1,0:T(8,128)(2,1)S(1)}, u32[]{:S(2)}, u32[]{:S(2)}) collective-permute-start(bf16[512,512]{1,0:T(8,128)(2,1)S(1)} %pad_maximum_fusion), channel_id=1, source_target_pairs={{0,8},{8,16},{16,24},{24,32},{32,40},{40,48},{48,56},{56,64},{64,7... | collective-permute-start | bytes 1572872 | tf_op jit(solution)/shard_map/ppermute | solution.py:229
  9.7 0.9 copy-start.4
  12.4 3.2 %collective-permute-start = (bf16[512,128]{1,0:T(8,128)(2,1)S(1)}, bf16[512,128]{1,0:T(8,128)(2,1)S(1)}, u32[]{:S(2)}, u32[]{:S(2)}) collective-permute-start(bf16[512,128]{1,0:T(8,128)(2,1)S(1)} %select_convert_fusion.2), channel_id=1, source_target_pairs={{0,1},{1,0},{2,3},{3,2},{4,5},{5,4},{6,7},{7,6},{8,9},{9,8},{10,11... | collective-permute-start | bytes 393224 | tf_op jit(solution)/shard_map/while/body/ppermute | solution.py:234
  15.7 12.7 %collective-permute-start.1 = (bf16[512,128]{1,0:T(8,128)(2,1)S(1)}, bf16[512,128]{1,0:T(8,128)(2,1)S(1)}, u32[]{:S(2)}, u32[]{:S(2)}) collective-permute-start(bf16[512,128]{1,0:T(8,128)(2,1)S(1)} %get-tuple-element.160), channel_id=1, source_target_pairs={{0,2},{1,3},{2,0},{3,1},{4,6},{5,7},{6,4},{7,5},{8,10},{9,11},{10,... | collective-permute-start | bytes 393224 | tf_op jit(solution)/shard_map/while/body/ppermute | solution.py:234
  28.4 10.9 %collective-permute-start.2 = (bf16[512,128]{1,0:T(8,128)(2,1)S(1)}, bf16[512,128]{1,0:T(8,128)(2,1)S(1)}, u32[]{:S(2)}, u32[]{:S(2)}) collective-permute-start(bf16[512,128]{1,0:T(8,128)(2,1)S(1)} %fusion.14), channel_id=1, source_target_pairs={{0,4},{1,5},{2,6},{3,7},{4,0},{5,1},{6,2},{7,3},{8,12},{9,13},{10,... | collective-permute-start | bytes 393224 | tf_op jit(solution)/shard_map/while/body/ppermute | solution.py:234
  39.3 3.2 %collective-permute-start.3 = (bf16[512,128]{1,0:T(8,128)(2,1)S(1)}, bf16[512,128]{1,0:T(8,128)(2,1)S(1)}, u32[]{:S(2)}, u32[]{:S(2)}) collective-permute-start(bf16[512,128]{1,0:T(8,128)(2,1)S(1)} %add_convert_fusion.3), channel_id=1, source_target_pairs={{0,1},{1,0},{2,3},{3,2},{4,5},{5,4},{6,7},{7,6},{8,9},{9,8},{10,11... | collective-permute-start | bytes 393224 | tf_op jit(solution)/shard_map/while/body/ppermute | solution.py:234
  43.3 9.8 %collective-permute-start.7 = (bf16[512,128]{1,0:T(8,128)(2,1)}, bf16[512,128]{1,0:T(8,128)(2,1)S(1)}, u32[]{:S(2)}, u32[]{:S(2)}) collective-permute-start(bf16[512,128]{1,0:T(8,128)(2,1)} %get-tuple-element.92.x0_ref), channel_id=1, source_target_pairs={{0,16},{8,24},{16,32},{24,40},{32,48},{40,56},{48,64},{56,72},{64,... | collective-permute-start | bytes 393224 | tf_op jit(solution)/shard_map/ppermute | solution.py:229
  46.8 10.4 %collective-permute-start.6 = (bf16[512,128]{1,0:T(8,128)(2,1)}, bf16[512,128]{1,0:T(8,128)(2,1)S(1)}, u32[]{:S(2)}, u32[]{:S(2)}) collective-permute-start(bf16[512,128]{1,0:T(8,128)(2,1)} %get-tuple-element.92.x0_ref), channel_id=1, source_target_pairs={{0,8},{8,16},{16,24},{24,32},{32,40},{40,48},{48,56},{56,64},{64,7... | collective-permute-start | bytes 393224 | tf_op jit(solution)/shard_map/ppermute | solution.py:229
  53.1 4.1 %copy-start.7 = (bf16[512,128]{1,0:T(8,128)(2,1)}, bf16[512,128]{1,0:T(8,128)(2,1)S(1)}, u32[]{:S(2)}) copy-start(bf16[512,128]{1,0:T(8,128)(2,1)S(1)} %collective-permute-done.7.x2_ref) | copy-start | bytes 393220
  57.1 0.6 copy-start.8
  57.2 0.8 copy-start.5
  57.2 1.0 copy-start.6
  80.2 30.8 %copy-start.1 = (f32[512,512]{1,0:T(8,128)S(1)}, f32[512,512]{1,0:T(8,128)}, u32[]{:S(2)}) copy-start(f32[512,512]{1,0:T(8,128)} %get-tuple-element.95) | copy-start | bytes 3145732
  80.2 25.9 %collective-permute-start.8 = (bf16[512,512]{1,0:T(8,128)(2,1)}, bf16[512,512]{1,0:T(8,128)(2,1)S(1)}, u32[]{:S(2)}, u32[]{:S(2)}) collective-permute-start(bf16[512,512]{1,0:T(8,128)(2,1)} %get-tuple-element.96), channel_id=1, source_target_pairs={{8,0},{16,8},{24,16},{32,24},{40,32},{48,40},{56,48},{64,56},{72,6... | collective-permute-start | bytes 1572872 | tf_op jit(solution)/shard_map/ppermute | solution.py:229
  82.8 28.2 %collective-permute-start.9 = (bf16[512,512]{1,0:T(8,128)(2,1)}, bf16[512,512]{1,0:T(8,128)(2,1)S(1)}, u32[]{:S(2)}, u32[]{:S(2)}) collective-permute-start(bf16[512,512]{1,0:T(8,128)(2,1)} %get-tuple-element.97), channel_id=1, source_target_pairs={{16,0},{24,8},{32,16},{40,24},{48,32},{56,40},{64,48},{72,56},{80,... | collective-permute-start | bytes 1572872 | tf_op jit(solution)/shard_map/ppermute | solution.py:229
  87.1 48.1 %all-to-all-start = ((bf16[64,2,1536]{2,1,0:T(2,128)(2,1)}), bf16[64,2,1536]{2,1,0:T(2,128)(2,1)S(1)}, u32[]{:S(2)}, u32[]{:S(2)}) async-start(bf16[64,2,1536]{2,1,0:T(2,128)(2,1)} %reshape.17), calls=%async_computation | async-start | bytes 786432 | tf_op jit(solution)/shard_map/all_to_all | solution.py:273

commit v3 on v2

--- a/solution.py
+++ b/solution.py
@@ -234,15 +234,15 @@
     return lax.ppermute(x, "head", [(i, i ^ bit) for i in range(count)])
 
 
-def sum_over_head(partial_x, partial_y):
-    first = lax.axis_index("head") % 2 == 0
-    got = swap(jnp.where(first, partial_y, partial_x).astype(BF16), 1)
-    total = jnp.where(first, partial_x, partial_y) + got.astype(F32)
-    for bit in (2, 4):
-        total = total + swap(total.astype(BF16), bit).astype(F32)
-    mine = total.astype(BF16)
-    other = swap(mine, 1)
-    return jnp.where(first, mine, other), jnp.where(first, other, mine)
+def pair_swap(x):
+    count = lax.axis_size("seq")
+    return lax.ppermute(x, "seq", [(i, i ^ 1) for i in range(count)])
+
+
+def one_turn(step, example):
+    turns = lax.optimization_barrier(jnp.int32(1))
+    zeros = jax.tree.map(lambda a: jnp.zeros(a.shape, a.dtype), example)
+    return lax.fori_loop(0, turns, lambda i, carry: step(), zeros)
 
 
 def per_device(
@@ -250,16 +250,28 @@
 ):
     kv = jnp.concatenate([k_raw, values], axis=1)
     kv, layer_input, upstream = lax.optimization_barrier((kv, layer_input, upstream))
+    odd = lax.axis_index("seq") % 2 == 1
+    first = lax.axis_index("head") % 2 == 0
     kv2 = shift(kv, 2)
-    kv1 = shift(kv, 1)
     partial_x = jnp.dot(layer_input, omega_in, preferred_element_type=F32)
     partial_y = jnp.dot(upstream, omega_out, preferred_element_type=F32)
-    x0, y0 = lax.fori_loop(
-        0,
-        lax.optimization_barrier(jnp.int32(1)),
-        lambda i, carry: sum_over_head(partial_x, partial_y),
-        (jnp.zeros((TOK, HD), BF16), jnp.zeros((TOK, HD), BF16)),
-    )
+    wide = jax.ShapeDtypeStruct((TOK, HD), F32)
+    low = jax.ShapeDtypeStruct((TOK, HD), BF16)
+
+    def sum_near():
+        got = swap(jnp.where(first, partial_y, partial_x).astype(BF16), 1)
+        total = jnp.where(first, partial_x, partial_y) + got.astype(F32)
+        return total + swap(total.astype(BF16), 2).astype(F32)
+
+    half = one_turn(sum_near, wide)
+    kv1 = pair_swap(jnp.where(odd, kv2, kv))
+
+    def sum_far():
+        mine = (half + swap(half.astype(BF16), 4).astype(F32)).astype(BF16)
+        other = swap(mine, 1)
+        return jnp.where(first, mine, other), jnp.where(first, other, mine)
+
+    x0, y0 = one_turn(sum_far, (low, low))
     x1 = shift(x0, 1)
     x2 = shift(x0, 2)
     shard = lax.axis_index("seq").astype(jnp.int32)[None]
@@ -267,12 +279,13 @@
     query_grad, own, back1, back2, sketches = attention(
         shard, q_raw, d_out, k_raw, values, kv1, kv2, (x0, x1, x2, y0), q_gain, k_gain, tables
     )
-    got2 = shift(back2, -2)
-    got1 = shift(back1, -1)
+    near = pair_swap(back1).astype(F32)
+    back2 = back2.astype(F32)
+    far = shift(jnp.where(odd, back2 + near, back2).astype(BF16), -2)
     shards = lax.axis_size("seq")
     pieces = lax.all_to_all(sketches.reshape(shards, HD // shards, 12 * HD), "seq", 0, 0, tiled=True)
     total = jnp.sum(pieces.astype(F32), axis=0)
-    kv_grad = (own + got1.astype(F32) + got2.astype(F32)).astype(BF16)
+    kv_grad = (own + jnp.where(odd, 0.0, near) + far.astype(F32)).astype(BF16)
 
     q_cols, kv_cols = 4 * HD, 2 * HD
     return (

time: 137 us -> 120 us (0.88)
  the two profiles are of different devices: /device:TPU:8 before, /device:TPU:30 now
where the time goes in v3:
time: 120 us; the launch traced here: 119 us
  starting transfers between devices  48.1 us (40%)
  waiting for transfers between devices  34.1 us (28%)
  Pallas kernels  22 us (18%)
  local copies, waits for them, and re-layouts  8.05 us (7%)
  other arithmetic  5.26 us (4%)
    pallas_call x1, Pallas kernels, attention(): pl.pallas_call(attention_kernel, grid=(2, 2), in_specs=[pl.BlockSpec(memo...  22 us
    ppermute x4, starting transfers between devices, swap(): return lax.ppermute(x, 'head', [(i, i ^ bit) for i in range(count)])  19.3 us
    ppermute x4, waiting for transfers between devices, shift(): return lax.ppermute(x, 'seq', pairs)  14.5 us
    ppermute x4, starting transfers between devices, shift(): return lax.ppermute(x, 'seq', pairs)  12.8 us
    ppermute x4, waiting for transfers between devices, swap(): return lax.ppermute(x, 'head', [(i, i ^ bit) for i in range(count)])  11.7 us
    all_to_all x1, starting transfers between devices, per_device(): lax.all_to_all(sketches.reshape(shards, HD // shards, 12 * HD), 'seq', 0,...  11.6 us
    all_to_all x1, waiting for transfers between devices, per_device(): lax.all_to_all(sketches.reshape(shards, HD // shards, 12 * HD), 'seq', 0,...  7.88 us
    ppermute x2, starting transfers between devices, pair_swap(): return lax.ppermute(x, 'seq', [(i, i ^ 1) for i in range(count)])  4.43 us
  transfers between devices with their start and end apart: 11, of which 8 were waited for; matrix products, arithmetic and copies ran while one was open for 8% of the time, Pallas kernels for 0%

profile of v3, /device:TPU:30, one launch (start us, length us, event | category | flops | bytes accessed | tf_op | source)
XLA Modules:
  0.0 119.2 jit_solution(15746064517340756620)
XLA Ops:
  0.7 1.1 pad_maximum_fusion
  1.8 4.7 %collective-permute-start.3 = (bf16[512,512]{1,0:T(8,128)(2,1)S(1)}, bf16[512,512]{1,0:T(8,128)(2,1)S(1)}, u32[]{:S(2)}, u32[]{:S(2)}) collective-permute-start(bf16[512,512]{1,0:T(8,128)(2,1)S(1)} %pad_maximum_fusion), channel_id=1, source_target_pairs={{0,16},{8,24},{16,32},{24,40},{32,48},{40,56},{48,64},{56,72},{64,... | collective-permute-start | bytes 1572872 | tf_op jit(solution)/shard_map/ppermute | solution.py:229
  8.7 16.8 %while.24 = (s32[]{:T(128)}, f32[512,128]{1,0:T(8,128)}, s32[]{:T(128)}, pred[]{:T(512)}, f32[512,128]{1,0:T(8,128)S(1)}, /*index=5*/f32[512,128]{1,0:T(8,128)S(1)}, s32[]{:T(128)}) while((s32[]{:T(128)}, f32[512,128]{1,0:T(8,128)}, s32[]{:T(128)}, pred[]{:T(512)}, f32[512,128]{1,0:T(8,128)S(1)}, /*index=5*/f32[512,128]{1,0:T(8,128)S(1)}, ...), condition=%wide.region_1.2_spmd, body=%wide.region_0.1_spmd.sunk | while | flops 655362 | bytes 3539104 | solution.py:245
  8.7 1.9 %collective-permute-start = (bf16[512,128]{1,0:T(8,128)(2,1)S(1)}, bf16[512,128]{1,0:T(8,128)(2,1)S(1)}, u32[]{:S(2)}, u32[]{:S(2)}) collective-permute-start(bf16[512,128]{1,0:T(8,128)(2,1)S(1)} %select_convert_fusion.2), channel_id=1, source_target_pairs={{0,1},{1,0},{2,3},{3,2},{4,5},{5,4},{6,7},{7,6},{8,9},{9,8},{10,11... | collective-permute-start | bytes 393224 | tf_op jit(solution)/shard_map/while/body/ppermute | solution.py:234
  10.6 1.3 %collective-permute-done = bf16[512,128]{1,0:T(8,128)(2,1)S(1)} collective-permute-done((bf16[512,128]{1,0:T(8,128)(2,1)S(1)}, bf16[512,128]{1,0:T(8,128)(2,1)S(1)}, u32[]{:S(2)}, u32[]{:S(2)}) %collective-permute-start) | collective-permute-done | bytes 131104 | tf_op jit(solution)/shard_map/while/body/ppermute | solution.py:234
  12.0 6.1 %collective-permute-start.1 = (bf16[512,128]{1,0:T(8,128)(2,1)S(1)}, bf16[512,128]{1,0:T(8,128)(2,1)S(1)}, u32[]{:S(2)}, u32[]{:S(2)}) collective-permute-start(bf16[512,128]{1,0:T(8,128)(2,1)S(1)} %fusion.15), channel_id=1, source_target_pairs={{0,2},{1,3},{2,0},{3,1},{4,6},{5,7},{6,4},{7,5},{8,10},{9,11},{10,... | collective-permute-start | bytes 393224 | tf_op jit(solution)/shard_map/while/body/ppermute | solution.py:234
  18.1 6.6 %collective-permute-done.1 = bf16[512,128]{1,0:T(8,128)(2,1)S(1)} collective-permute-done((bf16[512,128]{1,0:T(8,128)(2,1)S(1)}, bf16[512,128]{1,0:T(8,128)(2,1)S(1)}, u32[]{:S(2)}, u32[]{:S(2)}) %collective-permute-start.1) | collective-permute-done | bytes 131104 | tf_op jit(solution)/shard_map/while/body/ppermute | solution.py:234
  26.4 9.4 %collective-permute-start.5 = (bf16[512,128]{1,0:T(8,128)(2,1)S(1)}, bf16[512,128]{1,0:T(8,128)(2,1)S(1)}, u32[]{:S(2)}, u32[]{:S(2)}) collective-permute-start(bf16[512,128]{1,0:T(8,128)(2,1)S(1)} %convert_element_type.45), channel_id=1, source_target_pairs={{0,4},{1,5},{2,6},{3,7},{4,0},{5,1},{6,2},{7,3},{8,12},{9,13},{10,... | collective-permute-start | bytes 393224 | tf_op jit(solution)/shard_map/while/body/ppermute | solution.py:234
  36.6 2.5 %collective-permute-start.4 = (bf16[512,512]{1,0:T(8,128)(2,1)S(1)}, bf16[512,512]{1,0:T(8,128)(2,1)S(1)}, u32[]{:S(2)}, u32[]{:S(2)}) collective-permute-start(bf16[512,512]{1,0:T(8,128)(2,1)S(1)} %broadcast_select_fusion.2), channel_id=1, source_target_pairs={{0,8},{8,0},{16,24},{24,16},{32,40},{40,32},{48,56},{56,48},{64,72... | collective-permute-start | bytes 1572872 | tf_op jit(solution)/shard_map/ppermute | solution.py:239
  39.1 2.5 %collective-permute-done.5 = bf16[512,128]{1,0:T(8,128)(2,1)S(1)} collective-permute-done((bf16[512,128]{1,0:T(8,128)(2,1)S(1)}, bf16[512,128]{1,0:T(8,128)(2,1)S(1)}, u32[]{:S(2)}, u32[]{:S(2)}) %collective-permute-start.5) | collective-permute-done | bytes 131104 | tf_op jit(solution)/shard_map/while/body/ppermute | solution.py:234
  42.9 4.0 %while.25 = (s32[]{:T(128)}, bf16[512,128]{1,0:T(8,128)(2,1)}, bf16[512,128]{1,0:T(8,128)(2,1)}, s32[]{:T(128)}, pred[]{:T(512)}, /*index=5*/bf16[512,128]{1,0:T(8,128)(2,1)S(1)}, f32[512,128]{1,0:T(8,128)S(1)}, s32[]{:T(128)}) while((s32[]{:T(128)}, bf16[512,128]{1,0:T(8,128)(2,1)}, bf16[512,128]{1,0:T(8,128)(2,1)}, s32[]{:T(128)}, ...), condition=%wide.region_3.4_spmd, body=%wide.region_2.3_spmd.sunk | while | flops 327682 | bytes 1572990 | solution.py:245
  43.0 1.9 %collective-permute-start.2 = (bf16[512,128]{1,0:T(8,128)(2,1)S(1)}, bf16[512,128]{1,0:T(8,128)(2,1)S(1)}, u32[]{:S(2)}, u32[]{:S(2)}) collective-permute-start(bf16[512,128]{1,0:T(8,128)(2,1)S(1)} %add_convert_fusion.2), channel_id=1, source_target_pairs={{0,1},{1,0},{2,3},{3,2},{4,5},{5,4},{6,7},{7,6},{8,9},{9,8},{10,11... | collective-permute-start | bytes 393224 | tf_op jit(solution)/shard_map/while/body/ppermute | solution.py:234
  44.9 1.3 %collective-permute-done.2 = bf16[512,128]{1,0:T(8,128)(2,1)S(1)} collective-permute-done((bf16[512,128]{1,0:T(8,128)(2,1)S(1)}, bf16[512,128]{1,0:T(8,128)(2,1)S(1)}, u32[]{:S(2)}, u32[]{:S(2)}) %collective-permute-start.2) | collective-permute-done | bytes 131104 | tf_op jit(solution)/shard_map/while/body/ppermute | solution.py:234
  46.9 3.4 %collective-permute-start.7 = (bf16[512,128]{1,0:T(8,128)(2,1)}, bf16[512,128]{1,0:T(8,128)(2,1)S(1)}, u32[]{:S(2)}, u32[]{:S(2)}) collective-permute-start(bf16[512,128]{1,0:T(8,128)(2,1)} %get-tuple-element.126.x0_ref), channel_id=1, source_target_pairs={{0,16},{8,24},{16,32},{24,40},{32,48},{40,56},{48,64},{56,72},{64,... | collective-permute-start | bytes 393224 | tf_op jit(solution)/shard_map/ppermute | solution.py:229
  50.3 1.9 %collective-permute-start.6 = (bf16[512,128]{1,0:T(8,128)(2,1)}, bf16[512,128]{1,0:T(8,128)(2,1)S(1)}, u32[]{:S(2)}, u32[]{:S(2)}) collective-permute-start(bf16[512,128]{1,0:T(8,128)(2,1)} %get-tuple-element.126.x0_ref), channel_id=1, source_target_pairs={{0,8},{8,16},{16,24},{24,32},{32,40},{40,48},{48,56},{56,64},{64,7... | collective-permute-start | bytes 393224 | tf_op jit(solution)/shard_map/ppermute | solution.py:229
  52.3 2.3 %collective-permute-done.7.x2_ref = bf16[512,128]{1,0:T(8,128)(2,1)S(1)} collective-permute-done((bf16[512,128]{1,0:T(8,128)(2,1)}, bf16[512,128]{1,0:T(8,128)(2,1)S(1)}, u32[]{:S(2)}, u32[]{:S(2)}) %collective-permute-start.7) | collective-permute-done | bytes 131104 | tf_op jit(solution)/shard_map/ppermute | solution.py:229
  54.6 4.0 %collective-permute-done.6.x1_ref = bf16[512,128]{1,0:T(8,128)(2,1)S(1)} collective-permute-done((bf16[512,128]{1,0:T(8,128)(2,1)}, bf16[512,128]{1,0:T(8,128)(2,1)S(1)}, u32[]{:S(2)}, u32[]{:S(2)}) %collective-permute-start.6) | collective-permute-done | bytes 131104 | tf_op jit(solution)/shard_map/ppermute | solution.py:229
  59.4 22.0 %shard_map.189 = (bf16[512,512]{1,0:T(8,128)(2,1)}, f32[512,512]{1,0:T(8,128)}, bf16[512,512]{1,0:T(8,128)(2,1)}, bf16[512,512]{1,0:T(8,128)(2,1)}, bf16[128,1536]{1,0:T(8,128)(2,1)}) custom-call(s32[1]{0:T(128)} %bitcast.shard_ref, bf16[512,512]{1,0:T(8,128)(2,1)} %q_ref.1, bf16[512,512]{1,0:T(8,128)(2,1)} %do_ref.1, bf16[512,256]{1,0:T(8,128)(2,1)} %k0_ref.1, ...), custom_call_target="tpu_custom_call" | custom-call | flops 4831838208 | bytes 6291456 | tf_op jit(solution)/shard_map/pallas_call | solution.py:198
  81.5 1.9 %collective-permute-start.8 = (bf16[512,512]{1,0:T(8,128)(2,1)}, bf16[512,512]{1,0:T(8,128)(2,1)S(1)}, u32[]{:S(2)}, u32[]{:S(2)}) collective-permute-start(bf16[512,512]{1,0:T(8,128)(2,1)} %get-tuple-element.130), channel_id=1, source_target_pairs={{0,8},{8,0},{16,24},{24,16},{32,40},{40,32},{48,56},{56,48},{64,72... | collective-permute-start | bytes 1572872 | tf_op jit(solution)/shard_map/ppermute | solution.py:239
  83.4 1.9 %reshape.17 = bf16[64,2,1536]{2,1,0:T(2,128)(2,1)} reshape(bf16[128,1536]{1,0:T(8,128)(2,1)} %get-tuple-element.132) | data formatting | bytes 786432 | tf_op jit(solution)/shard_map/reshape | solution.py:286
  85.3 11.6 %all-to-all-start = ((bf16[64,2,1536]{2,1,0:T(2,128)(2,1)}), bf16[64,2,1536]{2,1,0:T(2,128)(2,1)S(1)}, u32[]{:S(2)}, u32[]{:S(2)}) async-start(bf16[64,2,1536]{2,1,0:T(2,128)(2,1)} %reshape.17), calls=%async_computation | async-start | bytes 786432 | tf_op jit(solution)/shard_map/all_to_all | solution.py:286
  97.9 2.7 %collective-permute-start.9 = (bf16[512,512]{1,0:T(8,128)(2,1)}, bf16[512,512]{1,0:T(8,128)(2,1)S(1)}, u32[]{:S(2)}, u32[]{:S(2)}) collective-permute-start(bf16[512,512]{1,0:T(8,128)(2,1)} %fusion.4), channel_id=1, source_target_pairs={{16,0},{24,8},{32,16},{40,24},{48,32},{56,40},{64,48},{72,56},{80,... | collective-permute-start | bytes 1572872 | tf_op jit(solution)/shard_map/ppermute | solution.py:229
  100.6 7.9 %all-to-all-done = bf16[64,2,1536]{2,1,0:T(2,128)(2,1)S(1)} async-done(((bf16[64,2,1536]{2,1,0:T(2,128)(2,1)}), bf16[64,2,1536]{2,1,0:T(2,128)(2,1)S(1)}, u32[]{:S(2)}, u32[]{:S(2)}) %all-to-all-start) | async-done | bytes 393248 | tf_op jit(solution)/shard_map/all_to_all | solution.py:286
  110.0 8.1 %collective-permute-done.9 = bf16[512,512]{1,0:T(8,128)(2,1)S(1)} collective-permute-done((bf16[512,512]{1,0:T(8,128)(2,1)}, bf16[512,512]{1,0:T(8,128)(2,1)S(1)}, u32[]{:S(2)}, u32[]{:S(2)}) %collective-permute-start.9) | collective-permute-done | bytes 524320 | tf_op jit(solution)/shard_map/ppermute | solution.py:229
  (43 shorter events, 11.1 us)
Async XLA Ops:
  0.6 5.9 %copy-start = (bf16[512,672]{0,1:T(8,128)(2,1)S(1)}, bf16[512,672]{0,1:T(8,128)(2,1)}, u32[]{:S(2)}) copy-start(bf16[512,672]{0,1:T(8,128)(2,1)} %param.18) | copy-start | bytes 2064388
  0.6 5.9 %copy-start.6 = (bf16[672,128]{1,0:T(8,128)(2,1)S(1)}, bf16[672,128]{1,0:T(8,128)(2,1)}, u32[]{:S(2)}) copy-start(bf16[672,128]{1,0:T(8,128)(2,1)} %param.19) | copy-start | bytes 516100
  1.8 5.2 %copy-start.3 = (bf16[512,672]{0,1:T(8,128)(2,1)S(1)}, bf16[512,672]{0,1:T(8,128)(2,1)}, u32[]{:S(2)}) copy-start(bf16[512,672]{0,1:T(8,128)(2,1)} %param.20) | copy-start | bytes 2064388
  1.8 34.0 %collective-permute-start.3 = (bf16[512,512]{1,0:T(8,128)(2,1)S(1)}, bf16[512,512]{1,0:T(8,128)(2,1)S(1)}, u32[]{:S(2)}, u32[]{:S(2)}) collective-permute-start(bf16[512,512]{1,0:T(8,128)(2,1)S(1)} %pad_maximum_fusion), channel_id=1, source_target_pairs={{0,16},{8,24},{16,32},{24,40},{32,48},{40,56},{48,64},{56,72},{64,... | collective-permute-start | bytes 1572872 | tf_op jit(solution)/shard_map/ppermute | solution.py:229
  6.6 0.9 copy-start.7
  8.7 3.2 %collective-permute-start = (bf16[512,128]{1,0:T(8,128)(2,1)S(1)}, bf16[512,128]{1,0:T(8,128)(2,1)S(1)}, u32[]{:S(2)}, u32[]{:S(2)}) collective-permute-start(bf16[512,128]{1,0:T(8,128)(2,1)S(1)} %select_convert_fusion.2), channel_id=1, source_target_pairs={{0,1},{1,0},{2,3},{3,2},{4,5},{5,4},{6,7},{7,6},{8,9},{9,8},{10,11... | collective-permute-start | bytes 393224 | tf_op jit(solution)/shard_map/while/body/ppermute | solution.py:234
  12.0 12.7 %collective-permute-start.1 = (bf16[512,128]{1,0:T(8,128)(2,1)S(1)}, bf16[512,128]{1,0:T(8,128)(2,1)S(1)}, u32[]{:S(2)}, u32[]{:S(2)}) collective-permute-start(bf16[512,128]{1,0:T(8,128)(2,1)S(1)} %fusion.15), channel_id=1, source_target_pairs={{0,2},{1,3},{2,0},{3,1},{4,6},{5,7},{6,4},{7,5},{8,10},{9,11},{10,... | collective-permute-start | bytes 393224 | tf_op jit(solution)/shard_map/while/body/ppermute | solution.py:234
  26.4 15.2 %collective-permute-start.5 = (bf16[512,128]{1,0:T(8,128)(2,1)S(1)}, bf16[512,128]{1,0:T(8,128)(2,1)S(1)}, u32[]{:S(2)}, u32[]{:S(2)}) collective-permute-start(bf16[512,128]{1,0:T(8,128)(2,1)S(1)} %convert_element_type.45), channel_id=1, source_target_pairs={{0,4},{1,5},{2,6},{3,7},{4,0},{5,1},{6,2},{7,3},{8,12},{9,13},{10,... | collective-permute-start | bytes 393224 | tf_op jit(solution)/shard_map/while/body/ppermute | solution.py:234
  35.8 0.8 copy-start.4
  36.6 6.3 %copy-start.1 = (f32[512,128]{1,0:T(8,128)S(1)}, f32[512,128]{1,0:T(8,128)}, u32[]{:S(2)}) copy-start(f32[512,128]{1,0:T(8,128)} %get-tuple-element.274) | copy-start | bytes 786436
  36.6 22.0 %collective-permute-start.4 = (bf16[512,512]{1,0:T(8,128)(2,1)S(1)}, bf16[512,512]{1,0:T(8,128)(2,1)S(1)}, u32[]{:S(2)}, u32[]{:S(2)}) collective-permute-start(bf16[512,512]{1,0:T(8,128)(2,1)S(1)} %broadcast_select_fusion.2), channel_id=1, source_target_pairs={{0,8},{8,0},{16,24},{24,16},{32,40},{40,32},{48,56},{56,48},{64,72... | collective-permute-start | bytes 1572872 | tf_op jit(solution)/shard_map/ppermute | solution.py:239
  43.0 3.2 %collective-permute-start.2 = (bf16[512,128]{1,0:T(8,128)(2,1)S(1)}, bf16[512,128]{1,0:T(8,128)(2,1)S(1)}, u32[]{:S(2)}, u32[]{:S(2)}) collective-permute-start(bf16[512,128]{1,0:T(8,128)(2,1)S(1)} %add_convert_fusion.2), channel_id=1, source_target_pairs={{0,1},{1,0},{2,3},{3,2},{4,5},{5,4},{6,7},{7,6},{8,9},{9,8},{10,11... | collective-permute-start | bytes 393224 | tf_op jit(solution)/shard_map/while/body/ppermute | solution.py:234
  46.9 7.6 %collective-permute-start.7 = (bf16[512,128]{1,0:T(8,128)(2,1)}, bf16[512,128]{1,0:T(8,128)(2,1)S(1)}, u32[]{:S(2)}, u32[]{:S(2)}) collective-permute-start(bf16[512,128]{1,0:T(8,128)(2,1)} %get-tuple-element.126.x0_ref), channel_id=1, source_target_pairs={{0,16},{8,24},{16,32},{24,40},{32,48},{40,56},{48,64},{56,72},{64,... | collective-permute-start | bytes 393224 | tf_op jit(solution)/shard_map/ppermute | solution.py:229
  50.3 8.3 %collective-permute-start.6 = (bf16[512,128]{1,0:T(8,128)(2,1)}, bf16[512,128]{1,0:T(8,128)(2,1)S(1)}, u32[]{:S(2)}, u32[]{:S(2)}) collective-permute-start(bf16[512,128]{1,0:T(8,128)(2,1)} %get-tuple-element.126.x0_ref), channel_id=1, source_target_pairs={{0,8},{8,16},{16,24},{24,32},{32,40},{40,48},{48,56},{56,64},{64,7... | collective-permute-start | bytes 393224 | tf_op jit(solution)/shard_map/ppermute | solution.py:229
  54.6 4.0 %copy-start.9 = (bf16[512,128]{1,0:T(8,128)(2,1)}, bf16[512,128]{1,0:T(8,128)(2,1)S(1)}, u32[]{:S(2)}) copy-start(bf16[512,128]{1,0:T(8,128)(2,1)S(1)} %collective-permute-done.7.x2_ref) | copy-start | bytes 393220
  58.6 0.7 copy-start.10
  58.6 0.8 copy-start.8
  81.5 15.4 %collective-permute-start.8 = (bf16[512,512]{1,0:T(8,128)(2,1)}, bf16[512,512]{1,0:T(8,128)(2,1)S(1)}, u32[]{:S(2)}, u32[]{:S(2)}) collective-permute-start(bf16[512,512]{1,0:T(8,128)(2,1)} %get-tuple-element.130), channel_id=1, source_target_pairs={{0,8},{8,0},{16,24},{24,16},{32,40},{40,32},{48,56},{56,48},{64,72... | collective-permute-start | bytes 1572872 | tf_op jit(solution)/shard_map/ppermute | solution.py:239
  85.3 11.6 %copy-start.5 = (bf16[512,512]{1,0:T(8,128)(2,1)S(1)}, bf16[512,512]{1,0:T(8,128)(2,1)}, u32[]{:S(2)}) copy-start(bf16[512,512]{1,0:T(8,128)(2,1)} %get-tuple-element.131) | copy-start | bytes 1572868
  85.3 23.2 %all-to-all-start = ((bf16[64,2,1536]{2,1,0:T(2,128)(2,1)}), bf16[64,2,1536]{2,1,0:T(2,128)(2,1)S(1)}, u32[]{:S(2)}, u32[]{:S(2)}) async-start(bf16[64,2,1536]{2,1,0:T(2,128)(2,1)} %reshape.17), calls=%async_computation | async-start | bytes 786432 | tf_op jit(solution)/shard_map/all_to_all | solution.py:286
  96.9 21.3 %copy-start.2 = (f32[512,512]{1,0:T(8,128)S(1)}, f32[512,512]{1,0:T(8,128)}, u32[]{:S(2)}) copy-start(f32[512,512]{1,0:T(8,128)} %get-tuple-element.129) | copy-start | bytes 3145732
  97.9 20.3 %collective-permute-start.9 = (bf16[512,512]{1,0:T(8,128)(2,1)}, bf16[512,512]{1,0:T(8,128)(2,1)S(1)}, u32[]{:S(2)}, u32[]{:S(2)}) collective-permute-start(bf16[512,512]{1,0:T(8,128)(2,1)} %fusion.4), channel_id=1, source_target_pairs={{16,0},{24,8},{32,16},{40,24},{48,32},{56,40},{64,48},{72,56},{80,... | collective-permute-start | bytes 1572872 | tf_op jit(solution)/shard_map/ppermute | solution.py:229

commit v4 on v3

v4 whole, which is shorter than its diff:
```python
import jax
import jax.numpy as jnp
import numpy as np
from jax import lax
from jax.experimental import pallas as pl
from jax.experimental.pallas import tpu as pltpu
from jax.sharding import PartitionSpec as P

WINDOW = 1024
HD = 128
TOK = 512
QT = 256
KB = 256
ATTN_VMEM = 60 << 20
SPAN = 1536
NBLK = 5
score_scale = 168.0 ** (-0.5)
LOG2E = 1.4426950408889634
epsilon = 1e-06
rope_base = 10000.0
F32 = jnp.float32
BF16 = jnp.bfloat16


def rope_tables(shards):
    freq = rope_base ** (-(np.arange(64, dtype=np.float64) * 2.0 / HD))
    freq = np.concatenate([freq, freq])[None, :]
    base = ((np.arange(shards + 2) - 2) * TOK).astype(np.float64)[:, None] * freq
    local = np.arange(TOK, dtype=np.float64)[:, None] * freq
    pad = (-base.shape[0]) % 8
    base = np.pad(base, ((0, pad), (0, 0)))
    tables = [np.cos(base), np.sin(base), np.cos(local), np.sin(local)]
    return [t.astype(np.float32) for t in tables]


def lane_mean(x):
    high = x.astype(BF16)
    low = (x - high.astype(F32)).astype(BF16)
    ones = jnp.full((HD, HD), 1.0 / HD, BF16)
    return mm(high, ones) + mm(low, ones)


def norm_scale(raw):
    return lax.rsqrt(lane_mean(raw * raw) + epsilon)


def rope_forward(normed, cos, sin_signed):
    return normed * cos + pltpu.roll(normed, 64, 1) * sin_signed


def prep_back(raw, r, gain, cos, sin_signed, grad):
    d_norm = (grad * cos - pltpu.roll(grad, 64, 1) * sin_signed) * gain
    return r * d_norm - raw * ((r * r * r) * lane_mean(raw * d_norm))


def mm(a, b):
    return lax.dot_general(a, b, (((1,), (0,)), ((), ())), preferred_element_type=F32)


def mm_t(a, b):
    return lax.dot_general(a, b, (((1,), (1,)), ((), ())), preferred_element_type=F32)


N_IN = 10


def attention_kernel(
    shard_ref, q_hbm, do_hbm, k0_hbm, v0_hbm, kv1_hbm, kv2_hbm, x0_hbm, x1_hbm, x2_hbm, y_hbm,
    qg_ref, kg_ref, cb_ref, sb_ref, cl_ref, sl_ref,
    qgrad_hbm, own_hbm, back1_hbm, back2_hbm, sk_ref,
    q_ref, do_ref, k0_ref, v0_ref, kv1_ref, kv2_ref, x0_ref, x1_ref, x2_ref, y_ref,
    qgrad_ref, own_ref, back1_ref, back2_ref,
    kp, vx, r_k, cos, sin, e_sc, dp_sc, dkt, dvt, xt, yt, skq, sko, in_sems, out_sems,
):
    sources = (k0_hbm, kv2_hbm, kv1_hbm, v0_hbm, x0_hbm, x1_hbm, x2_hbm, y_hbm, q_hbm, do_hbm)
    targets = (k0_ref, kv2_ref, kv1_ref, v0_ref, x0_ref, x1_ref, x2_ref, y_ref, q_ref, do_ref)
    loads = [pltpu.make_async_copy(a, b, in_sems.at[n]) for n, (a, b) in enumerate(zip(sources, targets))]
    for load in loads:
        load.start()
    shard = shard_ref[0]
    lane = lax.broadcasted_iota(jnp.int32, (1, HD), 1)
    sign = jnp.where(lane < HD // 2, -1.0, 1.0)
    for part in range(3):
        cb = cb_ref[pl.ds(shard + part, 1), :]
        sb = sb_ref[pl.ds(shard + part, 1), :]
        rows = slice(part * TOK, (part + 1) * TOK)
        cos[rows, :] = cb * cl_ref[...] - sb * sl_ref[...]
        sin[rows, :] = (sb * cl_ref[...] + cb * sl_ref[...]) * sign
    for load in loads:
        load.wait()
    for part, x_ref in enumerate((x2_ref, x1_ref, x0_ref)):
        xt[:, part * TOK : (part + 1) * TOK] = x_ref[...].astype(F32).T.astype(BF16)
    yt[...] = y_ref[...].astype(F32).T.astype(BF16)
    refs = (
        shard, q_ref, do_ref, k0_ref, v0_ref, kv1_ref, kv2_ref, qg_ref, kg_ref,
        qgrad_ref, own_ref, back1_ref, back2_ref, sk_ref,
        kp, vx, r_k, cos, sin, e_sc, dp_sc, dkt, dvt, xt, yt, skq, sko,
    )

    def stores(head):
        lanes = pl.ds(pl.multiple_of(head * 2 * HD, 2 * HD), 2 * HD)
        out = [(qgrad_ref.at[:, lanes], qgrad_hbm.at[:, lanes])]
        for kind in range(2):
            lanes = pl.ds(pl.multiple_of(head * HD + kind * 2 * HD, HD), HD)
            for a, b in ((own_ref, own_hbm), (back1_ref, back1_hbm), (back2_ref, back2_hbm)):
                out.append((a.at[:, lanes], b.at[:, lanes]))
        return [pltpu.make_async_copy(a, b, out_sems.at[head, n]) for n, (a, b) in enumerate(out)]

    @pl.loop(0, 4)
    def _(step):
        head = step // 2
        attention_step(head, step % 2, *refs)

        @pl.when(step % 2 == 1)
        def _():
            for store in stores(head):
                store.start()

    for head in range(2):
        for store in stores(head):
            store.wait()


def attention_step(
    head, tile, shard, q_ref, do_ref, k0_ref, v0_ref, kv1_ref, kv2_ref, qg_ref, kg_ref,
    qgrad_ref, own_ref, back1_ref, back2_ref, sk_ref,
    kp, vx, r_k, cos, sin, e_sc, dp_sc, dkt, dvt, xt, yt, skq, sko,
):
    k_lanes = pl.ds(pl.multiple_of(head * HD, HD), HD)
    v_lanes = pl.ds(pl.multiple_of(head * HD + 2 * HD, HD), HD)
    k_parts = (kv2_ref.at[:, k_lanes], kv1_ref.at[:, k_lanes], k0_ref.at[:, k_lanes])
    v_parts = (kv2_ref.at[:, v_lanes], kv1_ref.at[:, v_lanes], v0_ref.at[:, k_lanes])

    @pl.when(tile == 0)
    def _():
        skq[...] = jnp.zeros_like(skq)
        sko[...] = jnp.zeros_like(sko)
        for part, (k_ref, v_ref) in enumerate(zip(k_parts, v_parts)):
            rows = slice(part * TOK, (part + 1) * TOK)
            raw = k_ref[...].astype(F32)
            r = norm_scale(raw)
            r_k[rows, :] = r
            normed = raw * r * kg_ref[...]
            kp[rows, :] = rope_forward(normed, cos[rows, :], sin[rows, :]).astype(BF16)
            vx[rows, :] = v_ref[...]
        dkt[...] = jnp.zeros_like(dkt)
        dvt[...] = jnp.zeros_like(dvt)

    tile_rows = pl.ds(pl.multiple_of(tile * QT, QT), QT)
    q_rows = pl.ds(pl.multiple_of(2 * TOK + tile * QT, QT), QT)
    q_lanes = [pl.ds(pl.multiple_of(head * 2 * HD + g * HD, HD), HD) for g in range(2)]
    cos_q = cos[q_rows, :]
    sin_q = sin[q_rows, :]
    q_parts = []
    r_parts = []
    for lanes in q_lanes:
        raw = q_ref[tile_rows, lanes].astype(F32)
        r_parts.append(norm_scale(raw))
        q_parts.append(rope_forward(raw * r_parts[-1] * qg_ref[...], cos_q, sin_q))
    q = jnp.concatenate(q_parts, axis=0)
    d_out = jnp.concatenate([do_ref[tile_rows, lanes] for lanes in q_lanes], axis=0)
    q_low = q.astype(BF16)
    q_t = q.T.astype(BF16)
    do_t = d_out.astype(F32).T.astype(BF16)

    rows_i = lax.broadcasted_iota(jnp.int32, (2 * QT, KB), 0) % QT
    cols_i = lax.broadcasted_iota(jnp.int32, (2 * QT, KB), 1)

    l_acc = jnp.zeros((2 * QT, HD), F32)
    u_acc = jnp.zeros((2 * QT, HD), F32)
    for b in range(NBLK):
        at = pl.ds(pl.multiple_of(tile * QT + b * KB, KB), KB)
        cols = slice(b * KB, (b + 1) * KB)
        s = mm_t(q_low, kp[at, :])
        e = jnp.exp2(s * (score_scale * LOG2E))
        key_shard = shard - 2 + (tile * QT + b * KB) // TOK
        if b == 0:
            e = jnp.where((cols_i > rows_i) & (key_shard >= 0), e, 0.0)
        elif b == NBLK - 1:
            e = jnp.where(cols_i <= rows_i, e, 0.0)
        else:
            e = e * jnp.where(key_shard >= 0, 1.0, 0.0)
        dp = mm_t(d_out, vx[at, :])
        ed = e * dp
        l_acc = l_acc + e[:, :HD] + e[:, HD:]
        u_acc = u_acc + ed[:, :HD] + ed[:, HD:]
        e_sc[:, cols] = e
        dp_sc[:, cols] = dp
    inv = 1.0 / jnp.sum(l_acc, axis=-1, keepdims=True)
    delta = jnp.sum(u_acc, axis=-1, keepdims=True) * inv

    out = jnp.zeros((2 * QT, HD), F32)
    dq = jnp.zeros((2 * QT, HD), F32)
    for b in range(NBLK):
        at = pl.ds(pl.multiple_of(tile * QT + b * KB, KB), KB)
        cols = slice(b * KB, (b + 1) * KB)
        p = e_sc[:, cols] * inv
        ds = (p * (dp_sc[:, cols] - delta)).astype(BF16)
        p = p.astype(BF16)
        out = out + mm(p, vx[at, :])
        dq = dq + mm(ds, kp[at, :])
        dvt[:, at] += mm(do_t, p)
        dkt[:, at] += mm(q_t, ds)
    x_tile = xt[:, q_rows]
    y_tile = yt[:, tile_rows]
    for g in range(2):
        rows = slice(g * QT, (g + 1) * QT)
        lanes = slice(g * HD, (g + 1) * HD)
        raw = q_ref[tile_rows, q_lanes[g]].astype(F32)
        q_grad = prep_back(raw, r_parts[g], qg_ref[...], cos_q, sin_q, dq[rows] * score_scale).astype(BF16)
        qgrad_ref[tile_rows, q_lanes[g]] = q_grad
        skq[:, lanes] += mm(x_tile, q_grad)
        sko[:, lanes] += mm(y_tile, out[rows].astype(BF16))

    @pl.when(tile == 1)
    def _():
        sk_k = jnp.zeros((HD, HD), F32)
        sk_v = jnp.zeros((HD, HD), F32)
        for part, k_ref in enumerate(k_parts):
            rows = slice(part * TOK, (part + 1) * TOK)
            raw = k_ref[...].astype(F32)
            dk = prep_back(
                raw, r_k[rows, :], kg_ref[...], cos[rows, :], sin[rows, :], dkt[:, rows].T * score_scale
            )
            dv = dvt[:, rows].T
            sk_k = sk_k + mm(xt[:, rows], dk.astype(BF16))
            sk_v = sk_v + mm(xt[:, rows], dv.astype(BF16))
            target = (back2_ref, back1_ref, own_ref)[part]
            target[:, k_lanes] = dk.astype(target.dtype)
            target[:, v_lanes] = dv.astype(target.dtype)
        sk_ref[:, pl.ds(pl.multiple_of(head * 2 * HD, 2 * HD), 2 * HD)] = skq[...].astype(BF16)
        sk_ref[:, pl.ds(pl.multiple_of(head * HD + 4 * HD, HD), HD)] = sk_k.astype(BF16)
        sk_ref[:, pl.ds(pl.multiple_of(head * HD + 6 * HD, HD), HD)] = sk_v.astype(BF16)
        sk_ref[:, pl.ds(pl.multiple_of(head * 2 * HD + 8 * HD, 2 * HD), 2 * HD)] = sko[...].astype(BF16)


def attention(shard, q_raw, d_out, k_raw, values, kv1, kv2, sketches, q_gain, k_gain, tables):
    vmem = pl.BlockSpec(memory_space=pltpu.VMEM)
    arrays = [q_raw, d_out, k_raw, values, kv1, kv2, *sketches, q_gain[None, :], k_gain[None, :]] + tables
    return pl.pallas_call(
        attention_kernel,
        in_specs=[pl.BlockSpec(memory_space=pltpu.SMEM)] + [pl.BlockSpec(memory_space=pl.ANY)] * N_IN + [vmem] * 6,
        out_specs=[pl.BlockSpec(memory_space=pl.ANY)] * 4 + [vmem],
        out_shape=[
            jax.ShapeDtypeStruct((TOK, 4 * HD), BF16),
            jax.ShapeDtypeStruct((TOK, 4 * HD), F32),
            jax.ShapeDtypeStruct((TOK, 4 * HD), BF16),
            jax.ShapeDtypeStruct((TOK, 4 * HD), BF16),
            jax.ShapeDtypeStruct((HD, 12 * HD), BF16),
        ],
        scratch_shapes=[pltpu.VMEM(a.shape, a.dtype) for a in arrays[:N_IN]] + [
            pltpu.VMEM((TOK, 4 * HD), BF16),
            pltpu.VMEM((TOK, 4 * HD), F32),
            pltpu.VMEM((TOK, 4 * HD), BF16),
            pltpu.VMEM((TOK, 4 * HD), BF16),
            pltpu.VMEM((SPAN, HD), BF16),
            pltpu.VMEM((SPAN, HD), BF16),
            pltpu.VMEM((SPAN, HD), F32),
            pltpu.VMEM((SPAN, HD), F32),
            pltpu.VMEM((SPAN, HD), F32),
            pltpu.VMEM((2 * QT, NBLK * KB), F32),
            pltpu.VMEM((2 * QT, NBLK * KB), F32),
            pltpu.VMEM((HD, SPAN), F32),
            pltpu.VMEM((HD, SPAN), F32),
            pltpu.VMEM((HD, SPAN), BF16),
            pltpu.VMEM((HD, TOK), BF16),
            pltpu.VMEM((HD, 2 * HD), F32),
            pltpu.VMEM((HD, 2 * HD), F32),
            pltpu.SemaphoreType.DMA((N_IN,)),
            pltpu.SemaphoreType.DMA((2, 7)),
        ],
        compiler_params=pltpu.CompilerParams(vmem_limit_bytes=ATTN_VMEM),
        cost_estimate=pl.CostEstimate(
            flops=6 * 4 * 2 * TOK * SPAN * HD, bytes_accessed=6 << 20, transcendentals=4 * TOK * SPAN
        ),
    )(shard, *arrays)


def shift(x, by):
    count = lax.axis_size("seq")
    pairs = [(i, i + by) for i in range(count) if 0 <= i + by < count]
    return lax.ppermute(x, "seq", pairs)


def swap(x, bit):
    count = lax.axis_size("head")
    return lax.ppermute(x, "head", [(i, i ^ bit) for i in range(count)])


def pair_swap(x):
    count = lax.axis_size("seq")
    return lax.ppermute(x, "seq", [(i, i ^ 1) for i in range(count)])


def one_turn(step, start):
    return lax.fori_loop(0, lax.optimization_barrier(jnp.int32(1)), lambda i, carry: step(), start)


def per_device(
    layer_input, omega_in, upstream, omega_out, q_raw, k_raw, values, d_out, q_gain, k_gain
):
    kv = jnp.concatenate([k_raw, values], axis=1)
    kv, layer_input, upstream = lax.optimization_barrier((kv, layer_input, upstream))
    odd = lax.axis_index("seq") % 2 == 1
    first = lax.axis_index("head") % 2 == 0
    kv2 = shift(kv, 2)
    partial_x = jnp.dot(layer_input, omega_in, preferred_element_type=F32)
    partial_y = jnp.dot(upstream, omega_out, preferred_element_type=F32)

    def sum_near():
        got = swap(jnp.where(first, partial_y, partial_x).astype(BF16), 1)
        total = jnp.where(first, partial_x, partial_y) + got.astype(F32)
        return total + swap(total.astype(BF16), 2).astype(F32)

    half = one_turn(sum_near, partial_x)
    kv1 = pair_swap(jnp.where(odd, kv2, kv))

    def sum_far():
        mine = (half + swap(half.astype(BF16), 6).astype(F32)).astype(BF16)
        other = swap(mine, 1)
        return jnp.where(first, mine, other), jnp.where(first, other, mine)

    x0, y0 = sum_far()
    x1 = shift(x0, 1)
    x2 = shift(x0, 2)
    shard = lax.axis_index("seq").astype(jnp.int32)[None]
    tables = [jnp.asarray(t) for t in rope_tables(lax.axis_size("seq"))]
    query_grad, own, back1, back2, sketches = attention(
        shard, q_raw, d_out, k_raw, values, kv1, kv2, (x0, x1, x2, y0), q_gain, k_gain, tables
    )
    near = pair_swap(back1).astype(F32)
    back2 = back2.astype(F32)
    far = shift(jnp.where(odd, back2 + near, back2).astype(BF16), -2)
    shards = lax.axis_size("seq")
    pieces = lax.all_to_all(sketches.reshape(shards, HD // shards, 12 * HD), "seq", 0, 0, tiled=True)
    total = jnp.sum(pieces.astype(F32), axis=0)
    kv_grad = (own + jnp.where(odd, 0.0, near) + far.astype(F32)).astype(BF16)

    q_cols, kv_cols = 4 * HD, 2 * HD
    return (
        query_grad,
        kv_grad[:, :kv_cols],
        kv_grad[:, kv_cols:],
        total[:, :q_cols],
        total[:, q_cols : q_cols + kv_cols],
        total[:, q_cols + kv_cols : q_cols + 2 * kv_cols],
        total[:, q_cols + 2 * kv_cols :],
    )


def solution(mesh):
    split = P("seq", "head")
    in_specs = (split, P("head", None), split, P("head", None), split, split, split, split, P(), P())
    return jax.shard_map(
        per_device, mesh=mesh, in_specs=in_specs, out_specs=(split,) * 7, check_vma=False
    )
```

time: 120 us -> 115 us (0.958)
  waiting for transfers between devices: 34.1 us -> 30.5 us
  Pallas kernels: 22 us -> 20.4 us
  starting transfers between devices: 48.1 us -> 49.7 us
  local copies, waits for them, and re-layouts: 8.05 us -> 6.48 us
    ppermute x2, starting transfers between devices: 4.43 us -> 8.9 us  [pair_swap(): return lax.ppermute(x, 'seq', [(i, i ^ 1) for i in range(count)])]
    ppermute x4, starting transfers between devices: 19.3 us -> 16.6 us  [swap(): return lax.ppermute(x, 'head', [(i, i ^ bit) for i in range(count)])]
    ppermute x4, waiting for transfers between devices: 11.7 us -> 9.23 us  [swap(): return lax.ppermute(x, 'head', [(i, i ^ bit) for i in range(count)])]
    pallas_call x1, Pallas kernels: 22 us -> 20.4 us  [attention(): pl.pallas_call(attention_kernel, in_specs=[pl.BlockSpec(memory_space=pltp...]
    another operation x2 -> x0, local copies, waits for them, and re-layouts: 1.35 us -> none
    unnamed x22 -> x25, local copies, waits for them, and re-layouts: 2.08 us -> 2.59 us
  transfers between devices with their start and end apart: 11 -> 11, of which waited for: 8 -> 7; matrix products, arithmetic and copies ran while one was open for 8% -> 7% of each run, Pallas kernels for 0% -> 0%
where the time goes in v4:
time: 115 us; the launch traced here: 114 us
  starting transfers between devices  49.7 us (43%)
  waiting for transfers between devices  30.5 us (27%)
  Pallas kernels  20.4 us (18%)
  local copies, waits for them, and re-layouts  6.48 us (6%)
  other arithmetic  5.22 us (5%)
    pallas_call x1, Pallas kernels, attention(): pl.pallas_call(attention_kernel, in_specs=[pl.BlockSpec(memory_space=pltp...  20.4 us
    ppermute x4, starting transfers between devices, swap(): return lax.ppermute(x, 'head', [(i, i ^ bit) for i in range(count)])  16.6 us
    ppermute x4, starting transfers between devices, shift(): return lax.ppermute(x, 'seq', pairs)  13.6 us
    ppermute x4, waiting for transfers between devices, shift(): return lax.ppermute(x, 'seq', pairs)  13.3 us
    all_to_all x1, starting transfers between devices, per_device(): lax.all_to_all(sketches.reshape(shards, HD // shards, 12 * HD), 'seq', 0,...  10.7 us
    ppermute x4, waiting for transfers between devices, swap(): return lax.ppermute(x, 'head', [(i, i ^ bit) for i in range(count)])  9.23 us
    ppermute x2, starting transfers between devices, pair_swap(): return lax.ppermute(x, 'seq', [(i, i ^ 1) for i in range(count)])  8.9 us
    all_to_all x1, waiting for transfers between devices, per_device(): lax.all_to_all(sketches.reshape(shards, HD // shards, 12 * HD), 'seq', 0,...  7.88 us
  transfers between devices with their start and end apart: 11, of which 7 were waited for; matrix products, arithmetic and copies ran while one was open for 7% of the time, Pallas kernels for 0%

profile of v4, /device:TPU:30, one launch (start us, length us, event | category | flops | bytes accessed | tf_op | source)
XLA Modules:
  0.0 114.0 jit_solution(6956187248157932805)
XLA Ops:
  0.7 1.1 %pad_maximum_fusion = bf16[512,512]{1,0:T(8,128)(2,1)S(1)} fusion(bf16[512,256]{1,0:T(8,128)(2,1)} %v0_hbm.1, bf16[512,256]{1,0:T(8,128)(2,1)} %k0_hbm.1), kind=kLoop, calls=%fused_computation.11 | loop fusion | flops 1048576 | bytes 1048576 | tf_op jit(solution)/shard_map/concatenate | solution.py:302
  1.8 4.6 %collective-permute-start.2 = (bf16[512,512]{1,0:T(8,128)(2,1)S(1)}, bf16[512,512]{1,0:T(8,128)(2,1)S(1)}, u32[]{:S(2)}, u32[]{:S(2)}) collective-permute-start(bf16[512,512]{1,0:T(8,128)(2,1)S(1)} %pad_maximum_fusion), channel_id=1, source_target_pairs={{0,16},{8,24},{16,32},{24,40},{32,48},{40,56},{48,64},{56,72},{64,... | collective-permute-start | bytes 1572872 | tf_op jit(solution)/shard_map/ppermute | solution.py:282
  8.3 16.8 %while.10 = (s32[]{:T(128)}, f32[512,128]{1,0:T(8,128)}, s32[]{:T(128)}, pred[]{:T(512)}, f32[512,128]{1,0:T(8,128)S(1)}, /*index=5*/f32[512,128]{1,0:T(8,128)S(1)}, s32[]{:T(128)}) while((s32[]{:T(128)}, f32[512,128]{1,0:T(8,128)}, s32[]{:T(128)}, pred[]{:T(512)}, f32[512,128]{1,0:T(8,128)S(1)}, /*index=5*/f32[512,128]{1,0:T(8,128)S(1)}, ...), condition=%wide.region_1.2_spmd, body=%wide.region_0.1_spmd.sunk | while | flops 655362 | bytes 3539104 | solution.py:296
  8.4 1.9 %collective-permute-start = (bf16[512,128]{1,0:T(8,128)(2,1)S(1)}, bf16[512,128]{1,0:T(8,128)(2,1)S(1)}, u32[]{:S(2)}, u32[]{:S(2)}) collective-permute-start(bf16[512,128]{1,0:T(8,128)(2,1)S(1)} %select_convert_fusion.2), channel_id=1, source_target_pairs={{0,1},{1,0},{2,3},{3,2},{4,5},{5,4},{6,7},{7,6},{8,9},{9,8},{10,11... | collective-permute-start | bytes 393224 | tf_op jit(solution)/shard_map/while/body/ppermute | solution.py:287
  10.3 1.3 %collective-permute-done = bf16[512,128]{1,0:T(8,128)(2,1)S(1)} collective-permute-done((bf16[512,128]{1,0:T(8,128)(2,1)S(1)}, bf16[512,128]{1,0:T(8,128)(2,1)S(1)}, u32[]{:S(2)}, u32[]{:S(2)}) %collective-permute-start) | collective-permute-done | bytes 131104 | tf_op jit(solution)/shard_map/while/body/ppermute | solution.py:287
  11.7 6.1 %collective-permute-start.1 = (bf16[512,128]{1,0:T(8,128)(2,1)S(1)}, bf16[512,128]{1,0:T(8,128)(2,1)S(1)}, u32[]{:S(2)}, u32[]{:S(2)}) collective-permute-start(bf16[512,128]{1,0:T(8,128)(2,1)S(1)} %fusion.15), channel_id=1, source_target_pairs={{0,2},{1,3},{2,0},{3,1},{4,6},{5,7},{6,4},{7,5},{8,10},{9,11},{10,... | collective-permute-start | bytes 393224 | tf_op jit(solution)/shard_map/while/body/ppermute | solution.py:287
  17.8 6.6 %collective-permute-done.1 = bf16[512,128]{1,0:T(8,128)(2,1)S(1)} collective-permute-done((bf16[512,128]{1,0:T(8,128)(2,1)S(1)}, bf16[512,128]{1,0:T(8,128)(2,1)S(1)}, u32[]{:S(2)}, u32[]{:S(2)}) %collective-permute-start.1) | collective-permute-done | bytes 131104 | tf_op jit(solution)/shard_map/while/body/ppermute | solution.py:287
  25.1 1.0 convert_element_type.39
  26.1 6.7 %collective-permute-start.4 = (bf16[512,128]{1,0:T(8,128)(2,1)S(1)}, bf16[512,128]{1,0:T(8,128)(2,1)S(1)}, u32[]{:S(2)}, u32[]{:S(2)}) collective-permute-start(bf16[512,128]{1,0:T(8,128)(2,1)S(1)} %convert_element_type.39), channel_id=1, source_target_pairs={{0,6},{1,7},{2,4},{3,5},{4,2},{5,3},{6,0},{7,1},{8,14},{9,15},{10,... | collective-permute-start | bytes 393224 | tf_op jit(solution)/shard_map/ppermute | solution.py:287
  33.6 6.1 %collective-permute-start.3 = (bf16[512,512]{1,0:T(8,128)(2,1)S(1)}, bf16[512,512]{1,0:T(8,128)(2,1)S(1)}, u32[]{:S(2)}, u32[]{:S(2)}) collective-permute-start(bf16[512,512]{1,0:T(8,128)(2,1)S(1)} %broadcast_select_fusion), channel_id=1, source_target_pairs={{0,8},{8,0},{16,24},{24,16},{32,40},{40,32},{48,56},{56,48},{64,72... | collective-permute-start | bytes 1572872 | tf_op jit(solution)/shard_map/ppermute | solution.py:292
  39.7 1.9 %collective-permute-start.5 = (bf16[512,128]{1,0:T(8,128)(2,1)S(1)}, bf16[512,128]{1,0:T(8,128)(2,1)S(1)}, u32[]{:S(2)}, u32[]{:S(2)}) collective-permute-start(bf16[512,128]{1,0:T(8,128)(2,1)S(1)} %add_convert_fusion), channel_id=1, source_target_pairs={{0,1},{1,0},{2,3},{3,2},{4,5},{5,4},{6,7},{7,6},{8,9},{9,8},{10,11... | collective-permute-start | bytes 393224 | tf_op jit(solution)/shard_map/ppermute | solution.py:287
  41.7 1.3 %collective-permute-done.5 = bf16[512,128]{1,0:T(8,128)(2,1)S(1)} collective-permute-done((bf16[512,128]{1,0:T(8,128)(2,1)S(1)}, bf16[512,128]{1,0:T(8,128)(2,1)S(1)}, u32[]{:S(2)}, u32[]{:S(2)}) %collective-permute-start.5) | collective-permute-done | bytes 131104 | tf_op jit(solution)/shard_map/ppermute | solution.py:287
  43.6 3.4 %collective-permute-start.7 = (bf16[512,128]{1,0:T(8,128)(2,1)S(1)}, bf16[512,128]{1,0:T(8,128)(2,1)S(1)}, u32[]{:S(2)}, u32[]{:S(2)}) collective-permute-start(bf16[512,128]{1,0:T(8,128)(2,1)S(1)} %get-tuple-element.71.x0_hbm), channel_id=1, source_target_pairs={{0,16},{8,24},{16,32},{24,40},{32,48},{40,56},{48,64},{56,72},{64,... | collective-permute-start | bytes 393224 | tf_op jit(solution)/shard_map/ppermute | solution.py:282
  47.0 2.8 %collective-permute-start.6 = (bf16[512,128]{1,0:T(8,128)(2,1)S(1)}, bf16[512,128]{1,0:T(8,128)(2,1)S(1)}, u32[]{:S(2)}, u32[]{:S(2)}) collective-permute-start(bf16[512,128]{1,0:T(8,128)(2,1)S(1)} %get-tuple-element.71.x0_hbm), channel_id=1, source_target_pairs={{0,8},{8,16},{16,24},{24,32},{32,40},{40,48},{48,56},{56,64},{64,7... | collective-permute-start | bytes 393224 | tf_op jit(solution)/shard_map/ppermute | solution.py:282
  49.9 1.2 %collective-permute-done.7.x2_hbm = bf16[512,128]{1,0:T(8,128)(2,1)S(1)} collective-permute-done((bf16[512,128]{1,0:T(8,128)(2,1)S(1)}, bf16[512,128]{1,0:T(8,128)(2,1)S(1)}, u32[]{:S(2)}, u32[]{:S(2)}) %collective-permute-start.7) | collective-permute-done | bytes 131104 | tf_op jit(solution)/shard_map/ppermute | solution.py:282
  51.1 4.0 %collective-permute-done.6.x1_hbm = bf16[512,128]{1,0:T(8,128)(2,1)S(1)} collective-permute-done((bf16[512,128]{1,0:T(8,128)(2,1)S(1)}, bf16[512,128]{1,0:T(8,128)(2,1)S(1)}, u32[]{:S(2)}, u32[]{:S(2)}) %collective-permute-start.6) | collective-permute-done | bytes 131104 | tf_op jit(solution)/shard_map/ppermute | solution.py:282
  55.9 20.4 %shard_map.189 = (bf16[512,512]{1,0:T(8,128)(2,1)}, f32[512,512]{1,0:T(8,128)}, bf16[512,512]{1,0:T(8,128)(2,1)}, bf16[512,512]{1,0:T(8,128)(2,1)}, bf16[128,1536]{1,0:T(8,128)(2,1)}) custom-call(s32[1]{0:T(128)} %bitcast.shard_ref, bf16[512,512]{1,0:T(8,128)(2,1)} %q_hbm.1, bf16[512,512]{1,0:T(8,128)(2,1)} %do_hbm.1, bf16[512,256]{1,0:T(8,128)(2,1)} %k0_hbm.1, ...), custom_call_target="tpu_custom_call" | custom-call | flops 4831838208 | bytes 6291456 | tf_op jit(solution)/shard_map/pallas_call | solution.py:240
  76.3 2.8 %collective-permute-start.8 = (bf16[512,512]{1,0:T(8,128)(2,1)}, bf16[512,512]{1,0:T(8,128)(2,1)S(1)}, u32[]{:S(2)}, u32[]{:S(2)}) collective-permute-start(bf16[512,512]{1,0:T(8,128)(2,1)} %get-tuple-element.53), channel_id=1, source_target_pairs={{0,8},{8,0},{16,24},{24,16},{32,40},{40,32},{48,56},{56,48},{64,72... | collective-permute-start | bytes 1572872 | tf_op jit(solution)/shard_map/ppermute | solution.py:292
  79.2 1.9 %reshape.17 = bf16[64,2,1536]{2,1,0:T(2,128)(2,1)} reshape(bf16[128,1536]{1,0:T(8,128)(2,1)} %get-tuple-element.55) | data formatting | bytes 786432 | tf_op jit(solution)/shard_map/reshape | solution.py:335
  81.1 10.7 %all-to-all-start = ((bf16[64,2,1536]{2,1,0:T(2,128)(2,1)}), bf16[64,2,1536]{2,1,0:T(2,128)(2,1)S(1)}, u32[]{:S(2)}, u32[]{:S(2)}) async-start(bf16[64,2,1536]{2,1,0:T(2,128)(2,1)} %reshape.17), calls=%async_computation | async-start | bytes 786432 | tf_op jit(solution)/shard_map/all_to_all | solution.py:335
  91.7 1.0 fusion.4
  92.7 2.7 %collective-permute-start.9 = (bf16[512,512]{1,0:T(8,128)(2,1)}, bf16[512,512]{1,0:T(8,128)(2,1)S(1)}, u32[]{:S(2)}, u32[]{:S(2)}) collective-permute-start(bf16[512,512]{1,0:T(8,128)(2,1)} %fusion.4), channel_id=1, source_target_pairs={{16,0},{24,8},{32,16},{40,24},{48,32},{56,40},{64,48},{72,56},{80,... | collective-permute-start | bytes 1572872 | tf_op jit(solution)/shard_map/ppermute | solution.py:282
  95.5 7.9 %all-to-all-done = bf16[64,2,1536]{2,1,0:T(2,128)(2,1)S(1)} async-done(((bf16[64,2,1536]{2,1,0:T(2,128)(2,1)}), bf16[64,2,1536]{2,1,0:T(2,128)(2,1)S(1)}, u32[]{:S(2)}, u32[]{:S(2)}) %all-to-all-start) | async-done | bytes 393248 | tf_op jit(solution)/shard_map/all_to_all | solution.py:335
  104.9 8.1 %collective-permute-done.9 = bf16[512,512]{1,0:T(8,128)(2,1)S(1)} collective-permute-done((bf16[512,512]{1,0:T(8,128)(2,1)}, bf16[512,512]{1,0:T(8,128)(2,1)S(1)}, u32[]{:S(2)}, u32[]{:S(2)}) %collective-permute-start.9) | collective-permute-done | bytes 524320 | tf_op jit(solution)/shard_map/ppermute | solution.py:282
  (42 shorter events, 7.6 us)
Async XLA Ops:
  0.6 5.8 %copy-start = (bf16[512,672]{0,1:T(8,128)(2,1)S(1)}, bf16[512,672]{0,1:T(8,128)(2,1)}, u32[]{:S(2)}) copy-start(bf16[512,672]{0,1:T(8,128)(2,1)} %param.16) | copy-start | bytes 2064388
  0.6 5.8 %copy-start.6 = (bf16[672,128]{1,0:T(8,128)(2,1)S(1)}, bf16[672,128]{1,0:T(8,128)(2,1)}, u32[]{:S(2)}) copy-start(bf16[672,128]{1,0:T(8,128)(2,1)} %param.17) | copy-start | bytes 516100
  1.8 31.0 %collective-permute-start.2 = (bf16[512,512]{1,0:T(8,128)(2,1)S(1)}, bf16[512,512]{1,0:T(8,128)(2,1)S(1)}, u32[]{:S(2)}, u32[]{:S(2)}) collective-permute-start(bf16[512,512]{1,0:T(8,128)(2,1)S(1)} %pad_maximum_fusion), channel_id=1, source_target_pairs={{0,16},{8,24},{16,32},{24,40},{32,48},{40,56},{48,64},{56,72},{64,... | collective-permute-start | bytes 1572872 | tf_op jit(solution)/shard_map/ppermute | solution.py:282
  6.5 1.1 %copy-start.3 = (bf16[512,672]{0,1:T(8,128)(2,1)S(1)}, bf16[512,672]{0,1:T(8,128)(2,1)}, u32[]{:S(2)}) copy-start(bf16[512,672]{0,1:T(8,128)(2,1)} %param.18) | copy-start | bytes 2064388
  6.9 1.0 copy-start.7
  8.4 3.2 %collective-permute-start = (bf16[512,128]{1,0:T(8,128)(2,1)S(1)}, bf16[512,128]{1,0:T(8,128)(2,1)S(1)}, u32[]{:S(2)}, u32[]{:S(2)}) collective-permute-start(bf16[512,128]{1,0:T(8,128)(2,1)S(1)} %select_convert_fusion.2), channel_id=1, source_target_pairs={{0,1},{1,0},{2,3},{3,2},{4,5},{5,4},{6,7},{7,6},{8,9},{9,8},{10,11... | collective-permute-start | bytes 393224 | tf_op jit(solution)/shard_map/while/body/ppermute | solution.py:287
  11.7 12.7 %collective-permute-start.1 = (bf16[512,128]{1,0:T(8,128)(2,1)S(1)}, bf16[512,128]{1,0:T(8,128)(2,1)S(1)}, u32[]{:S(2)}, u32[]{:S(2)}) collective-permute-start(bf16[512,128]{1,0:T(8,128)(2,1)S(1)} %fusion.15), channel_id=1, source_target_pairs={{0,2},{1,3},{2,0},{3,1},{4,6},{5,7},{6,4},{7,5},{8,10},{9,11},{10,... | collective-permute-start | bytes 393224 | tf_op jit(solution)/shard_map/while/body/ppermute | solution.py:287
  26.1 13.6 %collective-permute-start.4 = (bf16[512,128]{1,0:T(8,128)(2,1)S(1)}, bf16[512,128]{1,0:T(8,128)(2,1)S(1)}, u32[]{:S(2)}, u32[]{:S(2)}) collective-permute-start(bf16[512,128]{1,0:T(8,128)(2,1)S(1)} %convert_element_type.39), channel_id=1, source_target_pairs={{0,6},{1,7},{2,4},{3,5},{4,2},{5,3},{6,0},{7,1},{8,14},{9,15},{10,... | collective-permute-start | bytes 393224 | tf_op jit(solution)/shard_map/ppermute | solution.py:287
  32.8 6.9 %copy-start.1 = (f32[512,128]{1,0:T(8,128)S(1)}, f32[512,128]{1,0:T(8,128)}, u32[]{:S(2)}) copy-start(f32[512,128]{1,0:T(8,128)} %get-tuple-element.50) | copy-start | bytes 786436
  32.8 0.8 copy-start.4
  33.6 21.5 %collective-permute-start.3 = (bf16[512,512]{1,0:T(8,128)(2,1)S(1)}, bf16[512,512]{1,0:T(8,128)(2,1)S(1)}, u32[]{:S(2)}, u32[]{:S(2)}) collective-permute-start(bf16[512,512]{1,0:T(8,128)(2,1)S(1)} %broadcast_select_fusion), channel_id=1, source_target_pairs={{0,8},{8,0},{16,24},{24,16},{32,40},{40,32},{48,56},{56,48},{64,72... | collective-permute-start | bytes 1572872 | tf_op jit(solution)/shard_map/ppermute | solution.py:292
  39.7 3.2 %collective-permute-start.5 = (bf16[512,128]{1,0:T(8,128)(2,1)S(1)}, bf16[512,128]{1,0:T(8,128)(2,1)S(1)}, u32[]{:S(2)}, u32[]{:S(2)}) collective-permute-start(bf16[512,128]{1,0:T(8,128)(2,1)S(1)} %add_convert_fusion), channel_id=1, source_target_pairs={{0,1},{1,0},{2,3},{3,2},{4,5},{5,4},{6,7},{7,6},{8,9},{9,8},{10,11... | collective-permute-start | bytes 393224 | tf_op jit(solution)/shard_map/ppermute | solution.py:287
  43.6 11.5 %copy-start.8 = (bf16[512,128]{1,0:T(8,128)(2,1)}, bf16[512,128]{1,0:T(8,128)(2,1)S(1)}, u32[]{:S(2)}) copy-start(bf16[512,128]{1,0:T(8,128)(2,1)S(1)} %get-tuple-element.71.x0_hbm) | copy-start | bytes 393220
  43.6 7.4 %collective-permute-start.7 = (bf16[512,128]{1,0:T(8,128)(2,1)S(1)}, bf16[512,128]{1,0:T(8,128)(2,1)S(1)}, u32[]{:S(2)}, u32[]{:S(2)}) collective-permute-start(bf16[512,128]{1,0:T(8,128)(2,1)S(1)} %get-tuple-element.71.x0_hbm), channel_id=1, source_target_pairs={{0,16},{8,24},{16,32},{24,40},{32,48},{40,56},{48,64},{56,72},{64,... | collective-permute-start | bytes 393224 | tf_op jit(solution)/shard_map/ppermute | solution.py:282
  47.0 8.1 %collective-permute-start.6 = (bf16[512,128]{1,0:T(8,128)(2,1)S(1)}, bf16[512,128]{1,0:T(8,128)(2,1)S(1)}, u32[]{:S(2)}, u32[]{:S(2)}) collective-permute-start(bf16[512,128]{1,0:T(8,128)(2,1)S(1)} %get-tuple-element.71.x0_hbm), channel_id=1, source_target_pairs={{0,8},{8,16},{16,24},{24,32},{32,40},{40,48},{48,56},{56,64},{64,7... | collective-permute-start | bytes 393224 | tf_op jit(solution)/shard_map/ppermute | solution.py:282
  51.1 4.0 %copy-start.10 = (bf16[512,128]{1,0:T(8,128)(2,1)}, bf16[512,128]{1,0:T(8,128)(2,1)S(1)}, u32[]{:S(2)}) copy-start(bf16[512,128]{1,0:T(8,128)(2,1)S(1)} %collective-permute-done.7.x2_hbm) | copy-start | bytes 393220
  55.1 0.7 copy-start.11
  55.1 0.8 copy-start.9
  76.3 15.4 %collective-permute-start.8 = (bf16[512,512]{1,0:T(8,128)(2,1)}, bf16[512,512]{1,0:T(8,128)(2,1)S(1)}, u32[]{:S(2)}, u32[]{:S(2)}) collective-permute-start(bf16[512,512]{1,0:T(8,128)(2,1)} %get-tuple-element.53), channel_id=1, source_target_pairs={{0,8},{8,0},{16,24},{24,16},{32,40},{40,32},{48,56},{56,48},{64,72... | collective-permute-start | bytes 1572872 | tf_op jit(solution)/shard_map/ppermute | solution.py:292
  81.1 10.7 %copy-start.5 = (bf16[512,512]{1,0:T(8,128)(2,1)S(1)}, bf16[512,512]{1,0:T(8,128)(2,1)}, u32[]{:S(2)}) copy-start(bf16[512,512]{1,0:T(8,128)(2,1)} %get-tuple-element.54) | copy-start | bytes 1572868
  81.1 22.3 %all-to-all-start = ((bf16[64,2,1536]{2,1,0:T(2,128)(2,1)}), bf16[64,2,1536]{2,1,0:T(2,128)(2,1)S(1)}, u32[]{:S(2)}, u32[]{:S(2)}) async-start(bf16[64,2,1536]{2,1,0:T(2,128)(2,1)} %reshape.17), calls=%async_computation | async-start | bytes 786432 | tf_op jit(solution)/shard_map/all_to_all | solution.py:335
  91.7 21.3 %copy-start.2 = (f32[512,512]{1,0:T(8,128)S(1)}, f32[512,512]{1,0:T(8,128)}, u32[]{:S(2)}) copy-start(f32[512,512]{1,0:T(8,128)} %get-tuple-element.52) | copy-start | bytes 3145732
  92.7 20.3 %collective-permute-start.9 = (bf16[512,512]{1,0:T(8,128)(2,1)}, bf16[512,512]{1,0:T(8,128)(2,1)S(1)}, u32[]{:S(2)}, u32[]{:S(2)}) collective-permute-start(bf16[512,512]{1,0:T(8,128)(2,1)} %fusion.4), channel_id=1, source_target_pairs={{16,0},{24,8},{32,16},{40,24},{48,32},{56,40},{64,48},{72,56},{80,... | collective-permute-start | bytes 1572872 | tf_op jit(solution)/shard_map/ppermute | solution.py:282

commit v5 on v4

--- a/solution.py
+++ b/solution.py
@@ -61,23 +61,26 @@
     return lax.dot_general(a, b, (((1,), (1,)), ((), ())), preferred_element_type=F32)
 
 
-N_IN = 10
+N_IN = 16
 
 
 def attention_kernel(
     shard_ref, q_hbm, do_hbm, k0_hbm, v0_hbm, kv1_hbm, kv2_hbm, x0_hbm, x1_hbm, x2_hbm, y_hbm,
+    qg_hbm, kg_hbm, cb_hbm, sb_hbm, cl_hbm, sl_hbm,
+    qgrad_hbm, own_hbm, back1_hbm, back2_hbm, sk_hbm,
+    q_ref, do_ref, k0_ref, v0_ref, kv1_ref, kv2_ref, x0_ref, x1_ref, x2_ref, y_ref,
     qg_ref, kg_ref, cb_ref, sb_ref, cl_ref, sl_ref,
-    qgrad_hbm, own_hbm, back1_hbm, back2_hbm, sk_ref,
-    q_ref, do_ref, k0_ref, v0_ref, kv1_ref, kv2_ref, x0_ref, x1_ref, x2_ref, y_ref,
-    qgrad_ref, own_ref, back1_ref, back2_ref,
+    qgrad_ref, own_ref, back1_ref, back2_ref, sk_ref,
     kp, vx, r_k, cos, sin, e_sc, dp_sc, dkt, dvt, xt, yt, skq, sko, in_sems, out_sems,
 ):
-    sources = (k0_hbm, kv2_hbm, kv1_hbm, v0_hbm, x0_hbm, x1_hbm, x2_hbm, y_hbm, q_hbm, do_hbm)
-    targets = (k0_ref, kv2_ref, kv1_ref, v0_ref, x0_ref, x1_ref, x2_ref, y_ref, q_ref, do_ref)
+    sources = (cb_hbm, sb_hbm, cl_hbm, sl_hbm, qg_hbm, kg_hbm) + (k0_hbm, kv2_hbm, kv1_hbm, v0_hbm, q_hbm, do_hbm, x0_hbm, x1_hbm, x2_hbm, y_hbm)
+    targets = (cb_ref, sb_ref, cl_ref, sl_ref, qg_ref, kg_ref) + (k0_ref, kv2_ref, kv1_ref, v0_ref, q_ref, do_ref, x0_ref, x1_ref, x2_ref, y_ref)
     loads = [pltpu.make_async_copy(a, b, in_sems.at[n]) for n, (a, b) in enumerate(zip(sources, targets))]
     for load in loads:
         load.start()
     shard = shard_ref[0]
+    for load in loads[:6]:
+        load.wait()
     lane = lax.broadcasted_iota(jnp.int32, (1, HD), 1)
     sign = jnp.where(lane < HD // 2, -1.0, 1.0)
     for part in range(3):
@@ -86,11 +89,20 @@
         rows = slice(part * TOK, (part + 1) * TOK)
         cos[rows, :] = cb * cl_ref[...] - sb * sl_ref[...]
         sin[rows, :] = (sb * cl_ref[...] + cb * sl_ref[...]) * sign
-    for load in loads:
+    for load in loads[6:10]:
         load.wait()
-    for part, x_ref in enumerate((x2_ref, x1_ref, x0_ref)):
-        xt[:, part * TOK : (part + 1) * TOK] = x_ref[...].astype(F32).T.astype(BF16)
-    yt[...] = y_ref[...].astype(F32).T.astype(BF16)
+
+    def wait_queries():
+        for load in loads[10:12]:
+            load.wait()
+
+    def wait_sketches():
+        for load in loads[12:]:
+            load.wait()
+        for part, x_ref in enumerate((x2_ref, x1_ref, x0_ref)):
+            xt[:, part * TOK : (part + 1) * TOK] = x_ref[...].T
+        yt[...] = y_ref[...].T
+
     refs = (
         shard, q_ref, do_ref, k0_ref, v0_ref, kv1_ref, kv2_ref, qg_ref, kg_ref,
         qgrad_ref, own_ref, back1_ref, back2_ref, sk_ref,
@@ -109,20 +121,23 @@
     @pl.loop(0, 4)
     def _(step):
         head = step // 2
-        attention_step(head, step % 2, *refs)
+        attention_step(head, step % 2, wait_queries, wait_sketches, *refs)
 
         @pl.when(step % 2 == 1)
         def _():
             for store in stores(head):
                 store.start()
 
+    sketch_store = pltpu.make_async_copy(sk_ref, sk_hbm, out_sems.at[0, 7])
+    sketch_store.start()
     for head in range(2):
         for store in stores(head):
             store.wait()
+    sketch_store.wait()
 
 
 def attention_step(
-    head, tile, shard, q_ref, do_ref, k0_ref, v0_ref, kv1_ref, kv2_ref, qg_ref, kg_ref,
+    head, tile, wait_queries, wait_sketches, shard, q_ref, do_ref, k0_ref, v0_ref, kv1_ref, kv2_ref, qg_ref, kg_ref,
     qgrad_ref, own_ref, back1_ref, back2_ref, sk_ref,
     kp, vx, r_k, cos, sin, e_sc, dp_sc, dkt, dvt, xt, yt, skq, sko,
 ):
@@ -146,6 +161,7 @@
         dkt[...] = jnp.zeros_like(dkt)
         dvt[...] = jnp.zeros_like(dvt)
 
+    pl.when((head == 0) & (tile == 0))(wait_queries)
     tile_rows = pl.ds(pl.multiple_of(tile * QT, QT), QT)
     q_rows = pl.ds(pl.multiple_of(2 * TOK + tile * QT, QT), QT)
     q_lanes = [pl.ds(pl.multiple_of(head * 2 * HD + g * HD, HD), HD) for g in range(2)]
@@ -160,10 +176,10 @@
     q = jnp.concatenate(q_parts, axis=0)
     d_out = jnp.concatenate([do_ref[tile_rows, lanes] for lanes in q_lanes], axis=0)
     q_low = q.astype(BF16)
-    q_t = q.T.astype(BF16)
-    do_t = d_out.astype(F32).T.astype(BF16)
-
-    rows_i = lax.broadcasted_iota(jnp.int32, (2 * QT, KB), 0) % QT
+    q_t = q_low.T
+    do_t = d_out.T
+
+    rows_i = lax.broadcasted_iota(jnp.int32, (2 * QT, KB), 0) & (QT - 1)
     cols_i = lax.broadcasted_iota(jnp.int32, (2 * QT, KB), 1)
 
     l_acc = jnp.zeros((2 * QT, HD), F32)
@@ -201,6 +217,7 @@
         dq = dq + mm(ds, kp[at, :])
         dvt[:, at] += mm(do_t, p)
         dkt[:, at] += mm(q_t, ds)
+    pl.when((head == 0) & (tile == 0))(wait_sketches)
     x_tile = xt[:, q_rows]
     y_tile = yt[:, tile_rows]
     for g in range(2):
@@ -228,31 +245,31 @@
             target = (back2_ref, back1_ref, own_ref)[part]
             target[:, k_lanes] = dk.astype(target.dtype)
             target[:, v_lanes] = dv.astype(target.dtype)
-        sk_ref[:, pl.ds(pl.multiple_of(head * 2 * HD, 2 * HD), 2 * HD)] = skq[...].astype(BF16)
-        sk_ref[:, pl.ds(pl.multiple_of(head * HD + 4 * HD, HD), HD)] = sk_k.astype(BF16)
-        sk_ref[:, pl.ds(pl.multiple_of(head * HD + 6 * HD, HD), HD)] = sk_v.astype(BF16)
-        sk_ref[:, pl.ds(pl.multiple_of(head * 2 * HD + 8 * HD, 2 * HD), 2 * HD)] = sko[...].astype(BF16)
+        sk_ref[:, :, pl.ds(pl.multiple_of(head * 2 * HD, 2 * HD), 2 * HD)] = skq[...].astype(BF16).reshape(64, 2, -1)
+        sk_ref[:, :, pl.ds(pl.multiple_of(head * HD + 4 * HD, HD), HD)] = sk_k.astype(BF16).reshape(64, 2, -1)
+        sk_ref[:, :, pl.ds(pl.multiple_of(head * HD + 6 * HD, HD), HD)] = sk_v.astype(BF16).reshape(64, 2, -1)
+        sk_ref[:, :, pl.ds(pl.multiple_of(head * 2 * HD + 8 * HD, 2 * HD), 2 * HD)] = sko[...].astype(BF16).reshape(64, 2, -1)
 
 
 def attention(shard, q_raw, d_out, k_raw, values, kv1, kv2, sketches, q_gain, k_gain, tables):
-    vmem = pl.BlockSpec(memory_space=pltpu.VMEM)
     arrays = [q_raw, d_out, k_raw, values, kv1, kv2, *sketches, q_gain[None, :], k_gain[None, :]] + tables
     return pl.pallas_call(
         attention_kernel,
-        in_specs=[pl.BlockSpec(memory_space=pltpu.SMEM)] + [pl.BlockSpec(memory_space=pl.ANY)] * N_IN + [vmem] * 6,
-        out_specs=[pl.BlockSpec(memory_space=pl.ANY)] * 4 + [vmem],
+        in_specs=[pl.BlockSpec(memory_space=pltpu.SMEM)] + [pl.BlockSpec(memory_space=pl.ANY)] * N_IN,
+        out_specs=[pl.BlockSpec(memory_space=pl.ANY)] * 5,
         out_shape=[
             jax.ShapeDtypeStruct((TOK, 4 * HD), BF16),
             jax.ShapeDtypeStruct((TOK, 4 * HD), F32),
             jax.ShapeDtypeStruct((TOK, 4 * HD), BF16),
             jax.ShapeDtypeStruct((TOK, 4 * HD), BF16),
-            jax.ShapeDtypeStruct((HD, 12 * HD), BF16),
+            jax.ShapeDtypeStruct((64, 2, 12 * HD), BF16),
         ],
         scratch_shapes=[pltpu.VMEM(a.shape, a.dtype) for a in arrays[:N_IN]] + [
             pltpu.VMEM((TOK, 4 * HD), BF16),
             pltpu.VMEM((TOK, 4 * HD), F32),
             pltpu.VMEM((TOK, 4 * HD), BF16),
             pltpu.VMEM((TOK, 4 * HD), BF16),
+            pltpu.VMEM((64, 2, 12 * HD), BF16),
             pltpu.VMEM((SPAN, HD), BF16),
             pltpu.VMEM((SPAN, HD), BF16),
             pltpu.VMEM((SPAN, HD), F32),
@@ -267,7 +284,7 @@
             pltpu.VMEM((HD, 2 * HD), F32),
             pltpu.VMEM((HD, 2 * HD), F32),
             pltpu.SemaphoreType.DMA((N_IN,)),
-            pltpu.SemaphoreType.DMA((2, 7)),
+            pltpu.SemaphoreType.DMA((2, 8)),
         ],
         compiler_params=pltpu.CompilerParams(vmem_limit_bytes=ATTN_VMEM),
         cost_estimate=pl.CostEstimate(
@@ -285,6 +302,11 @@
 def swap(x, bit):
     count = lax.axis_size("head")
     return lax.ppermute(x, "head", [(i, i ^ bit) for i in range(count)])
+
+
+def z_swap(x, turn):
+    count = lax.axis_size("head")
+    return lax.ppermute(x, "head", [(i, i ^ (2, 6)[(i + turn) % 2]) for i in range(count)])
 
 
 def pair_swap(x):
@@ -307,20 +329,18 @@
     partial_x = jnp.dot(layer_input, omega_in, preferred_element_type=F32)
     partial_y = jnp.dot(upstream, omega_out, preferred_element_type=F32)
 
+    keep = jnp.where(first, partial_x, partial_y)
+    give = jnp.where(first, partial_y, partial_x).astype(BF16)
+
     def sum_near():
-        got = swap(jnp.where(first, partial_y, partial_x).astype(BF16), 1)
-        total = jnp.where(first, partial_x, partial_y) + got.astype(F32)
-        return total + swap(total.astype(BF16), 2).astype(F32)
-
-    half = one_turn(sum_near, partial_x)
+        total = keep + swap(give, 1).astype(F32)
+        return (total + z_swap(total.astype(BF16), 0).astype(F32)).astype(BF16)
+
+    half = one_turn(sum_near, keep.astype(BF16))
     kv1 = pair_swap(jnp.where(odd, kv2, kv))
-
-    def sum_far():
-        mine = (half + swap(half.astype(BF16), 6).astype(F32)).astype(BF16)
-        other = swap(mine, 1)
-        return jnp.where(first, mine, other), jnp.where(first, other, mine)
-
-    x0, y0 = sum_far()
+    mine = (half.astype(F32) + z_swap(half, 1).astype(F32)).astype(BF16)
+    other = swap(mine, 1)
+    x0, y0 = jnp.where(first, mine, other), jnp.where(first, other, mine)
     x1 = shift(x0, 1)
     x2 = shift(x0, 2)
     shard = lax.axis_index("seq").astype(jnp.int32)[None]
@@ -331,16 +351,18 @@
     near = pair_swap(back1).astype(F32)
     back2 = back2.astype(F32)
     far = shift(jnp.where(odd, back2 + near, back2).astype(BF16), -2)
-    shards = lax.axis_size("seq")
-    pieces = lax.all_to_all(sketches.reshape(shards, HD // shards, 12 * HD), "seq", 0, 0, tiled=True)
+    pieces = lax.all_to_all(sketches, "seq", 0, 0, tiled=True)
     total = jnp.sum(pieces.astype(F32), axis=0)
-    kv_grad = (own + jnp.where(odd, 0.0, near) + far.astype(F32)).astype(BF16)
-
     q_cols, kv_cols = 4 * HD, 2 * HD
+
+    def finish(begin):
+        cols = slice(begin, begin + kv_cols)
+        return (own[:, cols] + jnp.where(odd, 0.0, near[:, cols]) + far[:, cols].astype(F32)).astype(BF16)
+
     return (
         query_grad,
-        kv_grad[:, :kv_cols],
-        kv_grad[:, kv_cols:],
+        finish(0),
+        finish(kv_cols),
         total[:, :q_cols],
         total[:, q_cols : q_cols + kv_cols],
         total[:, q_cols + kv_cols : q_cols + 2 * kv_cols],

time: 115 us -> 109 us (0.948)
  waiting for transfers between devices: 30.5 us -> 26.1 us
  local copies, waits for them, and re-layouts: 6.48 us -> 3.43 us
  starting transfers between devices: 49.7 us -> 51.8 us
  Pallas kernels: 20.4 us -> 19.1 us
    ppermute x0 -> x2, starting transfers between devices: none -> 16.6 us  [z_swap(): lax.ppermute(x, 'head', [(i, i ^ (2, 6)[(i + turn) % 2]) for i in range(c...]
    ppermute x4 -> x2, starting transfers between devices: 16.6 us -> 3.84 us  [swap(): return lax.ppermute(x, 'head', [(i, i ^ bit) for i in range(count)])]
    ppermute x4 -> x2, waiting for transfers between devices: 9.23 us -> 1.32 us  [swap(): return lax.ppermute(x, 'head', [(i, i ^ bit) for i in range(count)])]
    ppermute x0 -> x2, waiting for transfers between devices: none -> 2.93 us  [z_swap(): lax.ppermute(x, 'head', [(i, i ^ (2, 6)[(i + turn) % 2]) for i in range(c...]
    ppermute x2, starting transfers between devices: 8.9 us -> 6.62 us  [pair_swap(): return lax.ppermute(x, 'seq', [(i, i ^ 1) for i in range(count)])]
    ppermute x2, waiting for transfers between devices: 0.01 us -> 2.13 us  [pair_swap(): return lax.ppermute(x, 'seq', [(i, i ^ 1) for i in range(count)])]
    convert_element_type x5 -> x6, other arithmetic: 1.29 us -> 3.24 us  [the longest x1 2.32 us: finish(): (own[:, cols] + jnp.where(odd, 0.0, near[:, cols]) + far[:, cols].astype(...]
    reshape x1 -> x0, local copies, waits for them, and re-layouts: 1.88 us -> none  [per_device(): sketches.reshape(shards, HD // shards, 12 * HD)]
  transfers between devices with their start and end apart: 11 -> 11, of which waited for: 7 -> 7; matrix products, arithmetic and copies ran while one was open for 7% -> 3% of each run, Pallas kernels for 0% -> 0%
where the time goes in v5:
time: 109 us; the launch traced here: 108 us
  starting transfers between devices  51.8 us (48%)
  waiting for transfers between devices  26.1 us (24%)
  Pallas kernels  19.1 us (18%)
  other arithmetic  5.66 us (5%)
  local copies, waits for them, and re-layouts  3.43 us (3%)
  matrix products  1.49 us (1%)
    pallas_call x1, Pallas kernels, attention(): pl.pallas_call(attention_kernel, in_specs=[pl.BlockSpec(memory_space=pltp...  19.1 us
    ppermute x2, starting transfers between devices, z_swap(): lax.ppermute(x, 'head', [(i, i ^ (2, 6)[(i + turn) % 2]) for i in range(c...  16.6 us
    ppermute x4, starting transfers between devices, shift(): return lax.ppermute(x, 'seq', pairs)  13.8 us
    ppermute x4, waiting for transfers between devices, shift(): return lax.ppermute(x, 'seq', pairs)  12.9 us
    all_to_all x1, starting transfers between devices, per_device(): pieces = lax.all_to_all(sketches, 'seq', 0, 0, tiled=True)  10.9 us
    all_to_all x1, waiting for transfers between devices, per_device(): pieces = lax.all_to_all(sketches, 'seq', 0, 0, tiled=True)  6.73 us
    ppermute x2, starting transfers between devices, pair_swap(): return lax.ppermute(x, 'seq', [(i, i ^ 1) for i in range(count)])  6.62 us
    ppermute x2, starting transfers between devices, swap(): return lax.ppermute(x, 'head', [(i, i ^ bit) for i in range(count)])  3.84 us
  transfers between devices with their start and end apart: 11, of which 7 were waited for; matrix products, arithmetic and copies ran while one was open for 3% of the time, Pallas kernels for 0%

profile of v5, /device:TPU:30, one launch (start us, length us, event | category | flops | bytes accessed | tf_op | source)
XLA Modules:
  0.0 108.5 jit_solution(17306210711305282385)
XLA Ops:
  0.7 1.2 %pad_maximum_fusion = bf16[512,512]{1,0:T(8,128)(2,1)S(1)} fusion(bf16[512,256]{1,0:T(8,128)(2,1)} %v0_hbm.1, bf16[512,256]{1,0:T(8,128)(2,1)} %k0_hbm.1), kind=kLoop, calls=%fused_computation.14 | loop fusion | flops 1048576 | bytes 1048576 | tf_op jit(solution)/shard_map/concatenate | solution.py:324
  3.0 1.1 fusion.8
  4.1 1.9 %collective-permute-start.3 = (bf16[512,128]{1,0:T(8,128)(2,1)S(1)}, bf16[512,128]{1,0:T(8,128)(2,1)S(1)}, u32[]{:S(2)}, u32[]{:S(2)}) collective-permute-start(bf16[512,128]{1,0:T(8,128)(2,1)S(1)} %select_convert_fusion), channel_id=1, source_target_pairs={{0,1},{1,0},{2,3},{3,2},{4,5},{5,4},{6,7},{7,6},{8,9},{9,8},{10,11... | collective-permute-start | bytes 393224 | tf_op jit(solution)/shard_map/while/body/ppermute | solution.py:304
  6.0 4.6 %collective-permute-start.1 = (bf16[512,512]{1,0:T(8,128)(2,1)S(1)}, bf16[512,512]{1,0:T(8,128)(2,1)S(1)}, u32[]{:S(2)}, u32[]{:S(2)}) collective-permute-start(bf16[512,512]{1,0:T(8,128)(2,1)S(1)} %pad_maximum_fusion), channel_id=1, source_target_pairs={{0,16},{8,24},{16,32},{24,40},{32,48},{40,56},{48,64},{56,72},{64,... | collective-permute-start | bytes 1572872 | tf_op jit(solution)/shard_map/ppermute | solution.py:299
  10.6 9.8 %while.12 = (s32[]{:T(128)}, bf16[512,128]{1,0:T(8,128)(2,1)}, s32[]{:T(128)}, bf16[512,128]{1,0:T(8,128)(2,1)S(1)}, f32[512,128]{1,0:T(8,128)S(1)}, /*index=5*/s32[]{:T(128)}) while((s32[]{:T(128)}, bf16[512,128]{1,0:T(8,128)(2,1)}, s32[]{:T(128)}, bf16[512,128]{1,0:T(8,128)(2,1)S(1)}, f32[512,128]{1,0:T(8,128)S(1)}, ...), condition=%wide.region_1.2_spmd, body=%wide.region_0.1_spmd.sunk | while | flops 524290 | bytes 1704045 | solution.py:318
  10.7 6.1 %collective-permute-start = (bf16[512,128]{1,0:T(8,128)(2,1)S(1)}, bf16[512,128]{1,0:T(8,128)(2,1)S(1)}, u32[]{:S(2)}, u32[]{:S(2)}) collective-permute-start(bf16[512,128]{1,0:T(8,128)(2,1)S(1)} %fusion.17), channel_id=1, source_target_pairs={{0,2},{1,7},{2,0},{3,5},{4,6},{5,3},{6,4},{7,1},{8,10},{9,15},{10,... | collective-permute-start | bytes 393224 | tf_op jit(solution)/shard_map/while/body/ppermute | solution.py:309
  16.8 2.9 %collective-permute-done = bf16[512,128]{1,0:T(8,128)(2,1)S(1)} collective-permute-done((bf16[512,128]{1,0:T(8,128)(2,1)S(1)}, bf16[512,128]{1,0:T(8,128)(2,1)S(1)}, u32[]{:S(2)}, u32[]{:S(2)}) %collective-permute-start) | collective-permute-done | bytes 131104 | tf_op jit(solution)/shard_map/while/body/ppermute | solution.py:309
  19.7 0.7 add_convert_fusion.3
  20.4 10.5 %collective-permute-start.4 = (bf16[512,128]{1,0:T(8,128)(2,1)}, bf16[512,128]{1,0:T(8,128)(2,1)S(1)}, u32[]{:S(2)}, u32[]{:S(2)}) collective-permute-start(bf16[512,128]{1,0:T(8,128)(2,1)} %get-tuple-element.79), channel_id=1, source_target_pairs={{0,6},{1,3},{2,4},{3,1},{4,2},{5,7},{6,0},{7,5},{8,14},{9,11},{10,... | collective-permute-start | bytes 393224 | tf_op jit(solution)/shard_map/ppermute | solution.py:309
  31.0 0.7 copy-done.3
  31.8 4.0 %collective-permute-start.2 = (bf16[512,512]{1,0:T(8,128)(2,1)S(1)}, bf16[512,512]{1,0:T(8,128)(2,1)S(1)}, u32[]{:S(2)}, u32[]{:S(2)}) collective-permute-start(bf16[512,512]{1,0:T(8,128)(2,1)S(1)} %broadcast_select_fusion), channel_id=1, source_target_pairs={{0,8},{8,0},{16,24},{24,16},{32,40},{40,32},{48,56},{56,48},{64,72... | collective-permute-start | bytes 1572872 | tf_op jit(solution)/shard_map/ppermute | solution.py:314
  35.9 1.9 %collective-permute-start.5 = (bf16[512,128]{1,0:T(8,128)(2,1)S(1)}, bf16[512,128]{1,0:T(8,128)(2,1)S(1)}, u32[]{:S(2)}, u32[]{:S(2)}) collective-permute-start(bf16[512,128]{1,0:T(8,128)(2,1)S(1)} %add_convert_fusion.1), channel_id=1, source_target_pairs={{0,1},{1,0},{2,3},{3,2},{4,5},{5,4},{6,7},{7,6},{8,9},{9,8},{10,11... | collective-permute-start | bytes 393224 | tf_op jit(solution)/shard_map/ppermute | solution.py:304
  37.8 1.3 %collective-permute-done.5 = bf16[512,128]{1,0:T(8,128)(2,1)S(1)} collective-permute-done((bf16[512,128]{1,0:T(8,128)(2,1)S(1)}, bf16[512,128]{1,0:T(8,128)(2,1)S(1)}, u32[]{:S(2)}, u32[]{:S(2)}) %collective-permute-start.5) | collective-permute-done | bytes 131104 | tf_op jit(solution)/shard_map/ppermute | solution.py:304
  39.8 3.4 %collective-permute-start.7 = (bf16[512,128]{1,0:T(8,128)(2,1)S(1)}, bf16[512,128]{1,0:T(8,128)(2,1)S(1)}, u32[]{:S(2)}, u32[]{:S(2)}) collective-permute-start(bf16[512,128]{1,0:T(8,128)(2,1)S(1)} %get-tuple-element.100.x0_hbm), channel_id=1, source_target_pairs={{0,16},{8,24},{16,32},{24,40},{32,48},{40,56},{48,64},{56,72},{64,... | collective-permute-start | bytes 393224 | tf_op jit(solution)/shard_map/ppermute | solution.py:299
  43.2 3.3 %collective-permute-start.6 = (bf16[512,128]{1,0:T(8,128)(2,1)S(1)}, bf16[512,128]{1,0:T(8,128)(2,1)S(1)}, u32[]{:S(2)}, u32[]{:S(2)}) collective-permute-start(bf16[512,128]{1,0:T(8,128)(2,1)S(1)} %get-tuple-element.100.x0_hbm), channel_id=1, source_target_pairs={{0,8},{8,16},{16,24},{24,32},{32,40},{40,48},{48,56},{56,64},{64,7... | collective-permute-start | bytes 393224 | tf_op jit(solution)/shard_map/ppermute | solution.py:299
  47.2 4.0 %collective-permute-done.6.x1_hbm = bf16[512,128]{1,0:T(8,128)(2,1)S(1)} collective-permute-done((bf16[512,128]{1,0:T(8,128)(2,1)S(1)}, bf16[512,128]{1,0:T(8,128)(2,1)S(1)}, u32[]{:S(2)}, u32[]{:S(2)}) %collective-permute-start.6) | collective-permute-done | bytes 131104 | tf_op jit(solution)/shard_map/ppermute | solution.py:299
  52.1 19.1 %shard_map.189 = (bf16[512,512]{1,0:T(8,128)(2,1)}, f32[512,512]{1,0:T(8,128)}, bf16[512,512]{1,0:T(8,128)(2,1)}, bf16[512,512]{1,0:T(8,128)(2,1)}, bf16[64,2,1536]{2,1,0:T(2,128)(2,1)}) custom-call(s32[1]{0:T(128)} %bitcast.shard_ref, bf16[512,512]{1,0:T(8,128)(2,1)} %q_hbm.1, bf16[512,512]{1,0:T(8,128)(2,1)} %do_hbm.1, bf16[512,256]{1,0:T(8,128)(2,1)} %k0_hbm.1, ...), custom_call_target="tpu_custom_call" | custom-call | flops 4831838208 | bytes 6291456 | tf_op jit(solution)/shard_map/pallas_call | solution.py:256
  71.2 2.6 %collective-permute-start.8 = (bf16[512,512]{1,0:T(8,128)(2,1)}, bf16[512,512]{1,0:T(8,128)(2,1)S(1)}, u32[]{:S(2)}, u32[]{:S(2)}) collective-permute-start(bf16[512,512]{1,0:T(8,128)(2,1)} %get-tuple-element.82), channel_id=1, source_target_pairs={{0,8},{8,0},{16,24},{24,16},{32,40},{40,32},{48,56},{56,48},{64,72... | collective-permute-start | bytes 1572872 | tf_op jit(solution)/shard_map/ppermute | solution.py:314
  73.8 10.9 %all-to-all-start = ((bf16[64,2,1536]{2,1,0:T(2,128)(2,1)}), bf16[64,2,1536]{2,1,0:T(2,128)(2,1)S(1)}, u32[]{:S(2)}, u32[]{:S(2)}) async-start(bf16[64,2,1536]{2,1,0:T(2,128)(2,1)} %get-tuple-element.84), calls=%async_computation | async-start | bytes 786432 | tf_op jit(solution)/shard_map/all_to_all | solution.py:354
  84.8 2.1 %collective-permute-done.8 = bf16[512,512]{1,0:T(8,128)(2,1)S(1)} collective-permute-done((bf16[512,512]{1,0:T(8,128)(2,1)}, bf16[512,512]{1,0:T(8,128)(2,1)S(1)}, u32[]{:S(2)}, u32[]{:S(2)}) %collective-permute-start.8) | collective-permute-done | bytes 524320 | tf_op jit(solution)/shard_map/ppermute | solution.py:314
  87.1 2.4 %collective-permute-start.9 = (bf16[512,512]{1,0:T(8,128)(2,1)S(1)}, bf16[512,512]{1,0:T(8,128)(2,1)}, u32[]{:S(2)}, u32[]{:S(2)}) collective-permute-start(bf16[512,512]{1,0:T(8,128)(2,1)S(1)} %fusion.1), channel_id=1, source_target_pairs={{16,0},{24,8},{32,16},{40,24},{48,32},{56,40},{64,48},{72,56},{80,... | collective-permute-start | bytes 1572872 | tf_op jit(solution)/shard_map/ppermute | solution.py:299
  89.7 6.7 %all-to-all-done = bf16[64,2,1536]{2,1,0:T(2,128)(2,1)S(1)} async-done(((bf16[64,2,1536]{2,1,0:T(2,128)(2,1)}), bf16[64,2,1536]{2,1,0:T(2,128)(2,1)S(1)}, u32[]{:S(2)}, u32[]{:S(2)}) %all-to-all-start) | async-done | bytes 393248 | tf_op jit(solution)/shard_map/all_to_all | solution.py:354
  97.9 8.2 %collective-permute-done.9 = bf16[512,512]{1,0:T(8,128)(2,1)} collective-permute-done((bf16[512,512]{1,0:T(8,128)(2,1)S(1)}, bf16[512,512]{1,0:T(8,128)(2,1)}, u32[]{:S(2)}, u32[]{:S(2)}) %collective-permute-start.9) | collective-permute-done | bytes 524320 | tf_op jit(solution)/shard_map/ppermute | solution.py:299
  106.1 2.3 %fusion.4 = (bf16[512,256]{1,0:T(8,128)(2,1)}, bf16[512,256]{1,0:T(8,128)(2,1)}) fusion(f32[512,512]{1,0:T(8,128)S(1)} %convert_element_type.64, f32[512,512]{1,0:T(8,128)} %get-tuple-element.81, bf16[512,512]{1,0:T(8,128)(2,1)} %collective-permute-done.9, pred[]{:T(512)S(6)} %eq.9), kind=kLoop, calls=%fused_computation.9 | loop fusion | flops 1310720 | bytes 3145729 | tf_op jit(solution)/shard_map/convert_element_type | solution.py:360
  (37 shorter events, 5.3 us)
Async XLA Ops:
  0.6 1.8 %copy-start = (bf16[512,672]{0,1:T(8,128)(2,1)S(1)}, bf16[512,672]{0,1:T(8,128)(2,1)}, u32[]{:S(2)}) copy-start(bf16[512,672]{0,1:T(8,128)(2,1)} %param.16) | copy-start | bytes 2064388
  0.6 1.3 %copy-start.1 = (bf16[512,672]{0,1:T(8,128)(2,1)S(1)}, bf16[512,672]{0,1:T(8,128)(2,1)}, u32[]{:S(2)}) copy-start(bf16[512,672]{0,1:T(8,128)(2,1)} %param.18) | copy-start | bytes 2064388
  0.7 1.3 %copy-start.5 = (bf16[672,128]{1,0:T(8,128)(2,1)S(1)}, bf16[672,128]{1,0:T(8,128)(2,1)}, u32[]{:S(2)}) copy-start(bf16[672,128]{1,0:T(8,128)(2,1)} %param.19) | copy-start | bytes 516100
  2.0 1.0 copy-start.6
  4.1 6.6 %collective-permute-start.3 = (bf16[512,128]{1,0:T(8,128)(2,1)S(1)}, bf16[512,128]{1,0:T(8,128)(2,1)S(1)}, u32[]{:S(2)}, u32[]{:S(2)}) collective-permute-start(bf16[512,128]{1,0:T(8,128)(2,1)S(1)} %select_convert_fusion), channel_id=1, source_target_pairs={{0,1},{1,0},{2,3},{3,2},{4,5},{5,4},{6,7},{7,6},{8,9},{9,8},{10,11... | collective-permute-start | bytes 393224 | tf_op jit(solution)/shard_map/while/body/ppermute | solution.py:304
  6.0 25.0 %collective-permute-start.1 = (bf16[512,512]{1,0:T(8,128)(2,1)S(1)}, bf16[512,512]{1,0:T(8,128)(2,1)S(1)}, u32[]{:S(2)}, u32[]{:S(2)}) collective-permute-start(bf16[512,512]{1,0:T(8,128)(2,1)S(1)} %pad_maximum_fusion), channel_id=1, source_target_pairs={{0,16},{8,24},{16,32},{24,40},{32,48},{40,56},{48,64},{56,72},{64,... | collective-permute-start | bytes 1572872 | tf_op jit(solution)/shard_map/ppermute | solution.py:299
  10.7 9.0 %collective-permute-start = (bf16[512,128]{1,0:T(8,128)(2,1)S(1)}, bf16[512,128]{1,0:T(8,128)(2,1)S(1)}, u32[]{:S(2)}, u32[]{:S(2)}) collective-permute-start(bf16[512,128]{1,0:T(8,128)(2,1)S(1)} %fusion.17), channel_id=1, source_target_pairs={{0,2},{1,7},{2,0},{3,5},{4,6},{5,3},{6,4},{7,1},{8,10},{9,15},{10,... | collective-permute-start | bytes 393224 | tf_op jit(solution)/shard_map/while/body/ppermute | solution.py:309
  20.4 15.4 %copy-start.2 = (bf16[512,128]{1,0:T(8,128)(2,1)S(1)}, bf16[512,128]{1,0:T(8,128)(2,1)}, u32[]{:S(2)}) copy-start(bf16[512,128]{1,0:T(8,128)(2,1)} %get-tuple-element.79) | copy-start | bytes 393220
  20.4 15.4 %collective-permute-start.4 = (bf16[512,128]{1,0:T(8,128)(2,1)}, bf16[512,128]{1,0:T(8,128)(2,1)S(1)}, u32[]{:S(2)}, u32[]{:S(2)}) collective-permute-start(bf16[512,128]{1,0:T(8,128)(2,1)} %get-tuple-element.79), channel_id=1, source_target_pairs={{0,6},{1,3},{2,4},{3,1},{4,2},{5,7},{6,0},{7,5},{8,14},{9,11},{10,... | collective-permute-start | bytes 393224 | tf_op jit(solution)/shard_map/ppermute | solution.py:309
  31.0 0.8 copy-start.3
  31.8 19.5 %collective-permute-start.2 = (bf16[512,512]{1,0:T(8,128)(2,1)S(1)}, bf16[512,512]{1,0:T(8,128)(2,1)S(1)}, u32[]{:S(2)}, u32[]{:S(2)}) collective-permute-start(bf16[512,512]{1,0:T(8,128)(2,1)S(1)} %broadcast_select_fusion), channel_id=1, source_target_pairs={{0,8},{8,0},{16,24},{24,16},{32,40},{40,32},{48,56},{56,48},{64,72... | collective-permute-start | bytes 1572872 | tf_op jit(solution)/shard_map/ppermute | solution.py:314
  35.9 3.2 %collective-permute-start.5 = (bf16[512,128]{1,0:T(8,128)(2,1)S(1)}, bf16[512,128]{1,0:T(8,128)(2,1)S(1)}, u32[]{:S(2)}, u32[]{:S(2)}) collective-permute-start(bf16[512,128]{1,0:T(8,128)(2,1)S(1)} %add_convert_fusion.1), channel_id=1, source_target_pairs={{0,1},{1,0},{2,3},{3,2},{4,5},{5,4},{6,7},{7,6},{8,9},{9,8},{10,11... | collective-permute-start | bytes 393224 | tf_op jit(solution)/shard_map/ppermute | solution.py:304
  39.8 11.5 %copy-start.7 = (bf16[512,128]{1,0:T(8,128)(2,1)}, bf16[512,128]{1,0:T(8,128)(2,1)S(1)}, u32[]{:S(2)}) copy-start(bf16[512,128]{1,0:T(8,128)(2,1)S(1)} %get-tuple-element.100.x0_hbm) | copy-start | bytes 393220
  39.8 7.4 %collective-permute-start.7 = (bf16[512,128]{1,0:T(8,128)(2,1)S(1)}, bf16[512,128]{1,0:T(8,128)(2,1)S(1)}, u32[]{:S(2)}, u32[]{:S(2)}) collective-permute-start(bf16[512,128]{1,0:T(8,128)(2,1)S(1)} %get-tuple-element.100.x0_hbm), channel_id=1, source_target_pairs={{0,16},{8,24},{16,32},{24,40},{32,48},{40,56},{48,64},{56,72},{64,... | collective-permute-start | bytes 393224 | tf_op jit(solution)/shard_map/ppermute | solution.py:299
  43.2 8.1 %collective-permute-start.6 = (bf16[512,128]{1,0:T(8,128)(2,1)S(1)}, bf16[512,128]{1,0:T(8,128)(2,1)S(1)}, u32[]{:S(2)}, u32[]{:S(2)}) collective-permute-start(bf16[512,128]{1,0:T(8,128)(2,1)S(1)} %get-tuple-element.100.x0_hbm), channel_id=1, source_target_pairs={{0,8},{8,16},{16,24},{24,32},{32,40},{40,48},{48,56},{56,64},{64,7... | collective-permute-start | bytes 393224 | tf_op jit(solution)/shard_map/ppermute | solution.py:299
  47.2 4.0 %copy-start.9 = (bf16[512,128]{1,0:T(8,128)(2,1)}, bf16[512,128]{1,0:T(8,128)(2,1)S(1)}, u32[]{:S(2)}) copy-start(bf16[512,128]{1,0:T(8,128)(2,1)S(1)} %collective-permute-done.7.x2_hbm) | copy-start | bytes 393220
  51.2 0.7 copy-start.10
  51.3 0.8 copy-start.8
  71.2 15.7 %copy-start.4 = (bf16[512,512]{1,0:T(8,128)(2,1)S(1)}, bf16[512,512]{1,0:T(8,128)(2,1)}, u32[]{:S(2)}) copy-start(bf16[512,512]{1,0:T(8,128)(2,1)} %get-tuple-element.83) | copy-start | bytes 1572868
  71.2 15.7 %collective-permute-start.8 = (bf16[512,512]{1,0:T(8,128)(2,1)}, bf16[512,512]{1,0:T(8,128)(2,1)S(1)}, u32[]{:S(2)}, u32[]{:S(2)}) collective-permute-start(bf16[512,512]{1,0:T(8,128)(2,1)} %get-tuple-element.82), channel_id=1, source_target_pairs={{0,8},{8,0},{16,24},{24,16},{32,40},{40,32},{48,56},{56,48},{64,72... | collective-permute-start | bytes 1572872 | tf_op jit(solution)/shard_map/ppermute | solution.py:314
  73.8 22.5 %all-to-all-start = ((bf16[64,2,1536]{2,1,0:T(2,128)(2,1)}), bf16[64,2,1536]{2,1,0:T(2,128)(2,1)S(1)}, u32[]{:S(2)}, u32[]{:S(2)}) async-start(bf16[64,2,1536]{2,1,0:T(2,128)(2,1)} %get-tuple-element.84), calls=%async_computation | async-start | bytes 786432 | tf_op jit(solution)/shard_map/all_to_all | solution.py:354
  87.1 19.1 %collective-permute-start.9 = (bf16[512,512]{1,0:T(8,128)(2,1)S(1)}, bf16[512,512]{1,0:T(8,128)(2,1)}, u32[]{:S(2)}, u32[]{:S(2)}) collective-permute-start(bf16[512,512]{1,0:T(8,128)(2,1)S(1)} %fusion.1), channel_id=1, source_target_pairs={{16,0},{24,8},{32,16},{40,24},{48,32},{56,40},{64,48},{72,56},{80,... | collective-permute-start | bytes 1572872 | tf_op jit(solution)/shard_map/ppermute | solution.py:299

commit v6 on v5

--- a/solution.py
+++ b/solution.py
@@ -11,6 +11,7 @@
 TOK = 512
 QT = 256
 KB = 256
+GROUP = 64
 ATTN_VMEM = 60 << 20
 SPAN = 1536
 NBLK = 5
@@ -25,12 +26,9 @@
 def rope_tables(shards):
     freq = rope_base ** (-(np.arange(64, dtype=np.float64) * 2.0 / HD))
     freq = np.concatenate([freq, freq])[None, :]
-    base = ((np.arange(shards + 2) - 2) * TOK).astype(np.float64)[:, None] * freq
-    local = np.arange(TOK, dtype=np.float64)[:, None] * freq
-    pad = (-base.shape[0]) % 8
-    base = np.pad(base, ((0, pad), (0, 0)))
-    tables = [np.cos(base), np.sin(base), np.cos(local), np.sin(local)]
-    return [t.astype(np.float32) for t in tables]
+    starts = (np.arange(-2, shards + 6) * TOK, np.arange(TOK // GROUP) * GROUP, np.arange(GROUP))
+    angles = [at.astype(np.float64)[:, None] * freq for at in starts]
+    return [f(a).astype(np.float32) for a in angles for f in (np.cos, np.sin)]
 
 
 def lane_mean(x):
@@ -53,6 +51,10 @@
     return r * d_norm - raw * ((r * r * r) * lane_mean(raw * d_norm))
 
 
+def mult(a, n):
+    return a if isinstance(a, int) else pl.multiple_of(a, n)
+
+
 def mm(a, b):
     return lax.dot_general(a, b, (((1,), (0,)), ((), ())), preferred_element_type=F32)
 
@@ -61,43 +63,48 @@
     return lax.dot_general(a, b, (((1,), (1,)), ((), ())), preferred_element_type=F32)
 
 
-N_IN = 16
+N_IN = 18
 
 
 def attention_kernel(
     shard_ref, q_hbm, do_hbm, k0_hbm, v0_hbm, kv1_hbm, kv2_hbm, x0_hbm, x1_hbm, x2_hbm, y_hbm,
-    qg_hbm, kg_hbm, cb_hbm, sb_hbm, cl_hbm, sl_hbm,
+    qg_hbm, kg_hbm, cb_hbm, sb_hbm, cm_hbm, sm_hbm, cl_hbm, sl_hbm,
     qgrad_hbm, own_hbm, back1_hbm, back2_hbm, sk_hbm,
     q_ref, do_ref, k0_ref, v0_ref, kv1_ref, kv2_ref, x0_ref, x1_ref, x2_ref, y_ref,
-    qg_ref, kg_ref, cb_ref, sb_ref, cl_ref, sl_ref,
+    qg_ref, kg_ref, cb_ref, sb_ref, cm_ref, sm_ref, cl_ref, sl_ref,
     qgrad_ref, own_ref, back1_ref, back2_ref, sk_ref,
     kp, vx, r_k, cos, sin, e_sc, dp_sc, dkt, dvt, xt, yt, skq, sko, in_sems, out_sems,
 ):
-    sources = (cb_hbm, sb_hbm, cl_hbm, sl_hbm, qg_hbm, kg_hbm) + (k0_hbm, kv2_hbm, kv1_hbm, v0_hbm, q_hbm, do_hbm, x0_hbm, x1_hbm, x2_hbm, y_hbm)
-    targets = (cb_ref, sb_ref, cl_ref, sl_ref, qg_ref, kg_ref) + (k0_ref, kv2_ref, kv1_ref, v0_ref, q_ref, do_ref, x0_ref, x1_ref, x2_ref, y_ref)
+    sources = (cb_hbm, sb_hbm, cm_hbm, sm_hbm, cl_hbm, sl_hbm, qg_hbm, kg_hbm) + (k0_hbm, kv2_hbm, kv1_hbm, v0_hbm, q_hbm, do_hbm, x0_hbm, x1_hbm, x2_hbm, y_hbm)
+    targets = (cb_ref, sb_ref, cm_ref, sm_ref, cl_ref, sl_ref, qg_ref, kg_ref) + (k0_ref, kv2_ref, kv1_ref, v0_ref, q_ref, do_ref, x0_ref, x1_ref, x2_ref, y_ref)
     loads = [pltpu.make_async_copy(a, b, in_sems.at[n]) for n, (a, b) in enumerate(zip(sources, targets))]
     for load in loads:
         load.start()
     shard = shard_ref[0]
-    for load in loads[:6]:
+    for load in loads[:8]:
         load.wait()
     lane = lax.broadcasted_iota(jnp.int32, (1, HD), 1)
     sign = jnp.where(lane < HD // 2, -1.0, 1.0)
     for part in range(3):
         cb = cb_ref[pl.ds(shard + part, 1), :]
         sb = sb_ref[pl.ds(shard + part, 1), :]
-        rows = slice(part * TOK, (part + 1) * TOK)
-        cos[rows, :] = cb * cl_ref[...] - sb * sl_ref[...]
-        sin[rows, :] = (sb * cl_ref[...] + cb * sl_ref[...]) * sign
-    for load in loads[6:10]:
+        for group in range(TOK // GROUP):
+            cm = cm_ref[group : group + 1, :]
+            sm = sm_ref[group : group + 1, :]
+            c = cb * cm - sb * sm
+            s = sb * cm + cb * sm
+            rows = slice(part * TOK + group * GROUP, part * TOK + (group + 1) * GROUP)
+            cos[rows, :] = c * cl_ref[...] - s * sl_ref[...]
+            sin[rows, :] = (s * cl_ref[...] + c * sl_ref[...]) * sign
+    for load in loads[8:12]:
         load.wait()
 
     def wait_queries():
-        for load in loads[10:12]:
+        for load in loads[12:14]:
             load.wait()
 
     def wait_sketches():
-        for load in loads[12:]:
+        for load in loads[14:]:
             load.wait()
         for part, x_ref in enumerate((x2_ref, x1_ref, x0_ref)):
             xt[:, part * TOK : (part + 1) * TOK] = x_ref[...].T
@@ -110,23 +117,19 @@
     )
 
     def stores(head):
-        lanes = pl.ds(pl.multiple_of(head * 2 * HD, 2 * HD), 2 * HD)
+        lanes = pl.ds(mult(head * 2 * HD, 2 * HD), 2 * HD)
         out = [(qgrad_ref.at[:, lanes], qgrad_hbm.at[:, lanes])]
         for kind in range(2):
-            lanes = pl.ds(pl.multiple_of(head * HD + kind * 2 * HD, HD), HD)
+            lanes = pl.ds(mult(head * HD + kind * 2 * HD, HD), HD)
             for a, b in ((own_ref, own_hbm), (back1_ref, back1_hbm), (back2_ref, back2_hbm)):
                 out.append((a.at[:, lanes], b.at[:, lanes]))
         return [pltpu.make_async_copy(a, b, out_sems.at[head, n]) for n, (a, b) in enumerate(out)]
 
-    @pl.loop(0, 4)
-    def _(step):
-        head = step // 2
-        attention_step(head, step % 2, wait_queries, wait_sketches, *refs)
-
-        @pl.when(step % 2 == 1)
-        def _():
-            for store in stores(head):
-                store.start()
+    for head in range(2):
+        for tile in range(2):
+            attention_step(head, tile, wait_queries, wait_sketches, *refs)
+        for store in stores(head):
+            store.start()
 
     sketch_store = pltpu.make_async_copy(sk_ref, sk_hbm, out_sems.at[0, 7])
     sketch_store.start()
@@ -141,13 +144,12 @@
     qgrad_ref, own_ref, back1_ref, back2_ref, sk_ref,
     kp, vx, r_k, cos, sin, e_sc, dp_sc, dkt, dvt, xt, yt, skq, sko,
 ):
-    k_lanes = pl.ds(pl.multiple_of(head * HD, HD), HD)
-    v_lanes = pl.ds(pl.multiple_of(head * HD + 2 * HD, HD), HD)
+    k_lanes = pl.ds(mult(head * HD, HD), HD)
+    v_lanes = pl.ds(mult(head * HD + 2 * HD, HD), HD)
     k_parts = (kv2_ref.at[:, k_lanes], kv1_ref.at[:, k_lanes], k0_ref.at[:, k_lanes])
     v_parts = (kv2_ref.at[:, v_lanes], kv1_ref.at[:, v_lanes], v0_ref.at[:, k_lanes])
 
-    @pl.when(tile == 0)
-    def _():
+    if tile == 0:
         skq[...] = jnp.zeros_like(skq)
         sko[...] = jnp.zeros_like(sko)
         for part, (k_ref, v_ref) in enumerate(zip(k_parts, v_parts)):
@@ -161,10 +163,11 @@
         dkt[...] = jnp.zeros_like(dkt)
         dvt[...] = jnp.zeros_like(dvt)
 
-    pl.when((head == 0) & (tile == 0))(wait_queries)
-    tile_rows = pl.ds(pl.multiple_of(tile * QT, QT), QT)
-    q_rows = pl.ds(pl.multiple_of(2 * TOK + tile * QT, QT), QT)
-    q_lanes = [pl.ds(pl.multiple_of(head * 2 * HD + g * HD, HD), HD) for g in range(2)]
+    if head == 0 and tile == 0:
+        wait_queries()
+    tile_rows = pl.ds(mult(tile * QT, QT), QT)
+    q_rows = pl.ds(mult(2 * TOK + tile * QT, QT), QT)
+    q_lanes = [pl.ds(mult(head * 2 * HD + g * HD, HD), HD) for g in range(2)]
     cos_q = cos[q_rows, :]
     sin_q = sin[q_rows, :]
     q_parts = []
@@ -185,7 +188,7 @@
     l_acc = jnp.zeros((2 * QT, HD), F32)
     u_acc = jnp.zeros((2 * QT, HD), F32)
     for b in range(NBLK):
-        at = pl.ds(pl.multiple_of(tile * QT + b * KB, KB), KB)
+        at = pl.ds(mult(tile * QT + b * KB, KB), KB)
         cols = slice(b * KB, (b + 1) * KB)
         s = mm_t(q_low, kp[at, :])
         e = jnp.exp2(s * (score_scale * LOG2E))
@@ -208,7 +211,7 @@
     out = jnp.zeros((2 * QT, HD), F32)
     dq = jnp.zeros((2 * QT, HD), F32)
     for b in range(NBLK):
-        at = pl.ds(pl.multiple_of(tile * QT + b * KB, KB), KB)
+        at = pl.ds(mult(tile * QT + b * KB, KB), KB)
         cols = slice(b * KB, (b + 1) * KB)
         p = e_sc[:, cols] * inv
         ds = (p * (dp_sc[:, cols] - delta)).astype(BF16)
@@ -217,7 +220,8 @@
         dq = dq + mm(ds, kp[at, :])
         dvt[:, at] += mm(do_t, p)
         dkt[:, at] += mm(q_t, ds)
-    pl.when((head == 0) & (tile == 0))(wait_sketches)
+    if head == 0 and tile == 0:
+        wait_sketches()
     x_tile = xt[:, q_rows]
     y_tile = yt[:, tile_rows]
     for g in range(2):
@@ -229,8 +233,7 @@
         skq[:, lanes] += mm(x_tile, q_grad)
         sko[:, lanes] += mm(y_tile, out[rows].astype(BF16))
 
-    @pl.when(tile == 1)
-    def _():
+    if tile == 1:
         sk_k = jnp.zeros((HD, HD), F32)
         sk_v = jnp.zeros((HD, HD), F32)
         for part, k_ref in enumerate(k_parts):
@@ -245,10 +248,10 @@
             target = (back2_ref, back1_ref, own_ref)[part]
             target[:, k_lanes] = dk.astype(target.dtype)
             target[:, v_lanes] = dv.astype(target.dtype)
-        sk_ref[:, :, pl.ds(pl.multiple_of(head * 2 * HD, 2 * HD), 2 * HD)] = skq[...].astype(BF16).reshape(64, 2, -1)
-        sk_ref[:, :, pl.ds(pl.multiple_of(head * HD + 4 * HD, HD), HD)] = sk_k.astype(BF16).reshape(64, 2, -1)
-        sk_ref[:, :, pl.ds(pl.multiple_of(head * HD + 6 * HD, HD), HD)] = sk_v.astype(BF16).reshape(64, 2, -1)
-        sk_ref[:, :, pl.ds(pl.multiple_of(head * 2 * HD + 8 * HD, 2 * HD), 2 * HD)] = sko[...].astype(BF16).reshape(64, 2, -1)
+        sk_ref[:, :, pl.ds(mult(head * 2 * HD, 2 * HD), 2 * HD)] = skq[...].astype(BF16).reshape(64, 2, -1)
+        sk_ref[:, :, pl.ds(mult(head * HD + 4 * HD, HD), HD)] = sk_k.astype(BF16).reshape(64, 2, -1)
+        sk_ref[:, :, pl.ds(mult(head * HD + 6 * HD, HD), HD)] = sk_v.astype(BF16).reshape(64, 2, -1)
+        sk_ref[:, :, pl.ds(mult(head * 2 * HD + 8 * HD, 2 * HD), 2 * HD)] = sko[...].astype(BF16).reshape(64, 2, -1)
 
 
 def attention(shard, q_raw, d_out, k_raw, values, kv1, kv2, sketches, q_gain, k_gain, tables):
@@ -259,14 +262,14 @@
         out_specs=[pl.BlockSpec(memory_space=pl.ANY)] * 5,
         out_shape=[
             jax.ShapeDtypeStruct((TOK, 4 * HD), BF16),
-            jax.ShapeDtypeStruct((TOK, 4 * HD), F32),
+            jax.ShapeDtypeStruct((TOK, 4 * HD), BF16),
             jax.ShapeDtypeStruct((TOK, 4 * HD), BF16),
             jax.ShapeDtypeStruct((TOK, 4 * HD), BF16),
             jax.ShapeDtypeStruct((64, 2, 12 * HD), BF16),
         ],
         scratch_shapes=[pltpu.VMEM(a.shape, a.dtype) for a in arrays[:N_IN]] + [
             pltpu.VMEM((TOK, 4 * HD), BF16),
-            pltpu.VMEM((TOK, 4 * HD), F32),
+            pltpu.VMEM((TOK, 4 * HD), BF16),
             pltpu.VMEM((TOK, 4 * HD), BF16),
             pltpu.VMEM((TOK, 4 * HD), BF16),
             pltpu.VMEM((64, 2, 12 * HD), BF16),
@@ -315,7 +318,7 @@
 
 
 def one_turn(step, start):
-    return lax.fori_loop(0, lax.optimization_barrier(jnp.int32(1)), lambda i, carry: step(), start)
+    return lax.fori_loop(0, lax.optimization_barrier(jnp.int32(1)), lambda i, carry: step(carry), start)
 
 
 def per_device(
@@ -329,16 +332,18 @@
     partial_x = jnp.dot(layer_input, omega_in, preferred_element_type=F32)
     partial_y = jnp.dot(upstream, omega_out, preferred_element_type=F32)
 
-    keep = jnp.where(first, partial_x, partial_y)
-    give = jnp.where(first, partial_y, partial_x).astype(BF16)
 
     def sum_near():
-        total = keep + swap(give, 1).astype(F32)
+        got = swap(jnp.where(first, partial_y, partial_x).astype(BF16), 1)
+        total = jnp.where(first, partial_x, partial_y) + got.astype(F32)
         return (total + z_swap(total.astype(BF16), 0).astype(F32)).astype(BF16)
 
-    half = one_turn(sum_near, keep.astype(BF16))
+    def sum_far(half):
+        return (half.astype(F32) + z_swap(half, 1).astype(F32)).astype(BF16)
+
+    half = one_turn(lambda carry: sum_near(), partial_x.astype(BF16))
     kv1 = pair_swap(jnp.where(odd, kv2, kv))
-    mine = (half.astype(F32) + z_swap(half, 1).astype(F32)).astype(BF16)
+    mine = one_turn(sum_far, half)
     other = swap(mine, 1)
     x0, y0 = jnp.where(first, mine, other), jnp.where(first, other, mine)
     x1 = shift(x0, 1)
@@ -355,14 +360,11 @@
     total = jnp.sum(pieces.astype(F32), axis=0)
     q_cols, kv_cols = 4 * HD, 2 * HD
 
-    def finish(begin):
-        cols = slice(begin, begin + kv_cols)
-        return (own[:, cols] + jnp.where(odd, 0.0, near[:, cols]) + far[:, cols].astype(F32)).astype(BF16)
-
+    kv_grad = (own.astype(F32) + jnp.where(odd, 0.0, near) + far.astype(F32)).astype(BF16)
     return (
         query_grad,
-        finish(0),
-        finish(kv_cols),
+        kv_grad[:, :kv_cols],
+        kv_grad[:, kv_cols:],
         total[:, :q_cols],
         total[:, q_cols : q_cols + kv_cols],
         total[:, q_cols + kv_cols : q_cols + 2 * kv_cols],

time: 109 us -> 127 us (1.17)
  waiting for transfers between devices: 26.1 us -> 42.5 us
  starting transfers between devices: 51.8 us -> 55.4 us
  Pallas kernels: 19.1 us -> 16.2 us
    ppermute x4, waiting for transfers between devices: 12.9 us -> 23.8 us  [shift(): return lax.ppermute(x, 'seq', pairs)]
    ppermute x2, waiting for transfers between devices: 2.93 us -> 6.18 us  [z_swap(): lax.ppermute(x, 'head', [(i, i ^ (2, 6)[(i + turn) % 2]) for i in range(c...]
    pallas_call x1, Pallas kernels: 19.1 us -> 16.2 us  [attention(): pl.pallas_call(attention_kernel, in_specs=[pl.BlockSpec(memory_space=pltp...]
    ppermute x4, starting transfers between devices: 13.8 us -> 16.2 us  [shift(): return lax.ppermute(x, 'seq', pairs)]
    ppermute x2, waiting for transfers between devices: 2.13 us -> 4.23 us  [pair_swap(): return lax.ppermute(x, 'seq', [(i, i ^ 1) for i in range(count)])]
  transfers between devices with their start and end apart: 11 -> 11, of which waited for: 7 -> 10; matrix products, arithmetic and copies ran while one was open for 3% -> 6% of each run, Pallas kernels for 0% -> 0%
where the time goes in v6:
time: 127 us; the launch traced here: 126 us
  starting transfers between devices  55.4 us (44%)
  waiting for transfers between devices  42.5 us (33%)
  Pallas kernels  16.2 us (13%)
  other arithmetic  5.91 us (5%)
  local copies, waits for them, and re-layouts  4.13 us (3%)
  matrix products  1.49 us (1%)
    ppermute x4, waiting for transfers between devices, shift(): return lax.ppermute(x, 'seq', pairs)  23.8 us
    ppermute x2, starting transfers between devices, z_swap(): lax.ppermute(x, 'head', [(i, i ^ (2, 6)[(i + turn) % 2]) for i in range(c...  17.8 us
    ppermute x4, starting transfers between devices, shift(): return lax.ppermute(x, 'seq', pairs)  16.2 us
    pallas_call x1, Pallas kernels, attention(): pl.pallas_call(attention_kernel, in_specs=[pl.BlockSpec(memory_space=pltp...  16.2 us
    all_to_all x1, starting transfers between devices, per_device(): pieces = lax.all_to_all(sketches, 'seq', 0, 0, tiled=True)  10.3 us
    ppermute x2, starting transfers between devices, pair_swap(): return lax.ppermute(x, 'seq', [(i, i ^ 1) for i in range(count)])  6.32 us
    ppermute x2, waiting for transfers between devices, z_swap(): lax.ppermute(x, 'head', [(i, i ^ (2, 6)[(i + turn) % 2]) for i in range(c...  6.18 us
    all_to_all x1, waiting for transfers between devices, per_device(): pieces = lax.all_to_all(sketches, 'seq', 0, 0, tiled=True)  5.78 us
  transfers between devices with their start and end apart: 11, of which 10 were waited for; matrix products, arithmetic and copies ran while one was open for 6% of the time, Pallas kernels for 0%

profile of v6, /device:TPU:30, one launch (start us, length us, event | category | flops | bytes accessed | tf_op | source)
XLA Modules:
  0.0 126.4 jit_solution(3307255184643714450)
XLA Ops:
  1.9 4.6 %collective-permute-start.3 = (bf16[512,512]{1,0:T(8,128)(2,1)S(1)}, bf16[512,512]{1,0:T(8,128)(2,1)S(1)}, u32[]{:S(2)}, u32[]{:S(2)}) collective-permute-start(bf16[512,512]{1,0:T(8,128)(2,1)S(1)} %pad_maximum_fusion), channel_id=1, source_target_pairs={{0,16},{8,24},{16,32},{24,40},{32,48},{40,56},{48,64},{56,72},{64,... | collective-permute-start | bytes 1572872 | tf_op jit(solution)/shard_map/ppermute | solution.py:302
  8.5 9.1 %collective-permute-done.3.kv2_hbm = bf16[512,512]{1,0:T(8,128)(2,1)S(1)} collective-permute-done((bf16[512,512]{1,0:T(8,128)(2,1)S(1)}, bf16[512,512]{1,0:T(8,128)(2,1)S(1)}, u32[]{:S(2)}, u32[]{:S(2)}) %collective-permute-start.3) | collective-permute-done | bytes 524320 | tf_op jit(solution)/shard_map/ppermute | solution.py:302
  18.4 4.3 %collective-permute-start.4 = (bf16[512,512]{1,0:T(8,128)(2,1)S(1)}, bf16[512,512]{1,0:T(8,128)(2,1)S(1)}, u32[]{:S(2)}, u32[]{:S(2)}) collective-permute-start(bf16[512,512]{1,0:T(8,128)(2,1)S(1)} %broadcast_select_fusion), channel_id=1, source_target_pairs={{0,8},{8,0},{16,24},{24,16},{32,40},{40,32},{48,56},{56,48},{64,72... | collective-permute-start | bytes 1572872 | tf_op jit(solution)/shard_map/ppermute | solution.py:317
  22.7 13.2 %while.20 = (s32[]{:T(128)}, bf16[512,128]{1,0:T(8,128)(2,1)}, s32[]{:T(128)}, pred[]{:T(512)}, f32[512,128]{1,0:T(8,128)S(1)}, /*index=5*/f32[512,128]{1,0:T(8,128)S(1)}, s32[]{:T(128)}) while((s32[]{:T(128)}, bf16[512,128]{1,0:T(8,128)(2,1)}, s32[]{:T(128)}, pred[]{:T(512)}, f32[512,128]{1,0:T(8,128)S(1)}, ...), condition=%wide.region_1.2_spmd, body=%wide.region_0.1_spmd.sunk | while | flops 720898 | bytes 3408032 | solution.py:321
  22.8 1.9 %collective-permute-start = (bf16[512,128]{1,0:T(8,128)(2,1)S(1)}, bf16[512,128]{1,0:T(8,128)(2,1)S(1)}, u32[]{:S(2)}, u32[]{:S(2)}) collective-permute-start(bf16[512,128]{1,0:T(8,128)(2,1)S(1)} %select_convert_fusion.2), channel_id=1, source_target_pairs={{0,1},{1,0},{2,3},{3,2},{4,5},{5,4},{6,7},{7,6},{8,9},{9,8},{10,11... | collective-permute-start | bytes 393224 | tf_op jit(solution)/shard_map/while/body/ppermute | solution.py:307
  26.1 6.1 %collective-permute-start.1 = (bf16[512,128]{1,0:T(8,128)(2,1)S(1)}, bf16[512,128]{1,0:T(8,128)(2,1)S(1)}, u32[]{:S(2)}, u32[]{:S(2)}) collective-permute-start(bf16[512,128]{1,0:T(8,128)(2,1)S(1)} %fusion.15), channel_id=1, source_target_pairs={{0,2},{1,7},{2,0},{3,5},{4,6},{5,3},{6,4},{7,1},{8,10},{9,15},{10,... | collective-permute-start | bytes 393224 | tf_op jit(solution)/shard_map/while/body/ppermute | solution.py:312
  32.2 3.0 %collective-permute-done.1 = bf16[512,128]{1,0:T(8,128)(2,1)S(1)} collective-permute-done((bf16[512,128]{1,0:T(8,128)(2,1)S(1)}, bf16[512,128]{1,0:T(8,128)(2,1)S(1)}, u32[]{:S(2)}, u32[]{:S(2)}) %collective-permute-start.1) | collective-permute-done | bytes 131104 | tf_op jit(solution)/shard_map/while/body/ppermute | solution.py:312
  35.9 16.5 %while.21 = (s32[]{:T(128)}, bf16[512,128]{1,0:T(8,128)(2,1)}, s32[]{:T(128)}, s32[]{:T(128)}) while((s32[]{:T(128)}, bf16[512,128]{1,0:T(8,128)(2,1)}, s32[]{:T(128)}, s32[]{:T(128)}) %tuple.45), condition=%wide.region_3.4_spmd, body=%wide.region_2.3_spmd.sunk | while | flops 262146 | bytes 917597 | solution.py:321
  35.9 11.7 %collective-permute-start.2 = (bf16[512,128]{1,0:T(8,128)(2,1)}, bf16[512,128]{1,0:T(8,128)(2,1)S(1)}, u32[]{:S(2)}, u32[]{:S(2)}) collective-permute-start(bf16[512,128]{1,0:T(8,128)(2,1)} %get-tuple-element.185), channel_id=1, source_target_pairs={{0,6},{1,3},{2,4},{3,1},{4,2},{5,7},{6,0},{7,5},{8,14},{9,11},{10,... | collective-permute-start | bytes 393224 | tf_op jit(solution)/shard_map/while/body/ppermute | solution.py:312
  47.6 3.2 %collective-permute-done.2 = bf16[512,128]{1,0:T(8,128)(2,1)S(1)} collective-permute-done((bf16[512,128]{1,0:T(8,128)(2,1)}, bf16[512,128]{1,0:T(8,128)(2,1)S(1)}, u32[]{:S(2)}, u32[]{:S(2)}) %collective-permute-start.2) | collective-permute-done | bytes 131104 | tf_op jit(solution)/shard_map/while/body/ppermute | solution.py:312
  50.7 1.6 %add_convert_fusion.5 = bf16[512,128]{1,0:T(8,128)(2,1)} fusion(bf16[512,128]{1,0:T(8,128)(2,1)S(1)} %collective-permute-done.2, bf16[512,128]{1,0:T(8,128)(2,1)} %get-tuple-element.185), kind=kLoop, calls=%fused_computation.4.clone.1 | loop fusion | flops 262144 | bytes 393216 | tf_op jit(solution)/shard_map/while/body/convert_element_type | solution.py:342
  52.3 2.9 %collective-permute-start.5 = (bf16[512,128]{1,0:T(8,128)(2,1)}, bf16[512,128]{1,0:T(8,128)(2,1)S(1)}, u32[]{:S(2)}, u32[]{:S(2)}) collective-permute-start(bf16[512,128]{1,0:T(8,128)(2,1)} %get-tuple-element.69), channel_id=1, source_target_pairs={{0,1},{1,0},{2,3},{3,2},{4,5},{5,4},{6,7},{7,6},{8,9},{9,8},{10,11... | collective-permute-start | bytes 393224 | tf_op jit(solution)/shard_map/ppermute | solution.py:307
  56.5 1.6 %broadcast_select_fusion.1 = (bf16[512,128]{1,0:T(8,128)(2,1)}, bf16[512,128]{1,0:T(8,128)(2,1)S(1)}) fusion(bf16[512,128]{1,0:T(8,128)(2,1)S(1)} %collective-permute-done.5, bf16[512,128]{1,0:T(8,128)(2,1)} %get-tuple-element.69, pred[]{:T(512)} %eq.10), kind=kLoop, calls=%fused_computation.14 | loop fusion | flops 131072 | bytes 524289 | tf_op jit(solution)/shard_map/jit(_where)/select_n | solution.py:348
  58.0 7.7 %collective-permute-start.7 = (bf16[512,128]{1,0:T(8,128)(2,1)S(1)}, bf16[512,128]{1,0:T(8,128)(2,1)S(1)}, u32[]{:S(2)}, u32[]{:S(2)}) collective-permute-start(bf16[512,128]{1,0:T(8,128)(2,1)S(1)} %get-tuple-element.96.x0_hbm), channel_id=1, source_target_pairs={{0,16},{8,24},{16,32},{24,40},{32,48},{40,56},{48,64},{56,72},{64,... | collective-permute-start | bytes 393224 | tf_op jit(solution)/shard_map/ppermute | solution.py:302
  65.8 1.9 %collective-permute-start.6 = (bf16[512,128]{1,0:T(8,128)(2,1)S(1)}, bf16[512,128]{1,0:T(8,128)(2,1)S(1)}, u32[]{:S(2)}, u32[]{:S(2)}) collective-permute-start(bf16[512,128]{1,0:T(8,128)(2,1)S(1)} %get-tuple-element.96.x0_hbm), channel_id=1, source_target_pairs={{0,8},{8,16},{16,24},{24,32},{32,40},{40,48},{48,56},{56,64},{64,7... | collective-permute-start | bytes 393224 | tf_op jit(solution)/shard_map/ppermute | solution.py:302
  67.7 1.3 %collective-permute-done.7.x2_hbm = bf16[512,128]{1,0:T(8,128)(2,1)S(1)} collective-permute-done((bf16[512,128]{1,0:T(8,128)(2,1)S(1)}, bf16[512,128]{1,0:T(8,128)(2,1)S(1)}, u32[]{:S(2)}, u32[]{:S(2)}) %collective-permute-start.7) | collective-permute-done | bytes 131104 | tf_op jit(solution)/shard_map/ppermute | solution.py:302
  69.0 5.0 %collective-permute-done.6.x1_hbm = bf16[512,128]{1,0:T(8,128)(2,1)S(1)} collective-permute-done((bf16[512,128]{1,0:T(8,128)(2,1)S(1)}, bf16[512,128]{1,0:T(8,128)(2,1)S(1)}, u32[]{:S(2)}, u32[]{:S(2)}) %collective-permute-start.6) | collective-permute-done | bytes 131104 | tf_op jit(solution)/shard_map/ppermute | solution.py:302
  74.9 16.2 %shard_map.207 = (bf16[512,512]{1,0:T(8,128)(2,1)}, bf16[512,512]{1,0:T(8,128)(2,1)}, bf16[512,512]{1,0:T(8,128)(2,1)}, bf16[512,512]{1,0:T(8,128)(2,1)}, bf16[64,2,1536]{2,1,0:T(2,128)(2,1)}) custom-call(s32[1]{0:T(128)} %bitcast.shard_ref, bf16[512,512]{1,0:T(8,128)(2,1)} %q_hbm.1, bf16[512,512]{1,0:T(8,128)(2,1)} %do_hbm.1, bf16[512,256]{1,0:T(8,128)(2,1)} %k0_hbm.1, ...), custom_call_target="tpu_custom_call" | custom-call | flops 4831838208 | bytes 6291456 | tf_op jit(solution)/shard_map/pallas_call | solution.py:259
  91.1 2.1 %collective-permute-start.8 = (bf16[512,512]{1,0:T(8,128)(2,1)}, bf16[512,512]{1,0:T(8,128)(2,1)S(1)}, u32[]{:S(2)}, u32[]{:S(2)}) collective-permute-start(bf16[512,512]{1,0:T(8,128)(2,1)} %get-tuple-element.72), channel_id=1, source_target_pairs={{0,8},{8,0},{16,24},{24,16},{32,40},{40,32},{48,56},{56,48},{64,72... | collective-permute-start | bytes 1572872 | tf_op jit(solution)/shard_map/ppermute | solution.py:317
  93.1 10.3 %all-to-all-start = ((bf16[64,2,1536]{2,1,0:T(2,128)(2,1)}), bf16[64,2,1536]{2,1,0:T(2,128)(2,1)S(1)}, u32[]{:S(2)}, u32[]{:S(2)}) async-start(bf16[64,2,1536]{2,1,0:T(2,128)(2,1)} %get-tuple-element.74), calls=%async_computation | async-start | bytes 786432 | tf_op jit(solution)/shard_map/all_to_all | solution.py:359
  103.4 4.2 %collective-permute-done.8 = bf16[512,512]{1,0:T(8,128)(2,1)S(1)} collective-permute-done((bf16[512,512]{1,0:T(8,128)(2,1)}, bf16[512,512]{1,0:T(8,128)(2,1)S(1)}, u32[]{:S(2)}, u32[]{:S(2)}) %collective-permute-start.8) | collective-permute-done | bytes 524320 | tf_op jit(solution)/shard_map/ppermute | solution.py:317
  107.8 1.9 %collective-permute-start.9 = (bf16[512,512]{1,0:T(8,128)(2,1)S(1)}, bf16[512,512]{1,0:T(8,128)(2,1)S(1)}, u32[]{:S(2)}, u32[]{:S(2)}) collective-permute-start(bf16[512,512]{1,0:T(8,128)(2,1)S(1)} %fusion.4), channel_id=1, source_target_pairs={{16,0},{24,8},{32,16},{40,24},{48,32},{56,40},{64,48},{72,56},{80,... | collective-permute-start | bytes 1572872 | tf_op jit(solution)/shard_map/ppermute | solution.py:302
  109.7 5.8 %all-to-all-done = bf16[64,2,1536]{2,1,0:T(2,128)(2,1)S(1)} async-done(((bf16[64,2,1536]{2,1,0:T(2,128)(2,1)}), bf16[64,2,1536]{2,1,0:T(2,128)(2,1)S(1)}, u32[]{:S(2)}, u32[]{:S(2)}) %all-to-all-start) | async-done | bytes 393248 | tf_op jit(solution)/shard_map/all_to_all | solution.py:359
  117.0 8.4 %collective-permute-done.9 = bf16[512,512]{1,0:T(8,128)(2,1)S(1)} collective-permute-done((bf16[512,512]{1,0:T(8,128)(2,1)S(1)}, bf16[512,512]{1,0:T(8,128)(2,1)S(1)}, u32[]{:S(2)}, u32[]{:S(2)}) %collective-permute-start.9) | collective-permute-done | bytes 524320 | tf_op jit(solution)/shard_map/ppermute | solution.py:302
  (38 shorter events, 10.8 us)
Async XLA Ops:
  0.6 6.3 %copy-start = (bf16[512,672]{0,1:T(8,128)(2,1)S(1)}, bf16[512,672]{0,1:T(8,128)(2,1)}, u32[]{:S(2)}) copy-start(bf16[512,672]{0,1:T(8,128)(2,1)} %param.20) | copy-start | bytes 2064388
  0.6 5.8 %copy-start.1 = (bf16[512,672]{0,1:T(8,128)(2,1)S(1)}, bf16[512,672]{0,1:T(8,128)(2,1)}, u32[]{:S(2)}) copy-start(bf16[512,672]{0,1:T(8,128)(2,1)} %param.22) | copy-start | bytes 2064388
  0.7 5.8 %copy-start.5 = (bf16[672,128]{1,0:T(8,128)(2,1)S(1)}, bf16[672,128]{1,0:T(8,128)(2,1)}, u32[]{:S(2)}) copy-start(bf16[672,128]{1,0:T(8,128)(2,1)} %param.23) | copy-start | bytes 516100
  1.9 15.8 %collective-permute-start.3 = (bf16[512,512]{1,0:T(8,128)(2,1)S(1)}, bf16[512,512]{1,0:T(8,128)(2,1)S(1)}, u32[]{:S(2)}, u32[]{:S(2)}) collective-permute-start(bf16[512,512]{1,0:T(8,128)(2,1)S(1)} %pad_maximum_fusion), channel_id=1, source_target_pairs={{0,16},{8,24},{16,32},{24,40},{32,48},{40,56},{48,64},{56,72},{64,... | collective-permute-start | bytes 1572872 | tf_op jit(solution)/shard_map/ppermute | solution.py:302
  6.5 0.9 copy-start.6
  17.6 0.8 copy-start.3
  18.4 55.6 %collective-permute-start.4 = (bf16[512,512]{1,0:T(8,128)(2,1)S(1)}, bf16[512,512]{1,0:T(8,128)(2,1)S(1)}, u32[]{:S(2)}, u32[]{:S(2)}) collective-permute-start(bf16[512,512]{1,0:T(8,128)(2,1)S(1)} %broadcast_select_fusion), channel_id=1, source_target_pairs={{0,8},{8,0},{16,24},{24,16},{32,40},{40,32},{48,56},{56,48},{64,72... | collective-permute-start | bytes 1572872 | tf_op jit(solution)/shard_map/ppermute | solution.py:317
  22.8 3.2 %collective-permute-start = (bf16[512,128]{1,0:T(8,128)(2,1)S(1)}, bf16[512,128]{1,0:T(8,128)(2,1)S(1)}, u32[]{:S(2)}, u32[]{:S(2)}) collective-permute-start(bf16[512,128]{1,0:T(8,128)(2,1)S(1)} %select_convert_fusion.2), channel_id=1, source_target_pairs={{0,1},{1,0},{2,3},{3,2},{4,5},{5,4},{6,7},{7,6},{8,9},{9,8},{10,11... | collective-permute-start | bytes 393224 | tf_op jit(solution)/shard_map/while/body/ppermute | solution.py:307
  26.1 9.1 %collective-permute-start.1 = (bf16[512,128]{1,0:T(8,128)(2,1)S(1)}, bf16[512,128]{1,0:T(8,128)(2,1)S(1)}, u32[]{:S(2)}, u32[]{:S(2)}) collective-permute-start(bf16[512,128]{1,0:T(8,128)(2,1)S(1)} %fusion.15), channel_id=1, source_target_pairs={{0,2},{1,7},{2,0},{3,5},{4,6},{5,3},{6,4},{7,1},{8,10},{9,15},{10,... | collective-permute-start | bytes 393224 | tf_op jit(solution)/shard_map/while/body/ppermute | solution.py:312
  35.9 14.9 %collective-permute-start.2 = (bf16[512,128]{1,0:T(8,128)(2,1)}, bf16[512,128]{1,0:T(8,128)(2,1)S(1)}, u32[]{:S(2)}, u32[]{:S(2)}) collective-permute-start(bf16[512,128]{1,0:T(8,128)(2,1)} %get-tuple-element.185), channel_id=1, source_target_pairs={{0,6},{1,3},{2,4},{3,1},{4,2},{5,7},{6,0},{7,5},{8,14},{9,11},{10,... | collective-permute-start | bytes 393224 | tf_op jit(solution)/shard_map/while/body/ppermute | solution.py:312
  52.3 4.1 %collective-permute-start.5 = (bf16[512,128]{1,0:T(8,128)(2,1)}, bf16[512,128]{1,0:T(8,128)(2,1)S(1)}, u32[]{:S(2)}, u32[]{:S(2)}) collective-permute-start(bf16[512,128]{1,0:T(8,128)(2,1)} %get-tuple-element.69), channel_id=1, source_target_pairs={{0,1},{1,0},{2,3},{3,2},{4,5},{5,4},{6,7},{7,6},{8,9},{9,8},{10,11... | collective-permute-start | bytes 393224 | tf_op jit(solution)/shard_map/ppermute | solution.py:307
  58.0 16.0 %copy-start.7 = (bf16[512,128]{1,0:T(8,128)(2,1)}, bf16[512,128]{1,0:T(8,128)(2,1)S(1)}, u32[]{:S(2)}) copy-start(bf16[512,128]{1,0:T(8,128)(2,1)S(1)} %get-tuple-element.96.x0_hbm) | copy-start | bytes 393220
  58.0 11.0 %collective-permute-start.7 = (bf16[512,128]{1,0:T(8,128)(2,1)S(1)}, bf16[512,128]{1,0:T(8,128)(2,1)S(1)}, u32[]{:S(2)}, u32[]{:S(2)}) collective-permute-start(bf16[512,128]{1,0:T(8,128)(2,1)S(1)} %get-tuple-element.96.x0_hbm), channel_id=1, source_target_pairs={{0,16},{8,24},{16,32},{24,40},{32,48},{40,56},{48,64},{56,72},{64,... | collective-permute-start | bytes 393224 | tf_op jit(solution)/shard_map/ppermute | solution.py:302
  65.8 8.3 %collective-permute-start.6 = (bf16[512,128]{1,0:T(8,128)(2,1)S(1)}, bf16[512,128]{1,0:T(8,128)(2,1)S(1)}, u32[]{:S(2)}, u32[]{:S(2)}) collective-permute-start(bf16[512,128]{1,0:T(8,128)(2,1)S(1)} %get-tuple-element.96.x0_hbm), channel_id=1, source_target_pairs={{0,8},{8,16},{16,24},{24,32},{32,40},{40,48},{48,56},{56,64},{64,7... | collective-permute-start | bytes 393224 | tf_op jit(solution)/shard_map/ppermute | solution.py:302
  69.0 5.0 %copy-start.9 = (bf16[512,128]{1,0:T(8,128)(2,1)}, bf16[512,128]{1,0:T(8,128)(2,1)S(1)}, u32[]{:S(2)}) copy-start(bf16[512,128]{1,0:T(8,128)(2,1)S(1)} %collective-permute-done.7.x2_hbm) | copy-start | bytes 393220
  74.0 0.6 copy-start.10
  74.0 0.9 copy-start.8
  91.1 16.6 %copy-start.4 = (bf16[512,512]{1,0:T(8,128)(2,1)S(1)}, bf16[512,512]{1,0:T(8,128)(2,1)}, u32[]{:S(2)}) copy-start(bf16[512,512]{1,0:T(8,128)(2,1)} %get-tuple-element.73) | copy-start | bytes 1572868
  91.1 16.5 %collective-permute-start.8 = (bf16[512,512]{1,0:T(8,128)(2,1)}, bf16[512,512]{1,0:T(8,128)(2,1)S(1)}, u32[]{:S(2)}, u32[]{:S(2)}) collective-permute-start(bf16[512,512]{1,0:T(8,128)(2,1)} %get-tuple-element.72), channel_id=1, source_target_pairs={{0,8},{8,0},{16,24},{24,16},{32,40},{40,32},{48,56},{56,48},{64,72... | collective-permute-start | bytes 1572872 | tf_op jit(solution)/shard_map/ppermute | solution.py:317
  93.1 22.4 %all-to-all-start = ((bf16[64,2,1536]{2,1,0:T(2,128)(2,1)}), bf16[64,2,1536]{2,1,0:T(2,128)(2,1)S(1)}, u32[]{:S(2)}, u32[]{:S(2)}) async-start(bf16[64,2,1536]{2,1,0:T(2,128)(2,1)} %get-tuple-element.74), calls=%async_computation | async-start | bytes 786432 | tf_op jit(solution)/shard_map/all_to_all | solution.py:359
  107.6 17.8 %copy-start.2 = (bf16[512,512]{1,0:T(8,128)(2,1)S(1)}, bf16[512,512]{1,0:T(8,128)(2,1)}, u32[]{:S(2)}) copy-start(bf16[512,512]{1,0:T(8,128)(2,1)} %get-tuple-element.71) | copy-start | bytes 1572868
  107.8 17.6 %collective-permute-start.9 = (bf16[512,512]{1,0:T(8,128)(2,1)S(1)}, bf16[512,512]{1,0:T(8,128)(2,1)S(1)}, u32[]{:S(2)}, u32[]{:S(2)}) collective-permute-start(bf16[512,512]{1,0:T(8,128)(2,1)S(1)} %fusion.4), channel_id=1, source_target_pairs={{16,0},{24,8},{32,16},{40,24},{48,32},{56,40},{64,48},{72,56},{80,... | collective-permute-start | bytes 1572872 | tf_op jit(solution)/shard_map/ppermute | solution.py:302

commit v7 on v6

--- a/solution.py
+++ b/solution.py
@@ -318,7 +318,7 @@
 
 
 def one_turn(step, start):
-    return lax.fori_loop(0, lax.optimization_barrier(jnp.int32(1)), lambda i, carry: step(carry), start)
+    return lax.fori_loop(0, lax.optimization_barrier(jnp.int32(1)), lambda i, carry: step(), start)
 
 
 def per_device(
@@ -331,19 +331,16 @@
     kv2 = shift(kv, 2)
     partial_x = jnp.dot(layer_input, omega_in, preferred_element_type=F32)
     partial_y = jnp.dot(upstream, omega_out, preferred_element_type=F32)
-
+    keep = jnp.where(first, partial_x, partial_y)
+    give = jnp.where(first, partial_y, partial_x).astype(BF16)
 
     def sum_near():
-        got = swap(jnp.where(first, partial_y, partial_x).astype(BF16), 1)
-        total = jnp.where(first, partial_x, partial_y) + got.astype(F32)
+        total = keep + swap(give, 1).astype(F32)
         return (total + z_swap(total.astype(BF16), 0).astype(F32)).astype(BF16)
 
-    def sum_far(half):
-        return (half.astype(F32) + z_swap(half, 1).astype(F32)).astype(BF16)
-
-    half = one_turn(lambda carry: sum_near(), partial_x.astype(BF16))
+    half = one_turn(sum_near, keep.astype(BF16))
     kv1 = pair_swap(jnp.where(odd, kv2, kv))
-    mine = one_turn(sum_far, half)
+    mine = (half.astype(F32) + z_swap(half, 1).astype(F32)).astype(BF16)
     other = swap(mine, 1)
     x0, y0 = jnp.where(first, mine, other), jnp.where(first, other, mine)
     x1 = shift(x0, 1)

time: 127 us -> 105 us (0.83)
  waiting for transfers between devices: 42.5 us -> 26.1 us
  starting transfers between devices: 55.4 us -> 51.7 us
  other arithmetic: 5.91 us -> 3.44 us
    ppermute x4, waiting for transfers between devices: 23.8 us -> 12.9 us  [shift(): return lax.ppermute(x, 'seq', pairs)]
    ppermute x2, waiting for transfers between devices: 6.18 us -> 2.93 us  [z_swap(): lax.ppermute(x, 'head', [(i, i ^ (2, 6)[(i + turn) % 2]) for i in range(c...]
    ppermute x4, starting transfers between devices: 16.2 us -> 13.8 us  [shift(): return lax.ppermute(x, 'seq', pairs)]
    ppermute x2, waiting for transfers between devices: 4.23 us -> 2.14 us  [pair_swap(): return lax.ppermute(x, 'seq', [(i, i ^ 1) for i in range(count)])]
    convert_element_type x2, other arithmetic: 1.63 us -> 0.07 us  [the longest x1 0.04 us: per_device(): mine = (half.astype(F32) + z_swap(half, 1).astype(F32)).astype(BF16)]
  transfers between devices with their start and end apart: 11 -> 11, of which waited for: 10 -> 7; matrix products, arithmetic and copies ran while one was open for 6% -> 3% of each run, Pallas kernels for 0% -> 0%
where the time goes in v7:
time: 105 us; the launch traced here: 104 us
  starting transfers between devices  51.7 us (49%)
  waiting for transfers between devices  26.1 us (25%)
  Pallas kernels  16.2 us (15%)
  local copies, waits for them, and re-layouts  4.29 us (4%)
  other arithmetic  3.44 us (3%)
  matrix products  1.49 us (1%)
    ppermute x2, starting transfers between devices, z_swap(): lax.ppermute(x, 'head', [(i, i ^ (2, 6)[(i + turn) % 2]) for i in range(c...  16.6 us
    pallas_call x1, Pallas kernels, attention(): pl.pallas_call(attention_kernel, in_specs=[pl.BlockSpec(memory_space=pltp...  16.2 us
    ppermute x4, starting transfers between devices, shift(): return lax.ppermute(x, 'seq', pairs)  13.8 us
    ppermute x4, waiting for transfers between devices, shift(): return lax.ppermute(x, 'seq', pairs)  12.9 us
    all_to_all x1, starting transfers between devices, per_device(): pieces = lax.all_to_all(sketches, 'seq', 0, 0, tiled=True)  11 us
    all_to_all x1, waiting for transfers between devices, per_device(): pieces = lax.all_to_all(sketches, 'seq', 0, 0, tiled=True)  6.86 us
    ppermute x2, starting transfers between devices, pair_swap(): return lax.ppermute(x, 'seq', [(i, i ^ 1) for i in range(count)])  6.6 us
    ppermute x2, starting transfers between devices, swap(): return lax.ppermute(x, 'head', [(i, i ^ bit) for i in range(count)])  3.84 us
  transfers between devices with their start and end apart: 11, of which 7 were waited for; matrix products, arithmetic and copies ran while one was open for 3% of the time, Pallas kernels for 0%

profile of v7, /device:TPU:30, one launch (start us, length us, event | category | flops | bytes accessed | tf_op | source)
XLA Modules:
  0.0 104.2 jit_solution(14538208879926324755)
XLA Ops:
  0.7 1.2 %pad_maximum_fusion = bf16[512,512]{1,0:T(8,128)(2,1)S(1)} fusion(bf16[512,256]{1,0:T(8,128)(2,1)} %v0_hbm.1, bf16[512,256]{1,0:T(8,128)(2,1)} %k0_hbm.1), kind=kLoop, calls=%fused_computation.10 | loop fusion | flops 1048576 | bytes 1048576 | tf_op jit(solution)/shard_map/concatenate | solution.py:327
  3.0 1.1 %fusion.5 = (bf16[512,128]{1,0:T(8,128)(2,1)}, f32[512,128]{1,0:T(8,128)S(1)}, bf16[512,128]{1,0:T(8,128)(2,1)S(1)}) fusion(f32[512,128]{1,0:T(8,128)S(1)} %fusion.9, pred[]{:T(512)S(6)} %eq.10, bf16[512,672]{0,1:T(8,128)(2,1)S(1)} %copy-done, bf16[672,128]{1,0:T(8,128)(2,1)S(1)} %copy-done.7), kind=kOutput, calls=%fused_computation.17 | convolution fusion | flops 88276992 | bytes 1646593 | tf_op jit(solution)/shard_map/dot_general | solution.py:332
  4.1 1.9 %collective-permute-start.3 = (bf16[512,128]{1,0:T(8,128)(2,1)S(1)}, bf16[512,128]{1,0:T(8,128)(2,1)S(1)}, u32[]{:S(2)}, u32[]{:S(2)}) collective-permute-start(bf16[512,128]{1,0:T(8,128)(2,1)S(1)} %select_convert_fusion), channel_id=1, source_target_pairs={{0,1},{1,0},{2,3},{3,2},{4,5},{5,4},{6,7},{7,6},{8,9},{9,8},{10,11... | collective-permute-start | bytes 393224 | tf_op jit(solution)/shard_map/while/body/ppermute | solution.py:307
  6.0 4.6 %collective-permute-start.1 = (bf16[512,512]{1,0:T(8,128)(2,1)S(1)}, bf16[512,512]{1,0:T(8,128)(2,1)S(1)}, u32[]{:S(2)}, u32[]{:S(2)}) collective-permute-start(bf16[512,512]{1,0:T(8,128)(2,1)S(1)} %pad_maximum_fusion), channel_id=1, source_target_pairs={{0,16},{8,24},{16,32},{24,40},{32,48},{40,56},{48,64},{56,72},{64,... | collective-permute-start | bytes 1572872 | tf_op jit(solution)/shard_map/ppermute | solution.py:302
  10.7 9.8 %while.12 = (s32[]{:T(128)}, bf16[512,128]{1,0:T(8,128)(2,1)}, s32[]{:T(128)}, bf16[512,128]{1,0:T(8,128)(2,1)S(1)}, f32[512,128]{1,0:T(8,128)S(1)}, /*index=5*/s32[]{:T(128)}) while((s32[]{:T(128)}, bf16[512,128]{1,0:T(8,128)(2,1)}, s32[]{:T(128)}, bf16[512,128]{1,0:T(8,128)(2,1)S(1)}, f32[512,128]{1,0:T(8,128)S(1)}, ...), condition=%wide.region_1.2_spmd, body=%wide.region_0.1_spmd.sunk | while | flops 524290 | bytes 1704045 | solution.py:321
  10.7 6.1 %collective-permute-start = (bf16[512,128]{1,0:T(8,128)(2,1)S(1)}, bf16[512,128]{1,0:T(8,128)(2,1)S(1)}, u32[]{:S(2)}, u32[]{:S(2)}) collective-permute-start(bf16[512,128]{1,0:T(8,128)(2,1)S(1)} %fusion.15), channel_id=1, source_target_pairs={{0,2},{1,7},{2,0},{3,5},{4,6},{5,3},{6,4},{7,1},{8,10},{9,15},{10,... | collective-permute-start | bytes 393224 | tf_op jit(solution)/shard_map/while/body/ppermute | solution.py:312
  16.8 2.9 %collective-permute-done = bf16[512,128]{1,0:T(8,128)(2,1)S(1)} collective-permute-done((bf16[512,128]{1,0:T(8,128)(2,1)S(1)}, bf16[512,128]{1,0:T(8,128)(2,1)S(1)}, u32[]{:S(2)}, u32[]{:S(2)}) %collective-permute-start) | collective-permute-done | bytes 131104 | tf_op jit(solution)/shard_map/while/body/ppermute | solution.py:312
  20.4 10.5 %collective-permute-start.4 = (bf16[512,128]{1,0:T(8,128)(2,1)}, bf16[512,128]{1,0:T(8,128)(2,1)S(1)}, u32[]{:S(2)}, u32[]{:S(2)}) collective-permute-start(bf16[512,128]{1,0:T(8,128)(2,1)} %get-tuple-element.79), channel_id=1, source_target_pairs={{0,6},{1,3},{2,4},{3,1},{4,2},{5,7},{6,0},{7,5},{8,14},{9,11},{10,... | collective-permute-start | bytes 393224 | tf_op jit(solution)/shard_map/ppermute | solution.py:312
  31.0 0.7 copy-done.4
  31.8 4.0 %collective-permute-start.2 = (bf16[512,512]{1,0:T(8,128)(2,1)S(1)}, bf16[512,512]{1,0:T(8,128)(2,1)S(1)}, u32[]{:S(2)}, u32[]{:S(2)}) collective-permute-start(bf16[512,512]{1,0:T(8,128)(2,1)S(1)} %broadcast_select_fusion), channel_id=1, source_target_pairs={{0,8},{8,0},{16,24},{24,16},{32,40},{40,32},{48,56},{56,48},{64,72... | collective-permute-start | bytes 1572872 | tf_op jit(solution)/shard_map/ppermute | solution.py:317
  35.9 1.9 %collective-permute-start.5 = (bf16[512,128]{1,0:T(8,128)(2,1)S(1)}, bf16[512,128]{1,0:T(8,128)(2,1)S(1)}, u32[]{:S(2)}, u32[]{:S(2)}) collective-permute-start(bf16[512,128]{1,0:T(8,128)(2,1)S(1)} %add_convert_fusion.1), channel_id=1, source_target_pairs={{0,1},{1,0},{2,3},{3,2},{4,5},{5,4},{6,7},{7,6},{8,9},{9,8},{10,11... | collective-permute-start | bytes 393224 | tf_op jit(solution)/shard_map/ppermute | solution.py:307
  37.8 1.3 %collective-permute-done.5 = bf16[512,128]{1,0:T(8,128)(2,1)S(1)} collective-permute-done((bf16[512,128]{1,0:T(8,128)(2,1)S(1)}, bf16[512,128]{1,0:T(8,128)(2,1)S(1)}, u32[]{:S(2)}, u32[]{:S(2)}) %collective-permute-start.5) | collective-permute-done | bytes 131104 | tf_op jit(solution)/shard_map/ppermute | solution.py:307
  39.8 3.4 %collective-permute-start.7 = (bf16[512,128]{1,0:T(8,128)(2,1)S(1)}, bf16[512,128]{1,0:T(8,128)(2,1)S(1)}, u32[]{:S(2)}, u32[]{:S(2)}) collective-permute-start(bf16[512,128]{1,0:T(8,128)(2,1)S(1)} %get-tuple-element.100.x0_hbm), channel_id=1, source_target_pairs={{0,16},{8,24},{16,32},{24,40},{32,48},{40,56},{48,64},{56,72},{64,... | collective-permute-start | bytes 393224 | tf_op jit(solution)/shard_map/ppermute | solution.py:302
  43.2 3.3 %collective-permute-start.6 = (bf16[512,128]{1,0:T(8,128)(2,1)S(1)}, bf16[512,128]{1,0:T(8,128)(2,1)S(1)}, u32[]{:S(2)}, u32[]{:S(2)}) collective-permute-start(bf16[512,128]{1,0:T(8,128)(2,1)S(1)} %get-tuple-element.100.x0_hbm), channel_id=1, source_target_pairs={{0,8},{8,16},{16,24},{24,32},{32,40},{40,48},{48,56},{56,64},{64,7... | collective-permute-start | bytes 393224 | tf_op jit(solution)/shard_map/ppermute | solution.py:302
  46.5 0.7 collective-permute-done.7.x2_hbm
  47.2 4.0 %collective-permute-done.6.x1_hbm = bf16[512,128]{1,0:T(8,128)(2,1)S(1)} collective-permute-done((bf16[512,128]{1,0:T(8,128)(2,1)S(1)}, bf16[512,128]{1,0:T(8,128)(2,1)S(1)}, u32[]{:S(2)}, u32[]{:S(2)}) %collective-permute-start.6) | collective-permute-done | bytes 131104 | tf_op jit(solution)/shard_map/ppermute | solution.py:302
  52.1 16.2 %shard_map.207 = (bf16[512,512]{1,0:T(8,128)(2,1)}, bf16[512,512]{1,0:T(8,128)(2,1)}, bf16[512,512]{1,0:T(8,128)(2,1)}, bf16[512,512]{1,0:T(8,128)(2,1)}, bf16[64,2,1536]{2,1,0:T(2,128)(2,1)}) custom-call(s32[1]{0:T(128)} %bitcast.shard_ref, bf16[512,512]{1,0:T(8,128)(2,1)} %q_hbm.1, bf16[512,512]{1,0:T(8,128)(2,1)} %do_hbm.1, bf16[512,256]{1,0:T(8,128)(2,1)} %k0_hbm.1, ...), custom_call_target="tpu_custom_call" | custom-call | flops 4831838208 | bytes 6291456 | tf_op jit(solution)/shard_map/pallas_call | solution.py:259
  68.3 2.6 %collective-permute-start.8 = (bf16[512,512]{1,0:T(8,128)(2,1)}, bf16[512,512]{1,0:T(8,128)(2,1)S(1)}, u32[]{:S(2)}, u32[]{:S(2)}) collective-permute-start(bf16[512,512]{1,0:T(8,128)(2,1)} %get-tuple-element.82), channel_id=1, source_target_pairs={{0,8},{8,0},{16,24},{24,16},{32,40},{40,32},{48,56},{56,48},{64,72... | collective-permute-start | bytes 1572872 | tf_op jit(solution)/shard_map/ppermute | solution.py:317
  70.9 11.0 %all-to-all-start = ((bf16[64,2,1536]{2,1,0:T(2,128)(2,1)}), bf16[64,2,1536]{2,1,0:T(2,128)(2,1)S(1)}, u32[]{:S(2)}, u32[]{:S(2)}) async-start(bf16[64,2,1536]{2,1,0:T(2,128)(2,1)} %get-tuple-element.84), calls=%async_computation | async-start | bytes 786432 | tf_op jit(solution)/shard_map/all_to_all | solution.py:356
  81.8 2.1 %collective-permute-done.8 = bf16[512,512]{1,0:T(8,128)(2,1)S(1)} collective-permute-done((bf16[512,512]{1,0:T(8,128)(2,1)}, bf16[512,512]{1,0:T(8,128)(2,1)S(1)}, u32[]{:S(2)}, u32[]{:S(2)}) %collective-permute-start.8) | collective-permute-done | bytes 524320 | tf_op jit(solution)/shard_map/ppermute | solution.py:317
  84.1 2.4 %collective-permute-start.9 = (bf16[512,512]{1,0:T(8,128)(2,1)S(1)}, bf16[512,512]{1,0:T(8,128)(2,1)S(1)}, u32[]{:S(2)}, u32[]{:S(2)}) collective-permute-start(bf16[512,512]{1,0:T(8,128)(2,1)S(1)} %fusion.4), channel_id=1, source_target_pairs={{16,0},{24,8},{32,16},{40,24},{48,32},{56,40},{64,48},{72,56},{80,... | collective-permute-start | bytes 1572872 | tf_op jit(solution)/shard_map/ppermute | solution.py:302
  86.6 6.9 %all-to-all-done = bf16[64,2,1536]{2,1,0:T(2,128)(2,1)S(1)} async-done(((bf16[64,2,1536]{2,1,0:T(2,128)(2,1)}), bf16[64,2,1536]{2,1,0:T(2,128)(2,1)S(1)}, u32[]{:S(2)}, u32[]{:S(2)}) %all-to-all-start) | async-done | bytes 393248 | tf_op jit(solution)/shard_map/all_to_all | solution.py:356
  95.0 8.1 %collective-permute-done.9 = bf16[512,512]{1,0:T(8,128)(2,1)S(1)} collective-permute-done((bf16[512,512]{1,0:T(8,128)(2,1)S(1)}, bf16[512,512]{1,0:T(8,128)(2,1)S(1)}, u32[]{:S(2)}, u32[]{:S(2)}) %collective-permute-start.9) | collective-permute-done | bytes 524320 | tf_op jit(solution)/shard_map/ppermute | solution.py:302
  103.3 0.8 fusion.6
  (39 shorter events, 5.4 us)
Async XLA Ops:
  0.6 1.8 %copy-start = (bf16[512,672]{0,1:T(8,128)(2,1)S(1)}, bf16[512,672]{0,1:T(8,128)(2,1)}, u32[]{:S(2)}) copy-start(bf16[512,672]{0,1:T(8,128)(2,1)} %param.18) | copy-start | bytes 2064388
  0.6 1.3 %copy-start.1 = (bf16[512,672]{0,1:T(8,128)(2,1)S(1)}, bf16[512,672]{0,1:T(8,128)(2,1)}, u32[]{:S(2)}) copy-start(bf16[512,672]{0,1:T(8,128)(2,1)} %param.20) | copy-start | bytes 2064388
  0.7 1.3 %copy-start.6 = (bf16[672,128]{1,0:T(8,128)(2,1)S(1)}, bf16[672,128]{1,0:T(8,128)(2,1)}, u32[]{:S(2)}) copy-start(bf16[672,128]{1,0:T(8,128)(2,1)} %param.21) | copy-start | bytes 516100
  2.0 1.0 copy-start.7
  4.1 6.6 %collective-permute-start.3 = (bf16[512,128]{1,0:T(8,128)(2,1)S(1)}, bf16[512,128]{1,0:T(8,128)(2,1)S(1)}, u32[]{:S(2)}, u32[]{:S(2)}) collective-permute-start(bf16[512,128]{1,0:T(8,128)(2,1)S(1)} %select_convert_fusion), channel_id=1, source_target_pairs={{0,1},{1,0},{2,3},{3,2},{4,5},{5,4},{6,7},{7,6},{8,9},{9,8},{10,11... | collective-permute-start | bytes 393224 | tf_op jit(solution)/shard_map/while/body/ppermute | solution.py:307
  6.0 24.9 %collective-permute-start.1 = (bf16[512,512]{1,0:T(8,128)(2,1)S(1)}, bf16[512,512]{1,0:T(8,128)(2,1)S(1)}, u32[]{:S(2)}, u32[]{:S(2)}) collective-permute-start(bf16[512,512]{1,0:T(8,128)(2,1)S(1)} %pad_maximum_fusion), channel_id=1, source_target_pairs={{0,16},{8,24},{16,32},{24,40},{32,48},{40,56},{48,64},{56,72},{64,... | collective-permute-start | bytes 1572872 | tf_op jit(solution)/shard_map/ppermute | solution.py:302
  10.7 9.0 %collective-permute-start = (bf16[512,128]{1,0:T(8,128)(2,1)S(1)}, bf16[512,128]{1,0:T(8,128)(2,1)S(1)}, u32[]{:S(2)}, u32[]{:S(2)}) collective-permute-start(bf16[512,128]{1,0:T(8,128)(2,1)S(1)} %fusion.15), channel_id=1, source_target_pairs={{0,2},{1,7},{2,0},{3,5},{4,6},{5,3},{6,4},{7,1},{8,10},{9,15},{10,... | collective-permute-start | bytes 393224 | tf_op jit(solution)/shard_map/while/body/ppermute | solution.py:312
  20.4 15.4 %copy-start.3 = (bf16[512,128]{1,0:T(8,128)(2,1)S(1)}, bf16[512,128]{1,0:T(8,128)(2,1)}, u32[]{:S(2)}) copy-start(bf16[512,128]{1,0:T(8,128)(2,1)} %get-tuple-element.79) | copy-start | bytes 393220
  20.4 15.4 %collective-permute-start.4 = (bf16[512,128]{1,0:T(8,128)(2,1)}, bf16[512,128]{1,0:T(8,128)(2,1)S(1)}, u32[]{:S(2)}, u32[]{:S(2)}) collective-permute-start(bf16[512,128]{1,0:T(8,128)(2,1)} %get-tuple-element.79), channel_id=1, source_target_pairs={{0,6},{1,3},{2,4},{3,1},{4,2},{5,7},{6,0},{7,5},{8,14},{9,11},{10,... | collective-permute-start | bytes 393224 | tf_op jit(solution)/shard_map/ppermute | solution.py:312
  31.0 0.8 copy-start.4
  31.8 19.5 %collective-permute-start.2 = (bf16[512,512]{1,0:T(8,128)(2,1)S(1)}, bf16[512,512]{1,0:T(8,128)(2,1)S(1)}, u32[]{:S(2)}, u32[]{:S(2)}) collective-permute-start(bf16[512,512]{1,0:T(8,128)(2,1)S(1)} %broadcast_select_fusion), channel_id=1, source_target_pairs={{0,8},{8,0},{16,24},{24,16},{32,40},{40,32},{48,56},{56,48},{64,72... | collective-permute-start | bytes 1572872 | tf_op jit(solution)/shard_map/ppermute | solution.py:317
  35.9 3.2 %collective-permute-start.5 = (bf16[512,128]{1,0:T(8,128)(2,1)S(1)}, bf16[512,128]{1,0:T(8,128)(2,1)S(1)}, u32[]{:S(2)}, u32[]{:S(2)}) collective-permute-start(bf16[512,128]{1,0:T(8,128)(2,1)S(1)} %add_convert_fusion.1), channel_id=1, source_target_pairs={{0,1},{1,0},{2,3},{3,2},{4,5},{5,4},{6,7},{7,6},{8,9},{9,8},{10,11... | collective-permute-start | bytes 393224 | tf_op jit(solution)/shard_map/ppermute | solution.py:307
  39.8 11.5 %copy-start.8 = (bf16[512,128]{1,0:T(8,128)(2,1)}, bf16[512,128]{1,0:T(8,128)(2,1)S(1)}, u32[]{:S(2)}) copy-start(bf16[512,128]{1,0:T(8,128)(2,1)S(1)} %get-tuple-element.100.x0_hbm) | copy-start | bytes 393220
  39.8 7.4 %collective-permute-start.7 = (bf16[512,128]{1,0:T(8,128)(2,1)S(1)}, bf16[512,128]{1,0:T(8,128)(2,1)S(1)}, u32[]{:S(2)}, u32[]{:S(2)}) collective-permute-start(bf16[512,128]{1,0:T(8,128)(2,1)S(1)} %get-tuple-element.100.x0_hbm), channel_id=1, source_target_pairs={{0,16},{8,24},{16,32},{24,40},{32,48},{40,56},{48,64},{56,72},{64,... | collective-permute-start | bytes 393224 | tf_op jit(solution)/shard_map/ppermute | solution.py:302
  43.2 8.1 %collective-permute-start.6 = (bf16[512,128]{1,0:T(8,128)(2,1)S(1)}, bf16[512,128]{1,0:T(8,128)(2,1)S(1)}, u32[]{:S(2)}, u32[]{:S(2)}) collective-permute-start(bf16[512,128]{1,0:T(8,128)(2,1)S(1)} %get-tuple-element.100.x0_hbm), channel_id=1, source_target_pairs={{0,8},{8,16},{16,24},{24,32},{32,40},{40,48},{48,56},{56,64},{64,7... | collective-permute-start | bytes 393224 | tf_op jit(solution)/shard_map/ppermute | solution.py:302
  47.2 4.0 %copy-start.10 = (bf16[512,128]{1,0:T(8,128)(2,1)}, bf16[512,128]{1,0:T(8,128)(2,1)S(1)}, u32[]{:S(2)}) copy-start(bf16[512,128]{1,0:T(8,128)(2,1)S(1)} %collective-permute-done.7.x2_hbm) | copy-start | bytes 393220
  51.3 0.6 copy-start.11
  51.3 0.9 copy-start.9
  68.3 15.7 %copy-start.5 = (bf16[512,512]{1,0:T(8,128)(2,1)S(1)}, bf16[512,512]{1,0:T(8,128)(2,1)}, u32[]{:S(2)}) copy-start(bf16[512,512]{1,0:T(8,128)(2,1)} %get-tuple-element.83) | copy-start | bytes 1572868
  68.3 15.7 %collective-permute-start.8 = (bf16[512,512]{1,0:T(8,128)(2,1)}, bf16[512,512]{1,0:T(8,128)(2,1)S(1)}, u32[]{:S(2)}, u32[]{:S(2)}) collective-permute-start(bf16[512,512]{1,0:T(8,128)(2,1)} %get-tuple-element.82), channel_id=1, source_target_pairs={{0,8},{8,0},{16,24},{24,16},{32,40},{40,32},{48,56},{56,48},{64,72... | collective-permute-start | bytes 1572872 | tf_op jit(solution)/shard_map/ppermute | solution.py:317
  70.9 22.6 %all-to-all-start = ((bf16[64,2,1536]{2,1,0:T(2,128)(2,1)}), bf16[64,2,1536]{2,1,0:T(2,128)(2,1)S(1)}, u32[]{:S(2)}, u32[]{:S(2)}) async-start(bf16[64,2,1536]{2,1,0:T(2,128)(2,1)} %get-tuple-element.84), calls=%async_computation | async-start | bytes 786432 | tf_op jit(solution)/shard_map/all_to_all | solution.py:356
  84.0 19.1 %copy-start.2 = (bf16[512,512]{1,0:T(8,128)(2,1)S(1)}, bf16[512,512]{1,0:T(8,128)(2,1)}, u32[]{:S(2)}) copy-start(bf16[512,512]{1,0:T(8,128)(2,1)} %get-tuple-element.81) | copy-start | bytes 1572868
  84.1 19.0 %collective-permute-start.9 = (bf16[512,512]{1,0:T(8,128)(2,1)S(1)}, bf16[512,512]{1,0:T(8,128)(2,1)S(1)}, u32[]{:S(2)}, u32[]{:S(2)}) collective-permute-start(bf16[512,512]{1,0:T(8,128)(2,1)S(1)} %fusion.4), channel_id=1, source_target_pairs={{16,0},{24,8},{32,16},{40,24},{48,32},{56,40},{64,48},{72,56},{80,... | collective-permute-start | bytes 1572872 | tf_op jit(solution)/shard_map/ppermute | solution.py:302
